TPU v7x, 32 devices: a whole 2x2x4 slice. The times are simulated.
32 devices in a mesh: dp: 8 (over z, y), fsdp: 4 (over x, core).
Axes of the slice: x: 2, y: 2, z: 4, core: 2. Of those that a mesh axis runs over, the one named last changes fastest.
Arguments:
- tokens: bfloat16 [131072, 384], P(('dp', 'fsdp')), may hold values from -6 to 6
- centres: float32 [3, 131072], P(None, ('dp', 'fsdp')), may hold values from -1 to 1
- lengths: int32 [512], P(('dp', 'fsdp')), may hold values from 32 to 256, as said below
- cotangent: bfloat16 [131072, 384], P(('dp', 'fsdp')), may hold values from -6 to 6
- smalls: float32 [4736], P(('dp', 'fsdp')), may hold values from -1.5 to 1.5
- master_qkv: float32 [384, 1152], P(('dp', 'fsdp')), may hold values from -0.3125 to 0.3125
- master_out: float32 [384, 384], P(('dp', 'fsdp')), may hold values from -0.875 to 0.875
- master_up: float32 [384, 1536], P(('dp', 'fsdp')), may hold values from -0.3125 to 0.3125
- master_down: float32 [1536, 384], P(('dp', 'fsdp')), may hold values from -0.15625 to 0.15625
- master_pos: float32 [128, 384], P(('dp', 'fsdp')), may hold values from -0.5 to 0.5
- first_qkv: float32 [384, 1152], P(('dp', 'fsdp')), may hold values from -868.8928 to 868.8928
- first_out: float32 [384, 384], P(('dp', 'fsdp')), may hold values from -868.8928 to 868.8928
- first_up: float32 [384, 1536], P(('dp', 'fsdp')), may hold values from -868.8928 to 868.8928
- first_down: float32 [1536, 384], P(('dp', 'fsdp')), may hold values from -868.8928 to 868.8928
- first_pos: float32 [128, 384], P(('dp', 'fsdp')), may hold values from -868.8928 to 868.8928
- second_qkv: float32 [384, 1152], P(('dp', 'fsdp')), may hold values from 20971.52 to 83886.08
- second_out: float32 [384, 384], P(('dp', 'fsdp')), may hold values from 20971.52 to 83886.08
- second_up: float32 [384, 1536], P(('dp', 'fsdp')), may hold values from 20971.52 to 83886.08
- second_down: float32 [1536, 384], P(('dp', 'fsdp')), may hold values from 20971.52 to 83886.08
- second_pos: float32 [128, 384], P(('dp', 'fsdp')), may hold values from 20971.52 to 83886.08
- left_qkv: float32 [384, 384], P(('dp', 'fsdp')), may hold values from -1 to 1, as said below
- left_out: float32 [384, 384], P(('dp', 'fsdp')), may hold values from -1 to 1, as said below
- left_up: float32 [384, 384], P(('dp', 'fsdp')), may hold values from -1 to 1, as said below
- left_down: float32 [1536, 1536], P(('dp', 'fsdp')), may hold values from -1 to 1, as said below
- left_pos: float32 [128, 128], P(('dp', 'fsdp')), may hold values from -1 to 1, as said below
- right_qkv: float32 [1152, 1152], replicated, may hold values from -1 to 1, as said below
- right_out: float32 [384, 384], replicated, may hold values from -1 to 1, as said below
- right_up: float32 [1536, 1536], replicated, may hold values from -1 to 1, as said below
- right_down: float32 [384, 384], replicated, may hold values from -1 to 1, as said below
- right_pos: float32 [384, 384], replicated, may hold values from -1 to 1, as said below
Outputs:
- layer_out: bfloat16 [131072, 384], P(('dp', 'fsdp'))
- grad_tokens: bfloat16 [131072, 384], P(('dp', 'fsdp'))
- grad_smalls: float32 [4736], P(('dp', 'fsdp'))
- grad_qkv: float32 [384, 1152], P(('dp', 'fsdp'))
- grad_out: float32 [384, 384], P(('dp', 'fsdp'))
- grad_up: float32 [384, 1536], P(('dp', 'fsdp'))
- grad_down: float32 [1536, 384], P(('dp', 'fsdp'))
- grad_pos: float32 [128, 384], P(('dp', 'fsdp'))
- first_qkv_next: float32 [384, 1152], P(('dp', 'fsdp'))
- first_out_next: float32 [384, 384], P(('dp', 'fsdp'))
- first_up_next: float32 [384, 1536], P(('dp', 'fsdp'))
- first_down_next: float32 [1536, 384], P(('dp', 'fsdp'))
- first_pos_next: float32 [128, 384], P(('dp', 'fsdp'))
- second_qkv_next: float32 [384, 1152], P(('dp', 'fsdp'))
- second_out_next: float32 [384, 384], P(('dp', 'fsdp'))
- second_up_next: float32 [384, 1536], P(('dp', 'fsdp'))
- second_down_next: float32 [1536, 384], P(('dp', 'fsdp'))
- second_pos_next: float32 [128, 384], P(('dp', 'fsdp'))
- master_qkv_next: float32 [384, 1152], P(('dp', 'fsdp'))
- master_out_next: float32 [384, 384], P(('dp', 'fsdp'))
- master_up_next: float32 [384, 1536], P(('dp', 'fsdp'))
- master_down_next: float32 [1536, 384], P(('dp', 'fsdp'))
- master_pos_next: float32 [128, 384], P(('dp', 'fsdp'))
- weight_qkv_low: bfloat16 [384, 1152], P(('dp', 'fsdp'))
- weight_out_low: bfloat16 [384, 384], P(('dp', 'fsdp'))
- weight_up_low: bfloat16 [384, 1536], P(('dp', 'fsdp'))
- weight_down_low: bfloat16 [1536, 384], P(('dp', 'fsdp'))
- weight_pos_low: bfloat16 [128, 384], P(('dp', 'fsdp'))
Inputs may be any that keep to these rules, and one draw needn't show every extreme that they name: `lengths`: on every device one of its 16 clouds has exactly 256 patches. `left_qkv`: an orthogonal matrix. `left_out`: an orthogonal matrix. `left_up`: an orthogonal matrix. `left_down`: an orthogonal matrix. `left_pos`: an orthogonal matrix. `right_qkv`: an orthogonal matrix. `right_out`: an orthogonal matrix. `right_up`: an orthogonal matrix. `right_down`: an orthogonal matrix. `right_pos`: an orthogonal matrix.
All inputs are finite; a program needn't handle non-finite values.
Results may differ from a plain program's by a relative error of at most 0.011.
Values may be sent and summed in bfloat16 or wider, within the bound.
A program may use at most 320 MiB of HBM per device.

v0:
```python
import jax
import jax.numpy as jnp
from jax import lax
from jax.sharding import PartitionSpec as P

D = 384
HEADS = 6
HEAD = 64
FF = 1536
PH = 128
LMAX = 256


HIGHEST = lax.Precision.HIGHEST
EPSILON = 1e-05
ADAM_EPSILON = 1e-08
WEIGHT_DECAY = 0.05
DECAY = 0.5
NEG_FILL = -1e30


def layer_norm(inputs, gain_vec, shift_vec):
    centred = inputs - jnp.mean(inputs, axis=-1, keepdims=True)
    spread = jnp.mean(centred * centred, axis=-1, keepdims=True)
    return centred * lax.rsqrt(spread + EPSILON) * gain_vec + shift_vec


def gelu_exact(inputs):
    return jax.nn.gelu(inputs, approximate=False)


def left_product(inputs, grads):
    return jnp.einsum("tk,tn->kn", inputs, grads, preferred_element_type=jnp.float32)


def right_product(grads, weight):
    return jnp.einsum("tn,kn->tk", grads, weight, preferred_element_type=jnp.float32)


def unpack_smalls(flat_params):
    pieces = [flat_params[place * D : (place + 1) * D] for place in range(7)]
    offset = 7 * D
    up_bias = flat_params[offset : offset + FF]
    hidden_bias = flat_params[offset + FF : offset + FF + PH]
    pos_first = flat_params[offset + FF + PH :].reshape(3, PH)
    return pieces + [up_bias, hidden_bias, pos_first]


def on_device(
    tokens,
    centres,
    lengths,
    cotangent,
    smalls,
    master_qkv,
    master_out,
    master_up,
    master_down,
    master_pos,
    first_qkv,
    first_out,
    first_up,
    first_down,
    first_pos,
    second_qkv,
    second_out,
    second_up,
    second_down,
    second_pos,
    left_qkv,
    left_out,
    left_up,
    left_down,
    left_pos,
    right_qkv,
    right_out,
    right_up,
    right_down,
    right_pos,
):
    masters = (master_qkv, master_out, master_up, master_down, master_pos)
    firsts = (first_qkv, first_out, first_up, first_down, first_pos)
    seconds = (second_qkv, second_out, second_up, second_down, second_pos)
    left_bases = (left_qkv, left_out, left_up, left_down, left_pos)
    right_bases = (right_qkv, right_out, right_up, right_down, right_pos)
    lowered = tuple((weight.astype(jnp.bfloat16) for weight in masters)) + (
        smalls.astype(jnp.bfloat16),
    )
    gathered = (
        lax.all_gather(lowered[0], ("dp", "fsdp"), axis=0, tiled=True),
        lax.all_gather(lowered[1], ("dp", "fsdp"), axis=0, tiled=True),
        lax.all_gather(lowered[2], ("dp", "fsdp"), axis=0, tiled=True),
        lax.all_gather(lowered[3], ("dp", "fsdp"), axis=0, tiled=True),
        lax.all_gather(lowered[4], ("dp", "fsdp"), axis=0, tiled=True),
        lax.all_gather(lowered[5], ("dp", "fsdp"), axis=0, tiled=True),
    )
    w_qkv, w_out, w_up, w_down, w_pos, small_low = gathered
    (
        gain_one,
        shift_one,
        gain_two,
        shift_two,
        attn_bias,
        down_bias,
        embed_bias,
        up_bias,
        hidden_bias,
        pos_first,
    ) = unpack_smalls(small_low.astype(jnp.float32))
    clouds = lengths.shape[0]
    row_count = clouds * LMAX
    score_scale = HEAD ** (-0.5)
    positions = jnp.arange(LMAX, dtype=jnp.int32)
    key_mask = positions[None, :] < lengths[:, None]
    live_rows = key_mask.reshape(row_count).astype(jnp.float32)
    pos_hidden = jnp.einsum("ct,cp->tp", centres, pos_first, precision=HIGHEST) + hidden_bias
    pos_act, gelu_pos = jax.vjp(gelu_exact, pos_hidden)
    pos_low = pos_act.astype(jnp.bfloat16)
    embedded = (
        tokens.astype(jnp.float32)
        + jnp.dot(pos_low, w_pos, preferred_element_type=jnp.float32)
        + embed_bias
    )
    normed_one, norm_pull_one = jax.vjp(layer_norm, embedded, gain_one, shift_one)
    normed_one_low = normed_one.astype(jnp.bfloat16)
    qkv_low = jnp.dot(normed_one_low, w_qkv, preferred_element_type=jnp.float32).astype(
        jnp.bfloat16
    )
    head_split = qkv_low.reshape(clouds, LMAX, 3, HEADS, HEAD)
    queries = head_split[:, :, 0]
    key_heads = head_split[:, :, 1]
    value_heads = head_split[:, :, 2]

    def scores_of():
        raw_scores = (
            jnp.einsum("cqhd,ckhd->chqk", queries, key_heads, preferred_element_type=jnp.float32)
            * score_scale
        )
        return jnp.where(key_mask[:, None, None, :], raw_scores, NEG_FILL)

    scores = scores_of()
    row_top = jnp.max(scores, axis=-1, keepdims=True)
    exponent = jnp.exp(scores - row_top)
    row_total = jnp.sum(exponent, axis=-1, keepdims=True)
    softmax_probs = exponent / row_total
    log_total = row_top + jnp.log(row_total)
    probs_low = softmax_probs.astype(jnp.bfloat16)
    attended = (
        jnp.einsum("chqk,ckhd->cqhd", probs_low, value_heads, preferred_element_type=jnp.float32)
        .reshape(row_count, D)
        .astype(jnp.bfloat16)
    )
    branch_in = embedded + jnp.dot(attended, w_out, preferred_element_type=jnp.float32) + attn_bias
    normed_two, norm_pull_two = jax.vjp(layer_norm, branch_in, gain_two, shift_two)
    normed_two_low = normed_two.astype(jnp.bfloat16)
    hidden = jnp.dot(normed_two_low, w_up, preferred_element_type=jnp.float32) + up_bias
    activation, gelu_pull = jax.vjp(gelu_exact, hidden)
    activation_low = activation.astype(jnp.bfloat16)
    layer_out = (
        branch_in + jnp.dot(activation_low, w_down, preferred_element_type=jnp.float32) + down_bias
    ).astype(jnp.bfloat16)
    back_qkv, back_out, back_up, back_down, back_pos = (
        lax.all_gather(lowered[0], ("dp", "fsdp"), axis=0, tiled=True),
        lax.all_gather(lowered[1], ("dp", "fsdp"), axis=0, tiled=True),
        lax.all_gather(lowered[2], ("dp", "fsdp"), axis=0, tiled=True),
        lax.all_gather(lowered[3], ("dp", "fsdp"), axis=0, tiled=True),
        lax.all_gather(lowered[4], ("dp", "fsdp"), axis=0, tiled=True),
    )
    grad_y = cotangent.astype(jnp.float32) * live_rows[:, None]
    grad_y_low = grad_y.astype(jnp.bfloat16)
    down_grad = left_product(activation_low, grad_y_low)
    down_bias_grad = jnp.sum(grad_y, axis=0)
    activation_grad = right_product(grad_y_low, back_down)
    hidden_grad_low = gelu_pull(activation_grad)[0].astype(jnp.bfloat16)
    up_bias_grad = jnp.sum(hidden_grad_low.astype(jnp.float32), axis=0)
    up_grad = left_product(normed_two_low, hidden_grad_low)
    normed_two_grad = right_product(hidden_grad_low, back_up)
    branch_part, gain_two_grad, shift_two_grad = norm_pull_two(normed_two_grad)
    branch_grad = grad_y + branch_part
    attn_bias_grad = jnp.sum(branch_grad, axis=0)
    branch_grad_low = branch_grad.astype(jnp.bfloat16)
    out_grad = left_product(attended, branch_grad_low)
    attended_grad = (
        right_product(branch_grad_low, back_out)
        .astype(jnp.bfloat16)
        .reshape(clouds, LMAX, HEADS, HEAD)
    )
    probs_again = jnp.exp(scores_of() - log_total)
    probs_again_low = probs_again.astype(jnp.bfloat16)
    probs_grad = jnp.einsum(
        "cqhd,ckhd->chqk", attended_grad, value_heads, preferred_element_type=jnp.float32
    )
    row_dot = jnp.sum(probs_again * probs_grad, axis=-1, keepdims=True)
    score_grad = (probs_again * (probs_grad - row_dot)).astype(jnp.bfloat16)
    value_grad = jnp.einsum(
        "chqk,cqhd->ckhd", probs_again_low, attended_grad, preferred_element_type=jnp.float32
    )
    query_grad = (
        jnp.einsum("chqk,ckhd->cqhd", score_grad, key_heads, preferred_element_type=jnp.float32)
        * score_scale
    )
    key_grad = (
        jnp.einsum("chqk,cqhd->ckhd", score_grad, queries, preferred_element_type=jnp.float32)
        * score_scale
    )
    qkv_grad_low = (
        jnp.stack([query_grad, key_grad, value_grad], axis=2)
        .reshape(row_count, 3 * D)
        .astype(jnp.bfloat16)
    )
    qkv_grad = left_product(normed_one_low, qkv_grad_low)
    normed_one_grad = right_product(qkv_grad_low, back_qkv)
    embed_part, gain_one_grad, shift_one_grad = norm_pull_one(normed_one_grad)
    embed_grad = branch_grad + embed_part
    embed_bias_grad = jnp.sum(embed_grad, axis=0)
    embed_grad_low = embed_grad.astype(jnp.bfloat16)
    pos_grad = left_product(pos_low, embed_grad_low)
    pos_act_grad = right_product(embed_grad_low, back_pos)
    pos_hidden_grad = gelu_pos(pos_act_grad)[0]
    hidden_bias_grad = jnp.sum(pos_hidden_grad, axis=0)
    pos_first_grad = jnp.einsum("ct,tp->cp", centres, pos_hidden_grad, precision=HIGHEST)
    small_grad = jnp.concatenate(
        [
            gain_one_grad,
            shift_one_grad,
            gain_two_grad,
            shift_two_grad,
            attn_bias_grad,
            down_bias_grad,
            embed_bias_grad,
            up_bias_grad,
            hidden_bias_grad,
            pos_first_grad.reshape(3 * PH),
        ]
    )
    reduced = (
        lax.psum_scatter(qkv_grad, ("dp", "fsdp"), scatter_dimension=0, tiled=True),
        lax.psum_scatter(out_grad, ("dp", "fsdp"), scatter_dimension=0, tiled=True),
        lax.psum_scatter(up_grad, ("dp", "fsdp"), scatter_dimension=0, tiled=True),
        lax.psum_scatter(down_grad, ("dp", "fsdp"), scatter_dimension=0, tiled=True),
        lax.psum_scatter(pos_grad, ("dp", "fsdp"), scatter_dimension=0, tiled=True),
        lax.psum_scatter(small_grad, ("dp", "fsdp"), scatter_dimension=0, tiled=True),
    )
    terms_in = []
    for place in range(5):
        turned = jnp.dot(reduced[place], right_bases[place], precision=HIGHEST)
        terms_in.append(jnp.einsum("rk,rn->kn", left_bases[place], turned, precision=HIGHEST))
    rotated = (
        lax.psum_scatter(terms_in[0], ("dp", "fsdp"), scatter_dimension=0, tiled=True),
        lax.psum_scatter(terms_in[1], ("dp", "fsdp"), scatter_dimension=0, tiled=True),
        lax.psum_scatter(terms_in[2], ("dp", "fsdp"), scatter_dimension=0, tiled=True),
        lax.psum_scatter(terms_in[3], ("dp", "fsdp"), scatter_dimension=0, tiled=True),
        lax.psum_scatter(terms_in[4], ("dp", "fsdp"), scatter_dimension=0, tiled=True),
    )
    firsts_next = []
    seconds_next = []
    directions = []
    for place in range(5):
        first_next = DECAY * firsts[place] + (1.0 - DECAY) * rotated[place]
        second_next = DECAY * seconds[place] + (1.0 - DECAY) * rotated[place] * rotated[place]
        firsts_next.append(first_next)
        seconds_next.append(second_next)
        directions.append(first_next / (jnp.sqrt(second_next) + ADAM_EPSILON))
    whole_steps = (
        lax.all_gather(
            directions[0].astype(jnp.bfloat16), ("dp", "fsdp"), axis=0, tiled=True
        ).astype(jnp.float32),
        lax.all_gather(
            directions[1].astype(jnp.bfloat16), ("dp", "fsdp"), axis=0, tiled=True
        ).astype(jnp.float32),
        lax.all_gather(
            directions[2].astype(jnp.bfloat16), ("dp", "fsdp"), axis=0, tiled=True
        ).astype(jnp.float32),
        lax.all_gather(
            directions[3].astype(jnp.bfloat16), ("dp", "fsdp"), axis=0, tiled=True
        ).astype(jnp.float32),
        lax.all_gather(
            directions[4].astype(jnp.bfloat16), ("dp", "fsdp"), axis=0, tiled=True
        ).astype(jnp.float32),
    )
    masters_next = []
    lows_next = []
    for place in range(5):
        partway = jnp.dot(left_bases[place], whole_steps[place], precision=HIGHEST)
        update = jnp.einsum("rn,mn->rm", partway, right_bases[place], precision=HIGHEST)
        rate = left_bases[place].shape[1] ** (-0.5)
        master_next = masters[place] * (1.0 - rate * WEIGHT_DECAY) - rate * update
        masters_next.append(master_next)
        lows_next.append(master_next.astype(jnp.bfloat16))
    return (
        layer_out,
        embed_grad.astype(jnp.bfloat16),
        reduced[5],
        reduced[0],
        reduced[1],
        reduced[2],
        reduced[3],
        reduced[4],
        firsts_next[0],
        firsts_next[1],
        firsts_next[2],
        firsts_next[3],
        firsts_next[4],
        seconds_next[0],
        seconds_next[1],
        seconds_next[2],
        seconds_next[3],
        seconds_next[4],
        masters_next[0],
        masters_next[1],
        masters_next[2],
        masters_next[3],
        masters_next[4],
        lows_next[0],
        lows_next[1],
        lows_next[2],
        lows_next[3],
        lows_next[4],
    )


def solution(mesh):
    placed = (
        P(("dp", "fsdp"), None),
        P(None, ("dp", "fsdp")),
        P(("dp", "fsdp")),
        P(("dp", "fsdp"), None),
        P(("dp", "fsdp")),
        P(("dp", "fsdp"), None),
        P(("dp", "fsdp"), None),
        P(("dp", "fsdp"), None),
        P(("dp", "fsdp"), None),
        P(("dp", "fsdp"), None),
        P(("dp", "fsdp"), None),
        P(("dp", "fsdp"), None),
        P(("dp", "fsdp"), None),
        P(("dp", "fsdp"), None),
        P(("dp", "fsdp"), None),
        P(("dp", "fsdp"), None),
        P(("dp", "fsdp"), None),
        P(("dp", "fsdp"), None),
        P(("dp", "fsdp"), None),
        P(("dp", "fsdp"), None),
        P(("dp", "fsdp"), None),
        P(("dp", "fsdp"), None),
        P(("dp", "fsdp"), None),
        P(("dp", "fsdp"), None),
        P(("dp", "fsdp"), None),
        P(),
        P(),
        P(),
        P(),
        P(),
    )
    return jax.shard_map(
        on_device,
        mesh=mesh,
        in_specs=placed,
        out_specs=(
            P(("dp", "fsdp"), None),
            P(("dp", "fsdp"), None),
            P(("dp", "fsdp")),
            P(("dp", "fsdp"), None),
            P(("dp", "fsdp"), None),
            P(("dp", "fsdp"), None),
            P(("dp", "fsdp"), None),
            P(("dp", "fsdp"), None),
            P(("dp", "fsdp"), None),
            P(("dp", "fsdp"), None),
            P(("dp", "fsdp"), None),
            P(("dp", "fsdp"), None),
            P(("dp", "fsdp"), None),
            P(("dp", "fsdp"), None),
            P(("dp", "fsdp"), None),
            P(("dp", "fsdp"), None),
            P(("dp", "fsdp"), None),
            P(("dp", "fsdp"), None),
            P(("dp", "fsdp"), None),
            P(("dp", "fsdp"), None),
            P(("dp", "fsdp"), None),
            P(("dp", "fsdp"), None),
            P(("dp", "fsdp"), None),
            P(("dp", "fsdp"), None),
            P(("dp", "fsdp"), None),
            P(("dp", "fsdp"), None),
            P(("dp", "fsdp"), None),
            P(("dp", "fsdp"), None),
        ),
        check_vma=False,
    )
```

profile of v0, /device:TPU:1, one launch (start us, length us, event | category | flops | bytes accessed | tf_op | source)
XLA Modules:
  0.0 1228.1 jit_solution(8614421171036715747)
XLA Ops:
  11.4 41.0 %all-reduce = bf16[4736]{0:T(1024)(128)(2,1)S(1)} all-reduce(bf16[4736]{0:T(1024)(128)(2,1)S(1)} %dynamic-update-slice), channel_id=1, replica_groups=mesh['dp'=8,'fsdp'=4] {'dp','fsdp'}, use_global_device_ids=true, to_apply=%add | all-reduce | flops 4736 | bytes 18944
  56.7 41.6 %all-gather = bf16[32,4,384]{2,1,0:T(4,128)(2,1)S(1)} all-gather(bf16[1,4,384]{2,1,0:T(4,128)(2,1)S(1)} %convert_bitcast_fusion.6), channel_id=1, replica_groups=mesh['dp'=8,'fsdp'=4] {'dp','fsdp'}, dimensions={0}, use_global_device_ids=true | all-gather | bytes 101376 | tf_op jit(solution)/shard_map/all_gather | solution.py:94
  98.3 37.8 %all-gather.2 = bf16[32,12,384]{2,1,0:T(8,128)(2,1)S(1)} all-gather(bf16[1,12,384]{2,1,0:T(8,128)(2,1)S(1)} %convert_bitcast_fusion.5), channel_id=1, replica_groups=mesh['dp'=8,'fsdp'=4] {'dp','fsdp'}, dimensions={0}, use_global_device_ids=true | all-gather | bytes 304128 | tf_op jit(solution)/shard_map/all_gather | solution.py:91
  136.2 41.4 %all-gather.1 = bf16[32,12,1152]{2,1,0:T(8,128)(2,1)S(1)} all-gather(bf16[1,12,1152]{2,1,0:T(8,128)(2,1)S(1)} %convert_bitcast_fusion.3), channel_id=1, replica_groups=mesh['dp'=8,'fsdp'=4] {'dp','fsdp'}, dimensions={0}, use_global_device_ids=true | all-gather | bytes 912384 | tf_op jit(solution)/shard_map/all_gather | solution.py:90
  207.3 12.6 %copy.220 = bf16[4096,1152]{0,1:T(8,128)(2,1)} copy(bf16[4096,1152]{1,0:T(8,128)(2,1)} %convolution_convert_fusion) | data formatting | bytes 18874368 | tf_op jit(solution)/shard_map/convert_element_type | solution.py:126
  219.9 11.4 copy.272
  235.5 12.5 %fusion.15 = (f32[16,6,256]{2,1,0:T(8,128)S(1)}, f32[16,6,256,256]{2,3,1,0:T(8,128)}) fusion(pred[16,256]{1,0:T(8,128)(4,1)S(1)} %get-tuple-element.193, bf16[16,256,1,6,64]{1,0,4,3,2:T(8,128)(2,1)S(1)} %get-tuple-element.182, bf16[16,256,1,6,64]{1,0,4,3,2:T(8,128)(2,1)S(1)} %get-tuple-element.181), kind=kOutput, calls=%fused_computation.30 | convolution fusion | flops 824156160 | bytes 31559680 | tf_op jit(solution)/shard_map/cqhd,ckhd->chqk/dot_general | solution.py:136
  248.0 11.6 fusion.9
  260.2 13.3 %convert_bitcast_fusion.1 = bf16[16,256,6,64]{1,3,2,0:T(8,128)(2,1)} fusion(f32[16,6,256]{2,1,0:T(8,128)S(1)} %fusion.9, f32[16,6,256]{2,1,0:T(8,128)S(1)} %get-tuple-element.197, f32[16,6,256,256]{2,3,1,0:T(8,128)} %get-tuple-element.198, pred[16,256]{1,0:T(8,128)(4,1)S(1)} %get-tuple-element.193, bf16[16,256,1,6,64]{1,0,4,3,2:T(8,128)(2,1)S(1)} %get-tuple-element.180), kind=kOutput, calls=%fused_computation.60 | convolution fusion | flops 838336512 | bytes 31657984 | tf_op jit(solution)/shard_map/chqk,ckhd->cqhd/dot_general | solution.py:149
  289.2 63.2 %multiply_convert_fusion.1 = (bf16[4096,1536]{1,0:T(8,128)(2,1)}, f32[4096,1536]{1,0:T(8,128)}, f32[4096,1536]{1,0:T(8,128)}) fusion(f32[1536]{0:T(1024)S(1)} %slice.74, bf16[384,1536]{1,0:T(8,128)(2,1)S(1)} %reshape.204, bf16[4096,384]{0,1:T(8,128)(2,1)} %add_convert_fusion.5.clone.4), kind=kOutput, calls=%fused_computation.7 | convolution fusion | flops 5247074304 | bytes 67246080 | tf_op jit(solution)/shard_map/dot_general | solution.py:156
  352.5 32.6 %convert_reduce_fusion = (f32[1536]{0:T(1024)}, bf16[4096,1536]{1,0:T(8,128)(2,1)}) fusion(f32[4096,1536]{1,0:T(8,128)} %get-tuple-element.176, bf16[1536,384]{1,0:T(8,128)(2,1)} %all-gather.13.cloned.1.call-done, bf16[4096,384]{0,1:T(8,128)(2,1)} %copy.227, f32[4096]{0:T(1024)S(1)} %bitcast.266, f32[4096,1536]{1,0:T(8,128)} %get-tuple-element.201, ...), kind=kOutput, calls=%fused_computation.2 | convolution fusion | flops 4943510016 | bytes 67268608 | tf_op jit(solution)/shard_map/tn,kn->tk/dot_general | solution.py:37
  385.2 12.1 fusion.80
  397.3 9.4 fusion.99
  444.6 15.4 %convert_bitcast_fusion = bf16[16,256,1,6,64]{1,4,3,0,2:T(8,128)(2,1)} fusion(f32[16,6,256]{2,1,0:T(8,128)S(1)} %copy-done.20, f32[16,6,256,256]{2,3,1,0:T(8,128)} %get-tuple-element.198, pred[16,256]{1,0:T(8,128)(4,1)S(1)} %copy-done.34, bf16[16,256,6,64]{1,0,3,2:T(8,128)(2,1)} %bitcast.260), kind=kOutput, calls=%fused_computation.59 | convolution fusion | flops 832045056 | bytes 31559680 | tf_op jit(solution)/shard_map/chqk,cqhd->ckhd/dot_general | solution.py:195
  460.0 23.0 %multiply_reduce_fusion = (f32[16,6,256]{2,1,0:T(8,128)S(1)}, f32[16,6,256,256]{2,3,1,0:T(8,128)}) fusion(f32[16,6,256]{2,1,0:T(8,128)S(1)} %copy-done.20, f32[16,6,256,256]{2,3,1,0:T(8,128)} %get-tuple-element.198, pred[16,256]{1,0:T(8,128)(4,1)S(1)} %copy-done.34, bf16[16,256,1,6,64]{1,0,4,3,2:T(8,128)(2,1)} %copy-done.10, ...), kind=kOutput, calls=%fused_computation.4 | convolution fusion | flops 836739072 | bytes 56823808 | tf_op jit(solution)/shard_map/cqhd,ckhd->chqk/dot_general | solution.py:190
  483.0 21.8 %multiply_convert_fusion = bf16[16,6,256,256]{2,3,1,0:T(8,128)(2,1)} fusion(f32[16,6,256,256]{2,3,1,0:T(8,128)} %get-tuple-element.203, f32[16,6,256]{2,1,0:T(8,128)S(1)} %get-tuple-element.202, f32[16,6,256]{2,1,0:T(8,128)S(1)} %copy-done.20, f32[16,6,256,256]{2,3,1,0:T(8,128)} %get-tuple-element.198, pred[16,256]{1,0:T(8,128)(4,1)S(1)} %copy-done.34), kind=kLoop, calls=%fused_computation.3 | loop fusion | flops 37748736 | bytes 63115264 | tf_op jit(solution)/shard_map/convert_element_type | solution.py:194
  504.8 10.8 fusion.19
  515.6 10.0 fusion.18
  534.1 14.0 %copy.235 = bf16[16,256,3,6,64]{1,0,4,3,2:T(8,128)(2,1)} copy(bf16[16,256,3,6,64]{1,4,3,0,2:T(8,128)(2,1)} %pad_maximum_fusion) | data formatting | bytes 18874368 | tf_op jit(solution)/shard_map/stack | solution.py:207
  548.2 13.8 %copy.276 = bf16[144,8,16,256]{3,1,2,0:T(8,128)(2,1)} copy(bf16[144,8,16,256]{3,2,1,0:T(8,128)(2,1)} %bitcast.259) | data formatting | bytes 18874368
  562.0 11.8 fusion.82
  581.9 10.8 fusion.26
  625.6 79.2 %fusion.83 = (f32[16,1152]{1,0:T(8,128)}, f32[16,384]{1,0:T(8,128)}, f32[16,1536]{1,0:T(8,128)}) fusion(f32[384,1152]{1,0:T(8,128)} %fusion.82, f32[384,384]{1,0:T(8,128)S(1)} %fusion.57, f32[384,1536]{1,0:T(8,128)S(1)} %copy-done.18), kind=kCustom, calls=%all-reduce-scatter.3 | all-reduce-scatter fusion | flops 1572865 | bytes 4915200
  797.4 45.7 %reduce-scatter.15.cloned.1.call-done = f32[48,384]{1,0:T(8,128)} async-done(((f32[1536,384]{1,0:T(8,128)}), f32[48,384]{1,0:T(8,128)}) %reduce-scatter.15.cloned.1.call-update) | async-done | bytes 73744 | tf_op jit(solution)/shard_map/reduce_scatter | solution.py:240
  849.7 10.6 add_convert_fusion.1
  876.6 120.0 %all-reduce.20.cloned.1.call-done = (f32[384,1152]{0,1:T(8,128)}, f32[384,384]{0,1:T(8,128)}, f32[384,1536]{0,1:T(8,128)}, f32[128,384]{0,1:T(8,128)}) async-done(((f32[384,1152]{0,1:T(8,128)}, f32[384,384]{0,1:T(8,128)}, f32[384,1536]{0,1:T(8,128)}, f32[128,384]{0,1:T(8,128)}), (f32[384,1152]{0,1:T(8,128)}, f32[384,384]{0,1:T(8,128)}, f32[384,1536]{0,1:T(8,128)}, ...) | async-done | bytes 4915216
  999.3 39.8 %all-reduce.1 = f32[4736]{0:T(1024)S(1)} all-reduce(f32[4736]{0:T(1024)S(1)} %constant_dynamic-update-slice_fusion), channel_id=2, replica_groups=mesh['dp'=8,'fsdp'=4] {'dp','fsdp'}, use_global_device_ids=true, to_apply=%region_20.21.clone | all-reduce | flops 4736 | bytes 37888
  1044.6 42.8 %all-gather.5 = bf16[32,12,384]{2,1,0:T(8,128)(2,1)S(1)} all-gather(bf16[1,12,384]{2,1,0:T(8,128)(2,1)S(1)} %get-tuple-element.165), channel_id=1, replica_groups=mesh['dp'=8,'fsdp'=4] {'dp','fsdp'}, dimensions={0}, use_global_device_ids=true | all-gather | bytes 304128 | tf_op jit(solution)/shard_map/all_gather | solution.py:268
  1088.7 40.1 %all-gather.4 = bf16[32,12,1152]{2,1,0:T(8,128)(2,1)S(1)} all-gather(bf16[1,12,1152]{2,1,0:T(8,128)(2,1)S(1)} %get-tuple-element.168), channel_id=1, replica_groups=mesh['dp'=8,'fsdp'=4] {'dp','fsdp'}, dimensions={0}, use_global_device_ids=true | all-gather | bytes 912384 | tf_op jit(solution)/shard_map/all_gather | solution.py:265
  1130.4 38.7 %all-gather.7 = bf16[32,4,384]{2,1,0:T(4,128)(2,1)S(1)} all-gather(bf16[1,4,384]{2,1,0:T(4,128)(2,1)S(1)} %get-tuple-element.156), channel_id=1, replica_groups=mesh['dp'=8,'fsdp'=4] {'dp','fsdp'}, dimensions={0}, use_global_device_ids=true | all-gather | bytes 101376 | tf_op jit(solution)/shard_map/all_gather | solution.py:277
  1187.3 10.9 fusion.102
  1198.1 19.4 %all-gather.15.cloned.1.call-done = bf16[1536,384]{1,0:T(8,128)(2,1)} async-done(((bf16[48,384]{1,0:T(8,128)(2,1)}), bf16[1536,384]{1,0:T(8,128)(2,1)}) %all-gather.15.cloned.1.call-update) | async-done | bytes 1179664 | tf_op jit(solution)/shard_map/all_gather | solution.py:274
  (371 shorter events, 292.8 us)
Async XLA Ops:
  7.2 279.7 %all-gather.17.cloned.1.call-start = ((), (), s32[]{:S(2)}) async-start(), calls=%async_computation.5 | async-start | bytes 1622016 | tf_op jit(solution)/shard_map/all_gather | solution.py:92
  8.9 343.6 %all-gather.13.cloned.1.call-start = ((), (), s32[]{:S(2)}) async-start(), calls=%async_computation.2 | async-start | bytes 1216512 | tf_op jit(solution)/shard_map/all_gather | solution.py:93
  10.4 774.0 %all-reduce.18.cloned.1.call-start = ((), (), s32[]{:S(2)}) async-start(), calls=%async_computation.8 | async-start | bytes 393216
  619.2 223.9 %reduce-scatter.15.cloned.1.call-start = ((), (), s32[]{:S(2)}) async-start(), calls=%async_computation.3 | async-start | bytes 2433024 | tf_op jit(solution)/shard_map/reduce_scatter | solution.py:240
  625.5 371.1 %all-reduce.20.cloned.1.call-start = ((), (), s32[]{:S(2)}) async-start(), calls=%async_computation.9 | async-start | bytes 9830400
  704.7 16.1 %collective-permute-start.14 = (f32[16,384]{1,0:T(8,128)}, f32[16,384]{1,0:T(8,128)S(1)}, u32[]{:S(2)}, u32[]{:S(2)}) collective-permute-start(f32[16,384]{1,0:T(8,128)} %get-tuple-element.154), channel_id=1, source_target_pairs={{0,7},{1,8},{2,9},{3,10},{4,11},{5,12},{6,13},{7,14},{8,15},{9,16}... | collective-permute-start | bytes 73736
  706.1 17.8 %collective-permute-start.13 = (f32[16,384]{1,0:T(8,128)}, f32[16,384]{1,0:T(8,128)S(1)}, u32[]{:S(2)}, u32[]{:S(2)}) collective-permute-start(f32[16,384]{1,0:T(8,128)} %get-tuple-element.154), channel_id=1, source_target_pairs={{0,6},{1,7},{2,8},{3,9},{4,10},{5,11},{6,12},{7,13},{8,14},{9,15},... | collective-permute-start | bytes 73736
  708.2 11.3 collective-permute-start.15
  709.5 19.4 %collective-permute-start.12 = (f32[16,384]{1,0:T(8,128)}, f32[16,384]{1,0:T(8,128)S(1)}, u32[]{:S(2)}, u32[]{:S(2)}) collective-permute-start(f32[16,384]{1,0:T(8,128)} %get-tuple-element.154), channel_id=1, source_target_pairs={{0,5},{1,6},{2,7},{3,8},{4,9},{5,10},{6,11},{7,12},{8,13},{9,14},{... | collective-permute-start | bytes 73736
  710.8 19.9 %collective-permute-start.11 = (f32[16,384]{1,0:T(8,128)}, f32[16,384]{1,0:T(8,128)S(1)}, u32[]{:S(2)}, u32[]{:S(2)}) collective-permute-start(f32[16,384]{1,0:T(8,128)} %get-tuple-element.154), channel_id=1, source_target_pairs={{0,4},{1,5},{2,6},{3,7},{4,8},{5,9},{6,10},{7,11},{8,12},{9,13},{1... | collective-permute-start | bytes 73736
  719.5 15.2 %collective-permute-start.10 = (f32[16,384]{1,0:T(8,128)}, f32[16,384]{1,0:T(8,128)S(1)}, u32[]{:S(2)}, u32[]{:S(2)}) collective-permute-start(f32[16,384]{1,0:T(8,128)} %get-tuple-element.154), channel_id=1, source_target_pairs={{0,3},{1,4},{2,5},{3,6},{4,7},{5,8},{6,9},{7,10},{8,11},{9,12},{10... | collective-permute-start | bytes 73736
  720.8 15.2 %collective-permute-start.9 = (f32[16,384]{1,0:T(8,128)}, f32[16,384]{1,0:T(8,128)S(1)}, u32[]{:S(2)}, u32[]{:S(2)}) collective-permute-start(f32[16,384]{1,0:T(8,128)} %get-tuple-element.154), channel_id=1, source_target_pairs={{0,2},{1,3},{2,4},{3,5},{4,6},{5,7},{6,8},{7,9},{8,10},{9,11},{10,... | collective-permute-start | bytes 73736
  723.9 14.5 %collective-permute-start.8 = (f32[16,384]{1,0:T(8,128)}, f32[16,384]{1,0:T(8,128)S(1)}, u32[]{:S(2)}, u32[]{:S(2)}) collective-permute-start(f32[16,384]{1,0:T(8,128)} %get-tuple-element.154), channel_id=1, source_target_pairs={{0,1},{1,2},{2,3},{3,4},{4,5},{5,6},{6,7},{7,8},{8,9},{9,10},{10,1... | collective-permute-start | bytes 73736
  728.9 16.0 %collective-permute-start.6 = (f32[16,1152]{1,0:T(8,128)}, f32[16,1152]{1,0:T(8,128)S(1)}, u32[]{:S(2)}, u32[]{:S(2)}) collective-permute-start(f32[16,1152]{1,0:T(8,128)} %get-tuple-element.153), channel_id=1, source_target_pairs={{0,7},{1,8},{2,9},{3,10},{4,11},{5,12},{6,13},{7,14},{8,15},{9,16}... | collective-permute-start | bytes 221192
  730.7 16.7 %collective-permute-start.5 = (f32[16,1152]{1,0:T(8,128)}, f32[16,1152]{1,0:T(8,128)S(1)}, u32[]{:S(2)}, u32[]{:S(2)}) collective-permute-start(f32[16,1152]{1,0:T(8,128)} %get-tuple-element.153), channel_id=1, source_target_pairs={{0,6},{1,7},{2,8},{3,9},{4,10},{5,11},{6,12},{7,13},{8,14},{9,15},... | collective-permute-start | bytes 221192
  734.7 18.4 %collective-permute-start.4 = (f32[16,1152]{1,0:T(8,128)}, f32[16,1152]{1,0:T(8,128)S(1)}, u32[]{:S(2)}, u32[]{:S(2)}) collective-permute-start(f32[16,1152]{1,0:T(8,128)} %get-tuple-element.153), channel_id=1, source_target_pairs={{0,5},{1,6},{2,7},{3,8},{4,9},{5,10},{6,11},{7,12},{8,13},{9,14},{... | collective-permute-start | bytes 221192
  736.0 19.8 %collective-permute-start.3 = (f32[16,1152]{1,0:T(8,128)}, f32[16,1152]{1,0:T(8,128)S(1)}, u32[]{:S(2)}, u32[]{:S(2)}) collective-permute-start(f32[16,1152]{1,0:T(8,128)} %get-tuple-element.153), channel_id=1, source_target_pairs={{0,4},{1,5},{2,6},{3,7},{4,8},{5,9},{6,10},{7,11},{8,12},{9,13},{1... | collective-permute-start | bytes 221192
  738.5 4.5 collective-permute-start.7
  742.9 16.9 %collective-permute-start.2 = (f32[16,1152]{1,0:T(8,128)}, f32[16,1152]{1,0:T(8,128)S(1)}, u32[]{:S(2)}, u32[]{:S(2)}) collective-permute-start(f32[16,1152]{1,0:T(8,128)} %get-tuple-element.153), channel_id=1, source_target_pairs={{0,3},{1,4},{2,5},{3,6},{4,7},{5,8},{6,9},{7,10},{8,11},{9,12},{10... | collective-permute-start | bytes 221192
  744.9 16.9 %collective-permute-start.1 = (f32[16,1152]{1,0:T(8,128)}, f32[16,1152]{1,0:T(8,128)S(1)}, u32[]{:S(2)}, u32[]{:S(2)}) collective-permute-start(f32[16,1152]{1,0:T(8,128)} %get-tuple-element.153), channel_id=1, source_target_pairs={{0,2},{1,3},{2,4},{3,5},{4,6},{5,7},{6,8},{7,9},{8,10},{9,11},{10,... | collective-permute-start | bytes 221192
  747.4 16.0 %collective-permute-start = (f32[16,1152]{1,0:T(8,128)}, f32[16,1152]{1,0:T(8,128)S(1)}, u32[]{:S(2)}, u32[]{:S(2)}) collective-permute-start(f32[16,1152]{1,0:T(8,128)} %get-tuple-element.153), channel_id=1, source_target_pairs={{0,1},{1,2},{2,3},{3,4},{4,5},{5,6},{6,7},{7,8},{8,9},{9,10},{10,1... | collective-permute-start | bytes 221192
  753.1 21.4 %collective-permute-start.22 = (f32[16,1536]{1,0:T(8,128)}, f32[16,1536]{1,0:T(8,128)S(1)}, u32[]{:S(2)}, u32[]{:S(2)}) collective-permute-start(f32[16,1536]{1,0:T(8,128)} %get-tuple-element.155), channel_id=1, source_target_pairs={{0,7},{1,8},{2,9},{3,10},{4,11},{5,12},{6,13},{7,14},{8,15},{9,16}... | collective-permute-start | bytes 294920
  755.8 20.6 %collective-permute-start.21 = (f32[16,1536]{1,0:T(8,128)}, f32[16,1536]{1,0:T(8,128)S(1)}, u32[]{:S(2)}, u32[]{:S(2)}) collective-permute-start(f32[16,1536]{1,0:T(8,128)} %get-tuple-element.155), channel_id=1, source_target_pairs={{0,6},{1,7},{2,8},{3,9},{4,10},{5,11},{6,12},{7,13},{8,14},{9,15},... | collective-permute-start | bytes 294920
  759.8 23.3 %collective-permute-start.20 = (f32[16,1536]{1,0:T(8,128)}, f32[16,1536]{1,0:T(8,128)S(1)}, u32[]{:S(2)}, u32[]{:S(2)}) collective-permute-start(f32[16,1536]{1,0:T(8,128)} %get-tuple-element.155), channel_id=1, source_target_pairs={{0,5},{1,6},{2,7},{3,8},{4,9},{5,10},{6,11},{7,12},{8,13},{9,14},{... | collective-permute-start | bytes 294920
  761.8 21.3 %collective-permute-start.19 = (f32[16,1536]{1,0:T(8,128)}, f32[16,1536]{1,0:T(8,128)S(1)}, u32[]{:S(2)}, u32[]{:S(2)}) collective-permute-start(f32[16,1536]{1,0:T(8,128)} %get-tuple-element.155), channel_id=1, source_target_pairs={{0,4},{1,5},{2,6},{3,7},{4,8},{5,9},{6,10},{7,11},{8,12},{9,13},{1... | collective-permute-start | bytes 294920
  763.3 8.6 collective-permute-start.23
  771.9 11.2 collective-permute-start.18
  774.5 8.6 collective-permute-start.17
  776.4 6.7 collective-permute-start.16
  797.3 331.5 %reduce-scatter.17.cloned.1.call-start = ((), (), s32[]{:S(2)}) async-start(), calls=%async_computation.7 | async-start | bytes 2433024 | tf_op jit(solution)/shard_map/reduce_scatter | solution.py:252
  849.4 335.0 %all-gather.19.cloned.1.call-start = ((), (), s32[]{:S(2)}) async-start(), calls=%async_computation.6 | async-start | bytes 1622016 | tf_op jit(solution)/shard_map/all_gather | solution.py:271
  999.3 218.3 %all-gather.15.cloned.1.call-start = ((), (), s32[]{:S(2)}) async-start(), calls=%async_computation.4 | async-start | bytes 1216512 | tf_op jit(solution)/shard_map/all_gather | solution.py:274
  (91 other events, 5697.9 us)
Sparse Core Ops, SparseCore 0:
  11.5 57.4 all-gather.16
  72.5 52.9 all-gather.12
  619.3 119.3 all-reduce.17
  744.4 98.6 reduce-scatter.14
  850.3 146.2 all-reduce.19
  1002.6 98.3 reduce-scatter.16
  1104.4 56.7 all-gather.18
  1164.6 52.8 all-gather.14
where the time goes:
time: 1240 us; the launch traced here: 1230 us
  blocking collectives  402 us (32%)
  matrix products  338 us (27%)
  waiting for transfers between devices  185 us (15%)
  local copies, waits for them, and re-layouts  138 us (11%)
  other arithmetic  88.2 us (7%)
  starting transfers between devices  60.9 us (5%)
  between operations  16.3 us (1%)
    unnamed x3, blocking collectives  160 us
    unnamed x34, waiting for transfers between devices  120 us
    unnamed x226, local copies, waits for them, and re-layouts  83.2 us
    dot_general x1, matrix products, on_device(): jnp.dot(normed_two_low, w_up, preferred_element_type=jnp.float32) + up_bias  63.2 us
    unnamed x26, starting transfers between devices  60 us
    dot_general x5, matrix products, right_product(): jnp.einsum('tn,kn->tk', grads, weight, preferred_element_type=jnp.float32)  58.9 us
    reduce_scatter x1, waiting for transfers between devices, on_device(): lax.psum_scatter(down_grad, ('dp', 'fsdp'), scatter_dimension=0, tiled=True)  45.7 us
    all_gather x1, blocking collectives, on_device(): lax.all_gather(directions[1].astype(jnp.bfloat16), ('dp', 'fsdp'), axis=0...  42.8 us
  transfers between devices with their start and end apart: 32, of which 3 were waited for; matrix products, arithmetic and copies ran while one was open for 30% of the time, Pallas kernels for 0%

commit v1 on v0

v1 whole, which is shorter than its diff:
```python
import functools
import jax
import jax.numpy as jnp
from jax import lax
from jax.experimental import pallas as pl
from jax.experimental.pallas import tpu as pltpu
from jax.sharding import PartitionSpec as P

D = 384
HEADS = 6
HEAD = 64
FF = 1536
PH = 128
LMAX = 256
LANES = 128
EPSILON = 1e-05
NEG_FILL = -1e30
HIGHEST = lax.Precision.HIGHEST
BF = jnp.bfloat16
F32 = jnp.float32

QKV_AT, UP_AT, OUT_AT, DOWN_AT, POS_AT, BLOCKS = 0, 9, 21, 24, 36, 37
FLAT_ROWS = 14336
SMALL_ROWS = 37


def nn(a, b):
    return jnp.dot(a, b, preferred_element_type=F32)


def nt(a, b):
    return lax.dot_general(a, b, (((1,), (1,)), ((), ())), preferred_element_type=F32)


def tn(a, b):
    return lax.dot_general(a, b, (((0,), (0,)), ((), ())), preferred_element_type=F32)


INV_SQRT2 = 0.7071067811865476
INV_SQRT_2PI = 0.3989422804014327


def gelu_pair(x):
    cdf = 0.5 * (1.0 + lax.erf(x * INV_SQRT2))
    pdf = jnp.exp(-0.5 * x * x) * INV_SQRT_2PI
    return x * cdf, cdf + x * pdf


def norm_parts(x):
    mean = jnp.mean(x, axis=-1, keepdims=True)
    centred = x - mean
    spread = jnp.mean(centred * centred, axis=-1, keepdims=True)
    inv = lax.rsqrt(spread + EPSILON)
    return centred * inv, inv


def col8(x):
    rows, cols = x.shape
    return jnp.sum(x.reshape(rows // 8, 8, cols), axis=0)


def layer_kernel(
    len_ref,
    tok_ref,
    cen_ref,
    cot_ref,
    small_ref,
    wqkv_ref,
    wout_ref,
    wup_ref,
    wdown_ref,
    wpos_ref,
    out_ref,
    gtok_ref,
    grad_ref,
    sgrad_ref,
    sacc,
    posh_s,
    emb_s,
    xh1_s,
    n1_s,
    qkv_s,
    p_s,
    att_s,
    bin_s,
    n2g_s,
    ff_s,
    qg_s,
    *,
    fc,
):
    step = pl.program_id(0)
    last = pl.num_programs(0) - 1

    @pl.when(step == 0)
    def _():
        grad_ref[...] = jnp.zeros_like(grad_ref)
        sacc[...] = jnp.zeros_like(sacc)

    length = len_ref[step]

    def vec(at, blocks):
        return jnp.concatenate([small_ref[at + i : at + i + 1, :] for i in range(blocks)], axis=1)

    def add_small(at, value):
        cols = value.shape[1]
        sacc[:, at * LANES : at * LANES + cols] += value

    def add_grad(block, value):
        for i in range(value.shape[1] // LANES):
            rows = slice((block + i) * D, (block + i + 1) * D)
            grad_ref[rows, :] += value[:, i * LANES : (i + 1) * LANES]

    gain_one, shift_one, gain_two, shift_two, attn_bias, down_bias, embed_bias = (
        vec(3 * i, 3) for i in range(7)
    )
    hidden_bias = small_ref[33:34, :]
    pos_first = small_ref[34:37, :]
    cen = cen_ref[...]

    pos_hidden = (
        lax.dot_general(
            cen, pos_first, (((0,), (0,)), ((), ())), precision=HIGHEST, preferred_element_type=F32
        )
        + hidden_bias
    )
    pos_act, pos_slope = gelu_pair(pos_hidden)
    pos_low = pos_act.astype(BF)
    posh_s[...] = pos_slope
    embedded = tok_ref[...].astype(F32) + nn(pos_low, wpos_ref[...]) + embed_bias
    emb_s[...] = embedded
    xhat_one, inv_one = norm_parts(embedded)
    xh1_s[...] = xhat_one
    n1 = (xhat_one * gain_one + shift_one).astype(BF)
    n1_s[...] = n1
    qkv_s[...] = nn(n1, wqkv_ref[...]).astype(BF)

    key_live = lax.broadcasted_iota(jnp.int32, (LMAX, LMAX), 0) < length
    lane = lax.broadcasted_iota(jnp.int32, (1, LANES), 1)
    halves = [(lane < HEAD).astype(F32).astype(BF), (lane >= HEAD).astype(F32).astype(BF)]
    scale = HEAD ** (-0.5)
    scaled = [(h.astype(F32) * scale).astype(BF) for h in halves]

    for pair in range(HEADS // 2):
        cols = slice(pair * LANES, (pair + 1) * LANES)
        q = qkv_s[:, cols]
        k = qkv_s[:, D + pair * LANES : D + (pair + 1) * LANES]
        v = qkv_s[:, 2 * D + pair * LANES : 2 * D + (pair + 1) * LANES]
        v_t = v.T
        for h in range(2):
            s = nt(k, q * scaled[h])
            s = jnp.where(key_live, s, NEG_FILL)
            top = jnp.max(s, axis=0, keepdims=True)
            e = jnp.exp(s - top)
            total = jnp.sum(e, axis=0, keepdims=True)
            p = (e * (1.0 / total)).astype(BF)
            p_s[2 * pair + h] = p
            o_t = nn(v_t[h * HEAD : (h + 1) * HEAD, :], p)
            att_s[pair * LANES + h * HEAD : pair * LANES + (h + 1) * HEAD, :] = o_t.astype(BF)

    branch_in = emb_s[...] + tn(att_s[...], wout_ref[...]) + attn_bias
    bin_s[...] = branch_in
    xhat_two, inv_two = norm_parts(branch_in)
    n2 = (xhat_two * gain_two + shift_two).astype(BF)
    n2_t = n2.T
    row_live = lax.broadcasted_iota(jnp.int32, (LMAX, D), 0) < length
    gy = jnp.where(row_live, cot_ref[...].astype(F32), 0.0)
    gy_low = gy.astype(BF)
    gy_t = gy_low.T
    add_small(15, col8(gy))

    for c in range(FF // fc):
        cols = slice(c * fc, (c + 1) * fc)
        up_bias = vec(21 + c * (fc // LANES), fc // LANES)
        hidden = nn(n2, wup_ref[:, cols]) + up_bias
        act, slope = gelu_pair(hidden)
        act_low = act.astype(BF)
        part = nn(act_low, wdown_ref[cols, :])
        act_grad = nt(gy_low, wdown_ref[cols, :])
        hg = (act_grad * slope).astype(BF)
        add_small(21 + c * (fc // LANES), col8(hg.astype(F32)))
        back = nt(hg, wup_ref[:, cols])
        if c == 0:
            ff_s[...] = part
            n2g_s[...] = back
        else:
            ff_s[...] += part
            n2g_s[...] += back
        add_grad(UP_AT + c * (fc // LANES), nn(n2_t, hg))
        add_grad(DOWN_AT + c * (fc // LANES), nn(gy_t, act_low))

    out_ref[...] = (bin_s[...] + ff_s[...] + down_bias).astype(BF)

    n2g = n2g_s[...]
    add_small(6, col8(n2g * xhat_two))
    add_small(9, col8(n2g))
    u = n2g * gain_two
    bg = gy + inv_two * (
        u
        - jnp.mean(u, axis=-1, keepdims=True)
        - xhat_two * jnp.mean(u * xhat_two, axis=-1, keepdims=True)
    )
    bin_s[...] = bg
    add_small(12, col8(bg))
    bg_low = bg.astype(BF)
    add_grad(OUT_AT, nn(att_s[...], bg_low))
    ag = nt(bg_low, wout_ref[...]).astype(BF)

    for pair in range(HEADS // 2):
        cols = slice(pair * LANES, (pair + 1) * LANES)
        q = qkv_s[:, cols]
        k = qkv_s[:, D + pair * LANES : D + (pair + 1) * LANES]
        v = qkv_s[:, 2 * D + pair * LANES : 2 * D + (pair + 1) * LANES]
        k_t = k.T
        ago = ag[:, cols]
        dq_t = []
        dk = None
        dv = None
        for h in range(2):
            p_low = p_s[2 * pair + h]
            p = p_low.astype(F32)
            ago_h = ago * halves[h]
            dp = nt(v, ago_h)
            rd = jnp.sum(p * dp, axis=0, keepdims=True)
            ds = (p * (dp - rd)).astype(BF)
            dv_h = nn(p_low, ago_h)
            dk_h = nn(ds, q * scaled[h])
            dv = dv_h if dv is None else dv + dv_h
            dk = dk_h if dk is None else dk + dk_h
            dq_t.append((nn(k_t[h * HEAD : (h + 1) * HEAD, :], ds) * scale).astype(BF))
        qg_s[:, cols] = jnp.concatenate(dq_t, axis=0).T
        qg_s[:, D + pair * LANES : D + (pair + 1) * LANES] = dk.astype(BF)
        qg_s[:, 2 * D + pair * LANES : 2 * D + (pair + 1) * LANES] = dv.astype(BF)

    qg = qg_s[...]
    add_grad(QKV_AT, nn(n1_s[...].T, qg))
    n1g = nt(qg, wqkv_ref[...])
    xhat = xh1_s[...]
    add_small(0, col8(n1g * xhat))
    add_small(3, col8(n1g))
    u = n1g * gain_one
    eg = bin_s[...] + inv_one * (
        u
        - jnp.mean(u, axis=-1, keepdims=True)
        - xhat * jnp.mean(u * xhat, axis=-1, keepdims=True)
    )
    add_small(18, col8(eg))
    eg_low = eg.astype(BF)
    gtok_ref[...] = eg_low
    add_grad(POS_AT, tn(eg_low, pos_low))
    phg = nt(eg_low, wpos_ref[...]) * posh_s[...]
    add_small(33, col8(phg))
    pf_grad = jnp.dot(cen, phg, precision=HIGHEST, preferred_element_type=F32)
    for i in range(3):
        sacc[0:1, (34 + i) * LANES : (35 + i) * LANES] += pf_grad[i : i + 1, :]

    @pl.when(step == last)
    def _():
        for i in range(SMALL_ROWS):
            sgrad_ref[i : i + 1, :] = jnp.sum(
                sacc[:, i * LANES : (i + 1) * LANES], axis=0, keepdims=True
            )


def layer_pass(tokens, centres, lengths, cotangent, small_rows, wqkv, wout, wup, wdown, wpos, fc=512):
    clouds = lengths.shape[0]
    rows = clouds * LMAX
    whole = lambda shape: pl.BlockSpec(shape, lambda i, *_: (0, 0), pipeline_mode=pl.Buffered(1))
    tile = lambda: pl.BlockSpec((LMAX, D), lambda i, *_: (i, 0))
    return pl.pallas_call(
        functools.partial(layer_kernel, fc=fc),
        out_shape=(
            jax.ShapeDtypeStruct((rows, D), BF),
            jax.ShapeDtypeStruct((rows, D), BF),
            jax.ShapeDtypeStruct((FLAT_ROWS, LANES), F32),
            jax.ShapeDtypeStruct((SMALL_ROWS, LANES), F32),
        ),
        grid_spec=pltpu.PrefetchScalarGridSpec(
            num_scalar_prefetch=1,
            grid=(clouds,),
            in_specs=[
                tile(),
                pl.BlockSpec((3, LMAX), lambda i, *_: (0, i)),
                tile(),
                whole((SMALL_ROWS, LANES)),
                whole((D, 3 * D)),
                whole((D, D)),
                whole((D, FF)),
                whole((FF, D)),
                whole((PH, D)),
            ],
            out_specs=[
                tile(),
                tile(),
                whole((FLAT_ROWS, LANES)),
                whole((SMALL_ROWS, LANES)),
            ],
            scratch_shapes=[
                pltpu.VMEM((8, SMALL_ROWS * LANES), F32),
                pltpu.VMEM((LMAX, PH), F32),
                pltpu.VMEM((LMAX, D), F32),
                pltpu.VMEM((LMAX, D), F32),
                pltpu.VMEM((LMAX, D), BF),
                pltpu.VMEM((LMAX, 3 * D), BF),
                pltpu.VMEM((HEADS, LMAX, LMAX), BF),
                pltpu.VMEM((D, LMAX), BF),
                pltpu.VMEM((LMAX, D), F32),
                pltpu.VMEM((LMAX, D), F32),
                pltpu.VMEM((LMAX, D), F32),
                pltpu.VMEM((LMAX, 3 * D), BF),
            ],
        ),
        compiler_params=pltpu.CompilerParams(vmem_limit_bytes=60 * 1024 * 1024),
        name="layer",
    )(lengths, tokens, centres, cotangent, small_rows, wqkv, wout, wup, wdown, wpos)


MESH_ID = pl.DeviceIdType.MESH


def mesh_roles(mesh):
    dp, fs = mesh.shape["dp"], mesh.shape["fsdp"]
    if dp >= 32:
        return {
            "z": ("dp", dp // 4 // 2, 4) if dp == 32 else ("dp", 8, dp // 8),
            "y": ("dp", 2, 4),
            "c": ("dp", 1, 2),
            "x": ("fsdp", 1, fs),
        }
    return {
        "z": ("dp", 2, dp // 2),
        "y": ("dp", 1, 2),
        "x": ("fsdp", 2, fs // 2),
        "c": ("fsdp", 1, 2),
    }


def flipped(coord, offset, size):
    if offset == 0:
        return coord
    if size == 2:
        return 1 - coord
    return {1: coord + 1 - 2 * (coord % 2), 2: (coord + 2) % 4, 3: 3 - coord}[offset]


class Grid:
    def __init__(self, roles, sizes):
        self.roles, self.sizes = roles, sizes
        self.index = {axis: lax.axis_index(axis) for axis in sizes}
        self.coord = {
            role: (self.index[axis] // stride) % size
            for role, (axis, stride, size) in roles.items()
        }

    def place(self, **offsets):
        at = dict(self.index)
        for role, offset in offsets.items():
            axis, stride, size = self.roles[role]
            other = flipped(self.coord[role], offset, size)
            at[axis] = at[axis] + (other - self.coord[role]) * stride
        return at

    def slot(self, **offsets):
        at = self.place(**offsets)
        return at["dp"] * self.sizes["fsdp"] + at["fsdp"]

    def size(self, role):
        return self.roles[role][2]

    def offsets(self, role):
        return range(1, self.size(role))


class Wire:
    def __init__(self, grid, send_sems, recv_sems):
        self.grid, self.send_sems, self.recv_sems = grid, send_sems, recv_sems
        self.copies = {}

    def send(self, key, source, target, **offsets):
        number = len(self.copies)
        copy = pltpu.make_async_remote_copy(
            src_ref=source,
            dst_ref=target,
            send_sem=self.send_sems.at[number],
            recv_sem=self.recv_sems.at[number],
            device_id=self.grid.place(**offsets),
            device_id_type=MESH_ID,
        )
        copy.start()
        assert key not in self.copies
        self.copies[key] = copy

    def arrived(self, key):
        self.copies[key].wait_recv()

    def finish(self):
        for copy in self.copies.values():
            copy.wait_send()


def meet(grid):
    barrier = pltpu.get_barrier_semaphore()
    count = 0
    for role in ("z", "y", "x", "c"):
        for offset in grid.offsets(role):
            pl.semaphore_signal(
                barrier,
                inc=1,
                device_id=grid.place(**{role: offset}),
                device_id_type=MESH_ID,
            )
            count += 1
    pl.semaphore_wait(barrier, count)


def gather_copies(roles):
    nz, ny, nx, nc = (roles[role][2] for role in ("z", "y", "x", "c"))
    plane = (ny - 1) + (nx - 1) + 2 * (ny - 1) * (nx - 1)
    core = (nc - 1) * (1 + plane)
    return (nz - 1) + nz * (plane + core)


def gather_all(grid, wire, buf):
    rows = buf.shape[1]
    half = rows // 32 * 16
    parts = {"a": pl.ds(0, half), "b": pl.ds(half, rows - half)}

    def pass_on(key, slot, part, **offsets):
        ref = buf.at[slot] if part is None else buf.at[slot, parts[part]]
        wire.send(("gather",) + key, ref, ref, **offsets)

    zs, ys, xs, cs = ([*grid.offsets(role)] for role in ("z", "y", "x", "c"))

    def to_core(key, slot, part=None):
        for c in cs:
            pass_on(("c", c) + key, slot, part, c=c)

    def have(b):
        slot = grid.slot(z=b)
        for y in ys:
            pass_on(("y", b, y), slot, None, y=y)
        for x in xs:
            pass_on(("x", b, x), slot, None, x=x)
        to_core((b, 0, 0, 0), slot)

    def relay(b):
        for y in ys:
            wire.arrived(("gather", "y", b, y))
            for x in xs:
                pass_on(("a", b, y, x), grid.slot(z=b, y=y), "a", x=x)
            to_core((b, y, 0, 0), grid.slot(z=b, y=y))
        for x in xs:
            wire.arrived(("gather", "x", b, x))
            for y in ys:
                pass_on(("b", b, y, x), grid.slot(z=b, x=x), "b", y=y)
            to_core((b, 0, x, 0), grid.slot(z=b, x=x))

    for z in zs:
        pass_on(("z", z), grid.slot(), None, z=z)
    have(0)
    for b in zs:
        wire.arrived(("gather", "z", b))
        have(b)
        relay(b - 1)
    relay(len(zs))
    for b in [0] + zs:
        for y in ys:
            for x in xs:
                for part in ("a", "b"):
                    wire.arrived(("gather", part, b, y, x))
                    to_core((b, y, x, part), grid.slot(z=b, y=y, x=x), part)
    for key in list(wire.copies):
        if key[:2] == ("gather", "c"):
            wire.arrived(key)


def reduce_copies(roles):
    nz, ny, nx, nc = (roles[role][2] for role in ("z", "y", "x", "c"))
    plane = (ny - 1) + (nx - 1) + 2 * (ny - 1) * (nx - 1)
    return (nc - 1) * nz * ny * nx + nz * plane + (nz - 1)


def small_copies(roles):
    return sum(roles[role][2] - 1 for role in ("z", "y", "x", "c"))


def reduce_scatter(grid, wire, full, small, acc, out_c, in_c, out_p, in_p, out_z, in_z, s_out, s_in, extra):
    rows = full.shape[1]
    half = rows // 32 * 16
    first, second = pl.ds(0, half), pl.ds(half, rows - half)
    zs, ys, xs, cs = ([*grid.offsets(role)] for role in ("z", "y", "x", "c"))
    order = zs + [0]

    small_order = ["c", "y", "x", "z"]
    small_state = {"value": small[...], "stage": 0}

    def small_send():
        stage = small_state["stage"]
        role = small_order[stage]
        s_out[stage] = small_state["value"]
        for offset in grid.offsets(role):
            number = extra[(role, offset)]
            wire.send(("s", role, offset), s_out.at[stage], s_in.at[number], **{role: offset})

    def small_take():
        stage = small_state["stage"]
        role = small_order[stage]
        value = small_state["value"]
        for offset in grid.offsets(role):
            wire.arrived(("s", role, offset))
            value = value + s_in[extra[(role, offset)]]
        small_state["value"] = value
        small_state["stage"] = stage + 1

    small_send()
    for b in order:
        for y in [0] + ys:
            for x in [0] + xs:
                for c in cs:
                    out_c[c - 1, b, y, x] = full[grid.slot(z=b, y=y, x=x, c=c)].astype(BF)
                    wire.send(
                        ("c", c, b, y, x), out_c.at[c - 1, b, y, x], in_c.at[c - 1, b, y, x], c=c
                    )

    def core_sum(b, y, x):
        value = full[grid.slot(z=b, y=y, x=x)]
        for c in cs:
            wire.arrived(("c", c, b, y, x))
            value = value + in_c[c - 1, b, y, x].astype(F32)
        return value

    def diagonal(b):
        for y in ys:
            for x in xs:
                out_p[b, y, x] = core_sum(b, y, x).astype(BF)
                wire.send(("a", b, y, x), out_p.at[b, y, x, first], in_p.at[b, y, x, first], x=x)
                wire.send(("b", b, y, x), out_p.at[b, y, x, second], in_p.at[b, y, x, second], y=y)

    def neighbour(b):
        for y in ys:
            acc[...] = core_sum(b, y, 0)
            for x in xs:
                wire.arrived(("a", b, y, x))
                acc[first, :] += in_p[b, y, x, first].astype(F32)
            out_p[b, y, 0] = acc[...].astype(BF)
            wire.send(("y", b, y), out_p.at[b, y, 0], in_p.at[b, y, 0], y=y)
        for x in xs:
            acc[...] = core_sum(b, 0, x)
            for y in ys:
                wire.arrived(("b", b, y, x))
                acc[second, :] += in_p[b, y, x, second].astype(F32)
            out_p[b, 0, x] = acc[...].astype(BF)
            wire.send(("x", b, x), out_p.at[b, 0, x], in_p.at[b, 0, x], x=x)

    def plane_sum(b):
        value = core_sum(b, 0, 0)
        for y in ys:
            wire.arrived(("y", b, y))
            value = value + in_p[b, y, 0].astype(F32)
        for x in xs:
            wire.arrived(("x", b, x))
            value = value + in_p[b, 0, x].astype(F32)
        return value

    total = None
    for turn in range(len(order) + 2):
        if turn < len(order):
            diagonal(order[turn])
        if 1 <= turn <= len(order):
            neighbour(order[turn - 1])
            if small_state["stage"] < 3:
                small_take()
                small_send()
        if turn >= 2:
            b = order[turn - 2]
            value = plane_sum(b)
            if b:
                out_z[b - 1] = value.astype(BF)
                wire.send(("z", b), out_z.at[b - 1], in_z.at[b - 1], z=b)
            else:
                total = value
    small_take()
    for b in zs:
        wire.arrived(("z", b))
        total = total + in_z[b - 1].astype(F32)
    return total, small_state["value"]


DECAY = 0.5
ADAM_EPSILON = 1e-08
WEIGHT_DECAY = 0.05
VMEM_LIMIT = 60 * 1024 * 1024
NAMES = ("qkv", "out", "up", "down", "pos")
HEIGHT = {"qkv": D, "out": D, "up": D, "down": FF, "pos": PH}
WIDTH = {"qkv": 3 * D, "out": D, "up": FF, "down": D, "pos": D}
SMALLS = SMALL_ROWS * LANES


def pad16(rows):
    return -(-rows // 16) * 16


class Layout:
    def __init__(self, count, smalls):
        self.count = count
        self.rows = {name: HEIGHT[name] // count for name in NAMES}
        self.padded = {name: pad16(self.rows[name]) for name in NAMES}
        self.start = {}
        at = 0
        for name in NAMES:
            self.start[name] = at
            at += self.padded[name] * (WIDTH[name] // LANES)
        self.small_at = at
        self.small_len = SMALLS // count
        if smalls:
            at += 16
        self.total = at

    def span(self, name, block):
        at = self.start[name] + block * self.padded[name]
        return slice(at, at + self.padded[name])

    def spread(self, name):
        rows, padded = self.rows[name], self.padded[name]
        shape = (HEIGHT[name], self.count * padded)
        row = lax.broadcasted_iota(jnp.int32, shape, 0)
        col = lax.broadcasted_iota(jnp.int32, shape, 1)
        own, owner = col % padded, col // padded
        hit = (own < rows) & (owner * rows + own == row)
        return hit.astype(F32).astype(BF)


def pad_rows(value, rows):
    have = value.shape[0]
    if have == rows:
        return value
    return jnp.concatenate([value, jnp.zeros((rows - have, value.shape[1]), value.dtype)], axis=0)


def head_kernel(roles, sizes, lay, *refs):
    masters = dict(zip(NAMES, refs[:5]))
    small_ref = refs[5]
    outs = dict(zip(NAMES, refs[6:11]))
    flat_ref, buf, send_sems, recv_sems = refs[11:]
    grid = Grid(roles, sizes)
    wire = Wire(grid, send_sems, recv_sems)
    own = grid.slot()
    for name in NAMES:
        for block in range(WIDTH[name] // LANES):
            piece = masters[name][:, block * LANES : (block + 1) * LANES]
            buf[own, lay.span(name, block), :] = pad_rows(piece, lay.padded[name]).astype(BF)
    buf[own, lay.small_at : lay.small_at + 16, :] = pad_rows(small_ref[...], 16).astype(BF)
    meet(grid)
    gather_all(grid, wire, buf)
    for name in NAMES:
        spread = None if lay.rows[name] == lay.padded[name] else lay.spread(name)
        for block in range(WIDTH[name] // LANES):
            piece = buf[:, lay.span(name, block), :].reshape(lay.count * lay.padded[name], LANES)
            if spread is not None:
                piece = nn(spread, piece).astype(BF)
            outs[name][:, block * LANES : (block + 1) * LANES] = piece
    lane = lax.broadcasted_iota(jnp.int32, (1, LANES), 1)
    for row in range(SMALL_ROWS):
        line = jnp.zeros((1, LANES), F32)
        at = row * LANES
        while at < (row + 1) * LANES:
            owner, place = at // lay.small_len, at % lay.small_len
            source_row, source_lane = place // LANES, place % LANES
            take = min(
                (row + 1) * LANES - at, lay.small_len - place, LANES - source_lane
            )
            target = at - row * LANES
            piece = buf[owner, lay.small_at : lay.small_at + 16, :].astype(F32)
            piece = piece[source_row : source_row + 1, :]
            shift = (target - source_lane) % LANES
            if shift:
                piece = pltpu.roll(piece, shift, 1)
            line = jnp.where((lane >= target) & (lane < target + take), piece, line)
            at += take
        flat_ref[row : row + 1, :] = line
    wire.finish()


def vmem():
    return pl.BlockSpec(memory_space=pltpu.VMEM)


def gather_weights(roles, sizes, lay, masters, smalls):
    count = gather_copies(roles)
    lines = -(-lay.small_len // LANES)
    padded = jnp.pad(smalls, (0, lines * LANES - lay.small_len)).reshape(lines, LANES)
    return pl.pallas_call(
        functools.partial(head_kernel, roles, sizes, lay),
        out_shape=tuple(jax.ShapeDtypeStruct((HEIGHT[n], WIDTH[n]), BF) for n in NAMES)
        + (jax.ShapeDtypeStruct((SMALL_ROWS, LANES), F32),),
        in_specs=[vmem()] * 6,
        out_specs=tuple([vmem()] * 6),
        scratch_shapes=[
            pltpu.VMEM((lay.count, lay.total, LANES), BF),
            pltpu.SemaphoreType.DMA((count,)),
            pltpu.SemaphoreType.DMA((count,)),
        ],
        compiler_params=pltpu.CompilerParams(
            collective_id=0, has_side_effects=True, vmem_limit_bytes=VMEM_LIMIT
        ),
        name="gather_weights",
    )(*masters, padded)


def reduce_kernel(roles, sizes, extra, full, small, out, small_out, acc, out_c, in_c, out_p, in_p, out_z, in_z, s_out, s_in, send_sems, recv_sems):
    grid = Grid(roles, sizes)
    wire = Wire(grid, send_sems, recv_sems)
    meet(grid)
    total, smalls = reduce_scatter(
        grid, wire, full, small, acc, out_c, in_c, out_p, in_p, out_z, in_z, s_out, s_in, extra
    )
    small_out[...] = smalls
    out[grid.slot()] = total.astype(BF)
    gather_all(grid, wire, out)
    wire.finish()


def reduce_all(roles, sizes, full, small):
    slots, rows, _ = full.shape
    nz, ny, nx, nc = (roles[role][2] for role in ("z", "y", "x", "c"))
    count = reduce_copies(roles) + small_copies(roles) + gather_copies(roles)
    extra = {}
    for role in ("c", "y", "x", "z"):
        for offset in range(1, roles[role][2]):
            extra[(role, offset)] = len(extra)
    return pl.pallas_call(
        functools.partial(reduce_kernel, roles, sizes, extra),
        out_shape=(
            jax.ShapeDtypeStruct((slots, rows, LANES), BF),
            jax.ShapeDtypeStruct((SMALL_ROWS, LANES), F32),
        ),
        in_specs=[vmem()] * 2,
        out_specs=(vmem(), vmem()),
        scratch_shapes=[
            pltpu.VMEM((rows, LANES), F32),
            pltpu.VMEM((nc - 1, nz, ny, nx, rows, LANES), BF),
            pltpu.VMEM((nc - 1, nz, ny, nx, rows, LANES), BF),
            pltpu.VMEM((nz, ny, nx, rows, LANES), BF),
            pltpu.VMEM((nz, ny, nx, rows, LANES), BF),
            pltpu.VMEM((nz - 1, rows, LANES), BF),
            pltpu.VMEM((nz - 1, rows, LANES), BF),
            pltpu.VMEM((4, SMALL_ROWS, LANES), F32),
            pltpu.VMEM((len(extra), SMALL_ROWS, LANES), F32),
            pltpu.SemaphoreType.DMA((count,)),
            pltpu.SemaphoreType.DMA((count,)),
        ],
        compiler_params=pltpu.CompilerParams(
            collective_id=1, has_side_effects=True, vmem_limit_bytes=VMEM_LIMIT
        ),
        name="reduce_all",
    )(full, small)


def split(value):
    high = value.astype(BF)
    return jnp.concatenate([high, (value - high.astype(F32)).astype(BF)], axis=0)


def joined(value):
    half = value.shape[0] // 2
    return value[:half] + value[half:]


def turn_kernel(lay, chunk, index_ref, flat, *refs):
    lefts, rights, firsts, seconds, grads, firsts_next, seconds_next = (
        dict(zip(NAMES, refs[5 * i : 5 * i + 5])) for i in range(7)
    )
    slot = refs[35]
    me = index_ref[0]
    starts = {"qkv": QKV_AT, "up": UP_AT, "out": OUT_AT, "down": DOWN_AT, "pos": POS_AT}
    for name in NAMES:
        height, width = HEIGHT[name], WIDTH[name]
        rows, padded = lay.rows[name], lay.padded[name]
        row = lax.broadcasted_iota(jnp.int32, (padded, height), 0)
        col = lax.broadcasted_iota(jnp.int32, (padded, height), 1)
        pick = ((row < rows) & (col == me * rows + row)).astype(F32).astype(BF)
        left_rows = nt(pick, lefts[name][...]).astype(BF)
        lhs = jnp.concatenate([left_rows, pick], axis=0)
        blocks = []
        if name in ("down", "pos"):
            both = None
            for block in range(height // LANES):
                at = (starts[name] + block) * D
                part = nt(lhs[:, block * LANES : (block + 1) * LANES], flat[at : at + D, :])
                both = part if both is None else both + part
        else:
            for block in range(width // LANES):
                at = (starts[name] + block) * D
                blocks.append(nn(lhs, flat[at : at + D, :]))
            both = jnp.concatenate(blocks, axis=1)
        grads[name][...] = both[padded : padded + rows]
        terms = split(both[:padded])
        for at in range(0, width, chunk):
            cols = slice(at, at + chunk)
            rotated = joined(nn(terms, rights[name][:, cols].astype(BF)))[:rows]
            first = DECAY * firsts[name][:, cols] + (1.0 - DECAY) * rotated
            second = DECAY * seconds[name][:, cols] + (1.0 - DECAY) * rotated * rotated
            firsts_next[name][:, cols] = first
            seconds_next[name][:, cols] = second
            direction = pad_rows(first / (jnp.sqrt(second) + ADAM_EPSILON), padded).astype(BF)
            for i in range(chunk // LANES):
                slot[lay.span(name, at // LANES + i), :] = direction[:, i * LANES : (i + 1) * LANES]


def turn_in(lay, index, flat, lefts, rights, firsts, seconds):
    shapes = [jax.ShapeDtypeStruct((lay.rows[n], WIDTH[n]), F32) for n in NAMES]
    return pl.pallas_call(
        functools.partial(turn_kernel, lay, D),
        out_shape=tuple(shapes * 3) + (jax.ShapeDtypeStruct((lay.total, LANES), BF),),
        in_specs=[pl.BlockSpec(memory_space=pltpu.SMEM)] + [vmem()] * 21,
        out_specs=tuple([vmem()] * 16),
        compiler_params=pltpu.CompilerParams(vmem_limit_bytes=VMEM_LIMIT),
        name="turn_in",
    )(index, flat, *lefts, *rights, *firsts, *seconds)


def steps_kernel(roles, sizes, slot, buf, send_sems, recv_sems):
    grid = Grid(roles, sizes)
    wire = Wire(grid, send_sems, recv_sems)
    buf[grid.slot()] = slot[...]
    meet(grid)
    gather_all(grid, wire, buf)
    wire.finish()


def gather_steps(roles, sizes, lay, slot):
    count = gather_copies(roles)
    return pl.pallas_call(
        functools.partial(steps_kernel, roles, sizes),
        out_shape=jax.ShapeDtypeStruct((lay.count, lay.total, LANES), BF),
        in_specs=[vmem()],
        out_specs=vmem(),
        scratch_shapes=[
            pltpu.SemaphoreType.DMA((count,)),
            pltpu.SemaphoreType.DMA((count,)),
        ],
        compiler_params=pltpu.CompilerParams(
            collective_id=2, has_side_effects=True, vmem_limit_bytes=VMEM_LIMIT
        ),
        name="gather_steps",
    )(slot)


def back_kernel(lay, chunk, steps, *refs):
    lefts, rights, masters, nexts, lows = (
        dict(zip(NAMES, refs[5 * i : 5 * i + 5])) for i in range(5)
    )
    for name in NAMES:
        height, width = HEIGHT[name], WIDTH[name]
        rows, padded = lay.rows[name], lay.padded[name]
        left = split(pad_rows(lefts[name][...], padded))
        if rows != padded:
            left = nn(left, lay.spread(name)).astype(BF)
        parts = []
        for block in range(width // LANES):
            piece = steps[:, lay.span(name, block), :].reshape(lay.count * padded, LANES)
            parts.append(joined(nn(left, piece)))
        partway = split(jnp.concatenate(parts, axis=1))
        rate = height ** (-0.5)
        for at in range(0, width, chunk):
            cols = slice(at, at + chunk)
            update = joined(nt(partway, rights[name][cols, :].astype(BF)))[:rows]
            master = masters[name][:, cols] * (1.0 - rate * WEIGHT_DECAY) - rate * update
            nexts[name][:, cols] = master
            lows[name][:, cols] = master.astype(BF)


def turn_back(lay, steps, lefts, rights, masters):
    shapes = [(lay.rows[n], WIDTH[n]) for n in NAMES]
    return pl.pallas_call(
        functools.partial(back_kernel, lay, D),
        out_shape=tuple(jax.ShapeDtypeStruct(s, F32) for s in shapes)
        + tuple(jax.ShapeDtypeStruct(s, BF) for s in shapes),
        in_specs=[vmem()] * 16,
        out_specs=tuple([vmem()] * 10),
        compiler_params=pltpu.CompilerParams(vmem_limit_bytes=VMEM_LIMIT),
        name="turn_back",
    )(steps, *lefts, *rights, *masters)


AXES = ("dp", "fsdp")


def on_device(roles, sizes, tokens, centres, lengths, cotangent, smalls, *matrices):
    masters, firsts, seconds, lefts, rights = (matrices[5 * i : 5 * i + 5] for i in range(5))
    count = sizes["dp"] * sizes["fsdp"]
    heads = Layout(count, True)
    lay = Layout(count, False)
    *weights, small_rows = gather_weights(roles, sizes, heads, masters, smalls)
    w_qkv, w_out, w_up, w_down, w_pos = weights
    later = lax.optimization_barrier((small_rows,) + tuple(left.astype(BF) for left in lefts))
    small_rows = later[0]
    whole_lefts = [lax.all_gather(left, AXES, axis=0, tiled=True) for left in later[1:]]
    layer_out, grad_tokens, full, small_grads = layer_pass(
        tokens, centres, lengths, cotangent, small_rows, w_qkv, w_out, w_up, w_down, w_pos
    )
    flat, small_total = reduce_all(
        roles, sizes, full.reshape(count, FLAT_ROWS // count, LANES), small_grads
    )
    me = lax.axis_index("dp") * sizes["fsdp"] + lax.axis_index("fsdp")
    grad_smalls = lax.dynamic_slice(
        small_total.reshape(SMALLS), (me * heads.small_len,), (heads.small_len,)
    )
    *turned, slot = turn_in(
        lay,
        me.reshape(1),
        flat.reshape(FLAT_ROWS, LANES),
        whole_lefts,
        rights,
        firsts,
        seconds,
    )
    steps = gather_steps(roles, sizes, lay, slot)
    updated = turn_back(lay, steps, lefts, rights, masters)
    return (layer_out, grad_tokens, grad_smalls, *turned, *updated)


def solution(mesh):
    sizes = {axis: mesh.shape[axis] for axis in AXES}
    rows, flat = P(AXES, None), P(AXES)
    return jax.shard_map(
        functools.partial(on_device, mesh_roles(mesh), sizes),
        mesh=mesh,
        in_specs=(rows, P(None, AXES), flat, rows, flat) + (rows,) * 20 + (P(),) * 5,
        out_specs=(rows, rows, flat) + (rows,) * 25,
        check_vma=False,
    )
```

time: 1240 us -> 504 us (0.41)
  matrix products: 338 us -> 0 us
  Pallas kernels: 0 us -> 321 us
  blocking collectives: 402 us -> 158 us
  waiting for transfers between devices: 185 us -> 0.02 us
  local copies, waits for them, and re-layouts: 138 us -> 4.96 us
  other arithmetic: 88.2 us -> 4.53 us
  starting transfers between devices: 60.9 us -> 0.04 us
    dot_general x43 -> x0, matrix products: 338 us -> none  [the longest x1 63.2 us: on_device(): jnp.dot(normed_two_low, w_up, preferred_element_type=jnp.float32) + up_bias]
    pallas_call x0 -> x6, Pallas kernels: none -> 321 us  [the longest x1 168 us: layer_pass(): pl.pallas_call(functools.partial(layer_kernel, fc=fc), out_shape=(jax.Sha...]
    unnamed x3 -> x0, blocking collectives: 160 us -> none
    unnamed x34 -> x1, waiting for transfers between devices: 120 us -> 0.02 us
    all_gather x6 -> x4, blocking collectives: 242 us -> 158 us  [on_device(): lax.all_gather(left, AXES, axis=0, tiled=True)]
    unnamed x226 -> x3, local copies, waits for them, and re-layouts: 83.2 us -> 2.38 us
    unnamed x26 -> x0, starting transfers between devices: 60 us -> none
    reduce_scatter x2 -> x0, waiting for transfers between devices: 45.7 us -> none  [the longest x1 45.7 us: on_device(): lax.psum_scatter(down_grad, ('dp', 'fsdp'), scatter_dimension=0, tiled=True)]
  transfers between devices with their start and end apart: 32 -> 1, of which waited for: 3 -> 0; matrix products, arithmetic and copies ran while one was open for 30% -> 1% of each run, Pallas kernels for 0% -> 44%
where the time goes in v1:
time: 504 us; the launch traced here: 503 us
  Pallas kernels  321 us (64%)
  blocking collectives  158 us (31%)
  between operations  14.1 us (3%)
    pallas_call x1, Pallas kernels, layer_pass(): pl.pallas_call(functools.partial(layer_kernel, fc=fc), out_shape=(jax.Sha...  168 us
    all_gather x4, blocking collectives, on_device(): lax.all_gather(left, AXES, axis=0, tiled=True)  158 us
    pallas_call x1, Pallas kernels, reduce_all(): pl.pallas_call(functools.partial(reduce_kernel, roles, sizes, extra), out...  55.8 us
    pallas_call x1, Pallas kernels, gather_weights(): pl.pallas_call(functools.partial(head_kernel, roles, sizes, lay), out_sha...  39.5 us
    pallas_call x1, Pallas kernels, gather_steps(): pl.pallas_call(functools.partial(steps_kernel, roles, sizes), out_shape=j...  32.6 us
    pallas_call x1, Pallas kernels, turn_in(): pl.pallas_call(functools.partial(turn_kernel, lay, D), out_shape=tuple(sh...  13.6 us
    pallas_call x1, Pallas kernels, turn_back(): pl.pallas_call(functools.partial(back_kernel, lay, D), out_shape=tuple((j...  11.9 us
  transfers between devices with their start and end apart: 1, of which 0 were waited for; matrix products, arithmetic and copies ran while one was open for 1% of the time, Pallas kernels for 44%

profile of v1, /device:TPU:1, one launch (start us, length us, event | category | flops | bytes accessed | tf_op | source)
XLA Modules:
  0.0 503.0 jit_solution(8006991492004593541)
XLA Ops:
  7.2 0.0 all-gather.6.cloned.1.call-start
  7.2 1.2 pad_bitcast_fusion.refs_5_
  8.5 0.7 convert_element_type.17
  9.2 0.7 convert_element_type.18
  10.0 0.7 convert_element_type.19
  10.7 1.6 convert_element_type.20
  12.3 0.7 convert_element_type.21
  13.0 39.5 %gather_weights.1 = (bf16[384,1152]{1,0:T(8,128)(2,1)}, bf16[384,384]{1,0:T(8,128)(2,1)}, bf16[384,1536]{1,0:T(8,128)(2,1)}, bf16[1536,384]{1,0:T(8,128)(2,1)}, ...) custom-call(f32[12,1152]{1,0:T(8,128)} %refs_10_.3, f32[12,384]{1,0:T(8,128)} %refs_11_.3, f32[12,1536]{1,0:T(8,128)} %refs_12_.3, ...), custom_call_target="tpu_custom_call" | custom-call | tf_op jit(solution)/shard_map/gather_weights/pallas_call | solution.py:692
  52.6 0.0 all-gather.6.cloned.1.call-update
  52.6 39.1 %all-gather = bf16[32,12,384]{2,1,0:T(8,128)(2,1)S(1)} all-gather(bf16[1,12,384]{2,1,0:T(8,128)(2,1)S(1)} %bitcast.16), channel_id=1, replica_groups=mesh['dp'=8,'fsdp'=4] {'dp','fsdp'}, dimensions={0}, use_global_device_ids=true | all-gather | bytes 304128 | tf_op jit(solution)/shard_map/all_gather | solution.py:898
  91.7 0.8 reshape.77.refs_0_
  92.5 38.1 %all-gather.1 = bf16[32,12,384]{2,1,0:T(8,128)(2,1)S(1)} all-gather(bf16[1,12,384]{2,1,0:T(8,128)(2,1)S(1)} %bitcast.15), channel_id=1, replica_groups=mesh['dp'=8,'fsdp'=4] {'dp','fsdp'}, dimensions={0}, use_global_device_ids=true | all-gather | bytes 304128 | tf_op jit(solution)/shard_map/all_gather | solution.py:898
  130.6 0.8 reshape.79.refs_1_
  131.4 39.4 %all-gather.2 = bf16[32,12,384]{2,1,0:T(8,128)(2,1)S(1)} all-gather(bf16[1,12,384]{2,1,0:T(8,128)(2,1)S(1)} %bitcast.14), channel_id=1, replica_groups=mesh['dp'=8,'fsdp'=4] {'dp','fsdp'}, dimensions={0}, use_global_device_ids=true | all-gather | bytes 304128 | tf_op jit(solution)/shard_map/all_gather | solution.py:898
  170.8 0.8 reshape.81.refs_2_
  171.6 167.6 %layer.1 = (bf16[4096,384]{1,0:T(8,128)(2,1)}, bf16[4096,384]{1,0:T(8,128)(2,1)}, f32[14336,128]{1,0:T(8,128)}, f32[37,128]{1,0:T(8,128)}) custom-call(s32[16]{0:T(128)} %len_ref.1, bf16[4096,384]{1,0:T(8,128)(2,1)} %tok_ref.1, f32[3,4096]{1,0:T(4,128)} %cen_ref.1, bf16[4096,384]{1,0:T(8,128)(2,1)} %cot_ref.1, f32[37,128]{1,0:T(8,128)} %get-tuple-element.73.small_ref, ...), custom_call_target="tpu_custom_call" | custom-call | tf_op jit(solution)/shard_map/layer/pallas_call | solution.py:270
  339.2 55.8 %reduce_all.1 = (bf16[32,448,128]{2,1,0:T(8,128)(2,1)}, f32[37,128]{1,0:T(8,128)}) custom-call(f32[32,448,128]{2,1,0:T(8,128)} %bitcast.11, f32[37,128]{1,0:T(8,128)} %get-tuple-element.82.small), custom_call_target="tpu_custom_call" | custom-call | tf_op jit(solution)/shard_map/reduce_all/pallas_call | solution.py:731
  395.0 1.3 dynamic_slice.3
  396.3 41.8 %all-gather.3 = bf16[32,4,128]{2,1,0:T(4,128)(2,1)} all-gather(bf16[1,4,128]{2,1,0:T(4,128)(2,1)S(1)} %bitcast.17), channel_id=1, replica_groups=mesh['dp'=8,'fsdp'=4] {'dp','fsdp'}, dimensions={0}, use_global_device_ids=true | all-gather | bytes 33792 | tf_op jit(solution)/shard_map/all_gather | solution.py:898
  438.1 0.0 all-gather.6.cloned.1.call-done.refs_3_
  438.1 13.6 %turn_in.1 = (f32[12,1152]{1,0:T(8,128)}, f32[12,384]{1,0:T(8,128)}, f32[12,1536]{1,0:T(8,128)}, f32[48,384]{1,0:T(8,128)}, f32[4,384]{1,0:T(4,128)}, /*index=5*...) custom-call(s32[1]{0:T(128)} %bitcast.3.index_ref, ...), custom_call_target="tpu_custom_call" | custom-call | tf_op jit(solution)/shard_map/turn_in/pallas_call | solution.py:812
  451.7 32.6 %gather_steps.1.steps = bf16[32,576,128]{2,1,0:T(8,128)(2,1)} custom-call(bf16[576,128]{1,0:T(8,128)(2,1)} %get-tuple-element.105.slot), custom_call_target="tpu_custom_call" | custom-call | tf_op jit(solution)/shard_map/gather_steps/pallas_call | solution.py:833
  484.2 11.9 %turn_back.1 = (f32[12,1152]{1,0:T(8,128)}, f32[12,384]{1,0:T(8,128)}, f32[12,1536]{1,0:T(8,128)}, f32[48,384]{1,0:T(8,128)}, f32[4,384]{1,0:T(4,128)}, /*index=...) custom-call(bf16[32,576,128]{2,1,0:T(8,128)(2,1)} %gather_steps.1.st, ...), custom_call_target="tpu_custom_call" | custom-call | tf_op jit(solution)/shard_map/turn_back/pallas_call | solution.py:875
Async XLA Ops:
  7.2 430.9 %all-gather.6.cloned.1.call-start = ((), (), s32[]{:S(2)}) async-start(), calls=%async_computation | async-start | bytes 4866048 | tf_op jit(solution)/shard_map/all_gather | solution.py:898
Sparse Core Ops, SparseCore 0:
  52.7 63.3 all-gather.5

commit v2 on v1

--- a/solution.py
+++ b/solution.py
@@ -420,7 +420,7 @@
     return (nz - 1) + nz * (plane + core)
 
 
-def gather_all(grid, wire, buf):
+def gather_all(grid, wire, buf, meanwhile=None):
     rows = buf.shape[1]
     half = rows // 32 * 16
     parts = {"a": pl.ds(0, half), "b": pl.ds(half, rows - half)}
@@ -458,6 +458,8 @@
     for z in zs:
         pass_on(("z", z), grid.slot(), None, z=z)
     have(0)
+    if meanwhile is not None:
+        meanwhile()
     for b in zs:
         wire.arrived(("gather", "z", b))
         have(b)
@@ -616,6 +618,16 @@
             at += 16
         self.total = at
 
+    @property
+    def base_rows(self):
+        return self.padded["down"] + 16
+
+    def base_place(self, name):
+        if name == "down":
+            return slice(0, self.padded["down"]), slice(0, FF)
+        at = {"qkv": 0, "out": D, "up": 2 * D, "pos": 3 * D}[name]
+        return slice(self.padded["down"], self.base_rows), slice(at, at + HEIGHT[name])
+
     def span(self, name, block):
         at = self.start[name] + block * self.padded[name]
         return slice(at, at + self.padded[name])
@@ -640,8 +652,9 @@
 def head_kernel(roles, sizes, lay, *refs):
     masters = dict(zip(NAMES, refs[:5]))
     small_ref = refs[5]
-    outs = dict(zip(NAMES, refs[6:11]))
-    flat_ref, buf, send_sems, recv_sems = refs[11:]
+    lefts = dict(zip(NAMES, refs[6:11]))
+    outs = dict(zip(NAMES, refs[11:16]))
+    flat_ref, bases, buf, send_sems, recv_sems = refs[16:]
     grid = Grid(roles, sizes)
     wire = Wire(grid, send_sems, recv_sems)
     own = grid.slot()
@@ -650,8 +663,15 @@
             piece = masters[name][:, block * LANES : (block + 1) * LANES]
             buf[own, lay.span(name, block), :] = pad_rows(piece, lay.padded[name]).astype(BF)
     buf[own, lay.small_at : lay.small_at + 16, :] = pad_rows(small_ref[...], 16).astype(BF)
+
+    def pack_bases():
+        bases[lay.padded["down"] :, :] = jnp.zeros((16, FF), BF)
+        for name in NAMES:
+            rows, cols = lay.base_place(name)
+            bases[rows, cols] = pad_rows(lefts[name][...], rows.stop - rows.start).astype(BF)
+
     meet(grid)
-    gather_all(grid, wire, buf)
+    gather_all(grid, wire, buf, pack_bases)
     for name in NAMES:
         spread = None if lay.rows[name] == lay.padded[name] else lay.spread(name)
         for block in range(WIDTH[name] // LANES):
@@ -685,16 +705,19 @@
     return pl.BlockSpec(memory_space=pltpu.VMEM)
 
 
-def gather_weights(roles, sizes, lay, masters, smalls):
+def gather_weights(roles, sizes, lay, masters, smalls, lefts):
     count = gather_copies(roles)
     lines = -(-lay.small_len // LANES)
     padded = jnp.pad(smalls, (0, lines * LANES - lay.small_len)).reshape(lines, LANES)
     return pl.pallas_call(
         functools.partial(head_kernel, roles, sizes, lay),
         out_shape=tuple(jax.ShapeDtypeStruct((HEIGHT[n], WIDTH[n]), BF) for n in NAMES)
-        + (jax.ShapeDtypeStruct((SMALL_ROWS, LANES), F32),),
-        in_specs=[vmem()] * 6,
-        out_specs=tuple([vmem()] * 6),
+        + (
+            jax.ShapeDtypeStruct((SMALL_ROWS, LANES), F32),
+            jax.ShapeDtypeStruct((lay.base_rows, FF), BF),
+        ),
+        in_specs=[vmem()] * 11,
+        out_specs=tuple([vmem()] * 7),
         scratch_shapes=[
             pltpu.VMEM((lay.count, lay.total, LANES), BF),
             pltpu.SemaphoreType.DMA((count,)),
@@ -704,7 +727,7 @@
             collective_id=0, has_side_effects=True, vmem_limit_bytes=VMEM_LIMIT
         ),
         name="gather_weights",
-    )(*masters, padded)
+    )(*masters, padded, *lefts)
 
 
 def reduce_kernel(roles, sizes, extra, full, small, out, small_out, acc, out_c, in_c, out_p, in_p, out_z, in_z, s_out, s_in, send_sems, recv_sems):
@@ -766,11 +789,11 @@
     return value[:half] + value[half:]
 
 
-def turn_kernel(lay, chunk, index_ref, flat, *refs):
-    lefts, rights, firsts, seconds, grads, firsts_next, seconds_next = (
-        dict(zip(NAMES, refs[5 * i : 5 * i + 5])) for i in range(7)
-    )
-    slot = refs[35]
+def turn_kernel(lay, chunk, index_ref, flat, bases, *refs):
+    rights, firsts, seconds, grads, firsts_next, seconds_next = (
+        dict(zip(NAMES, refs[5 * i : 5 * i + 5])) for i in range(6)
+    )
+    slot = refs[30]
     me = index_ref[0]
     starts = {"qkv": QKV_AT, "up": UP_AT, "out": OUT_AT, "down": DOWN_AT, "pos": POS_AT}
     for name in NAMES:
@@ -779,7 +802,11 @@
         row = lax.broadcasted_iota(jnp.int32, (padded, height), 0)
         col = lax.broadcasted_iota(jnp.int32, (padded, height), 1)
         pick = ((row < rows) & (col == me * rows + row)).astype(F32).astype(BF)
-        left_rows = nt(pick, lefts[name][...]).astype(BF)
+        base_rows, base_cols = lay.base_place(name)
+        base = bases[:, base_rows, base_cols]
+        left_rows = nt(pick, base.reshape(base.shape[0] * base.shape[1], height)).astype(BF)
+        if rows != padded:
+            left_rows = nt(left_rows, lay.spread(name)).astype(BF)
         lhs = jnp.concatenate([left_rows, pick], axis=0)
         blocks = []
         if name in ("down", "pos"):
@@ -807,16 +834,16 @@
                 slot[lay.span(name, at // LANES + i), :] = direction[:, i * LANES : (i + 1) * LANES]
 
 
-def turn_in(lay, index, flat, lefts, rights, firsts, seconds):
+def turn_in(lay, index, flat, bases, rights, firsts, seconds):
     shapes = [jax.ShapeDtypeStruct((lay.rows[n], WIDTH[n]), F32) for n in NAMES]
     return pl.pallas_call(
         functools.partial(turn_kernel, lay, D),
         out_shape=tuple(shapes * 3) + (jax.ShapeDtypeStruct((lay.total, LANES), BF),),
-        in_specs=[pl.BlockSpec(memory_space=pltpu.SMEM)] + [vmem()] * 21,
+        in_specs=[pl.BlockSpec(memory_space=pltpu.SMEM)] + [vmem()] * 17,
         out_specs=tuple([vmem()] * 16),
         compiler_params=pltpu.CompilerParams(vmem_limit_bytes=VMEM_LIMIT),
         name="turn_in",
-    )(index, flat, *lefts, *rights, *firsts, *seconds)
+    )(index, flat, bases, *rights, *firsts, *seconds)
 
 
 def steps_kernel(roles, sizes, slot, buf, send_sems, recv_sems):
@@ -891,11 +918,9 @@
     count = sizes["dp"] * sizes["fsdp"]
     heads = Layout(count, True)
     lay = Layout(count, False)
-    *weights, small_rows = gather_weights(roles, sizes, heads, masters, smalls)
+    *weights, small_rows, bases = gather_weights(roles, sizes, heads, masters, smalls, lefts)
     w_qkv, w_out, w_up, w_down, w_pos = weights
-    later = lax.optimization_barrier((small_rows,) + tuple(left.astype(BF) for left in lefts))
-    small_rows = later[0]
-    whole_lefts = [lax.all_gather(left, AXES, axis=0, tiled=True) for left in later[1:]]
+    whole_bases = lax.all_gather(bases, AXES, axis=0, tiled=True)
     layer_out, grad_tokens, full, small_grads = layer_pass(
         tokens, centres, lengths, cotangent, small_rows, w_qkv, w_out, w_up, w_down, w_pos
     )
@@ -910,7 +935,7 @@
         lay,
         me.reshape(1),
         flat.reshape(FLAT_ROWS, LANES),
-        whole_lefts,
+        whole_bases.reshape(count, heads.base_rows, FF),
         rights,
         firsts,
         seconds,

time: 504 us -> 338 us (0.67)
  blocking collectives: 158 us -> 0 us
    all_gather x4 -> x0, blocking collectives: 158 us -> none  [on_device(): lax.all_gather(left, AXES, axis=0, tiled=True)]
  transfers between devices with their start and end apart: 1 -> 1, of which waited for: 0 -> 0; matrix products, arithmetic and copies ran while one was open for 1% -> 0% of each run, Pallas kernels for 44% -> 65%
where the time goes in v2:
time: 338 us
  Pallas kernels  321 us (95%)
  between operations  14.1 us (4%)
    pallas_call x1, Pallas kernels, layer_pass(): pl.pallas_call(functools.partial(layer_kernel, fc=fc), out_shape=(jax.Sha...  168 us
    pallas_call x1, Pallas kernels, reduce_all(): pl.pallas_call(functools.partial(reduce_kernel, roles, sizes, extra), out...  53.1 us
    pallas_call x1, Pallas kernels, gather_weights(): pl.pallas_call(functools.partial(head_kernel, roles, sizes, lay), out_sha...  39.7 us
    pallas_call x1, Pallas kernels, gather_steps(): pl.pallas_call(functools.partial(steps_kernel, roles, sizes), out_shape=j...  34.3 us
    pallas_call x1, Pallas kernels, turn_in(): pl.pallas_call(functools.partial(turn_kernel, lay, D), out_shape=tuple(sh...  14.5 us
    pallas_call x1, Pallas kernels, turn_back(): pl.pallas_call(functools.partial(back_kernel, lay, D), out_shape=tuple((j...  11.9 us
  transfers between devices with their start and end apart: 1, of which 0 were waited for; matrix products, arithmetic and copies ran while one was open for 0% of the time, Pallas kernels for 65%

profile of v2, /device:TPU:1, one launch (start us, length us, event | category | flops | bytes accessed | tf_op | source)
XLA Modules:
  0.0 337.9 jit_solution(1297775047353977407)
XLA Ops:
  7.2 0.0 all-gather.2.cloned.1.call-start
  7.2 1.2 pad_bitcast_fusion.refs_5_
  8.5 39.7 %gather_weights.1 = (bf16[384,1152]{1,0:T(8,128)(2,1)}, bf16[384,384]{1,0:T(8,128)(2,1)}, bf16[384,1536]{1,0:T(8,128)(2,1)}, bf16[1536,384]{1,0:T(8,128)(2,1)}, ...) custom-call(f32[12,1152]{1,0:T(8,128)} %refs_10_.5, f32[12,384]{1,0:T(8,128)} %refs_11_.3, ...), custom_call_target="tpu_custom_call" | custom-call | tf_op jit(solution)/shard_map/gather_weights/pallas_call | solution.py:712
  48.2 0.0 all-gather.2.cloned.1.call-update
  48.2 167.6 %layer.1 = (bf16[4096,384]{1,0:T(8,128)(2,1)}, bf16[4096,384]{1,0:T(8,128)(2,1)}, f32[14336,128]{1,0:T(8,128)}, f32[37,128]{1,0:T(8,128)}) custom-call(s32[16]{0:T(128)} %len_ref.1, bf16[4096,384]{1,0:T(8,128)(2,1)} %tok_ref.1, f32[3,4096]{1,0:T(4,128)} %cen_ref.1, bf16[4096,384]{1,0:T(8,128)(2,1)} %cot_ref.1, f32[37,128]{1,0:T(8,128)} %get-tuple-element.67.small_ref, ...), custom_call_target="tpu_custom_call" | custom-call | tf_op jit(solution)/shard_map/layer/pallas_call | solution.py:270
  215.8 53.1 %reduce_all.1 = (bf16[32,448,128]{2,1,0:T(8,128)(2,1)}, f32[37,128]{1,0:T(8,128)}) custom-call(f32[32,448,128]{2,1,0:T(8,128)} %bitcast.7, f32[37,128]{1,0:T(8,128)} %get-tuple-element.76.small), custom_call_target="tpu_custom_call" | custom-call | tf_op jit(solution)/shard_map/reduce_all/pallas_call | solution.py:754
  268.9 1.3 dynamic_slice.3
  270.3 0.0 all-gather.2.cloned.1.call-done
  270.3 14.5 %turn_in.1 = (f32[12,1152]{1,0:T(8,128)}, f32[12,384]{1,0:T(8,128)}, f32[12,1536]{1,0:T(8,128)}, f32[48,384]{1,0:T(8,128)}, f32[4,384]{1,0:T(4,128)}, /*index=5*...) custom-call(s32[1]{0:T(128)} %bitcast.3.index_ref, ...), custom_call_target="tpu_custom_call" | custom-call | tf_op jit(solution)/shard_map/turn_in/pallas_call | solution.py:839
  284.8 34.3 %gather_steps.1.steps = bf16[32,576,128]{2,1,0:T(8,128)(2,1)} custom-call(bf16[576,128]{1,0:T(8,128)(2,1)} %get-tuple-element.95.slot), custom_call_target="tpu_custom_call" | custom-call | tf_op jit(solution)/shard_map/gather_steps/pallas_call | solution.py:860
  319.1 11.9 %turn_back.1 = (f32[12,1152]{1,0:T(8,128)}, f32[12,384]{1,0:T(8,128)}, f32[12,1536]{1,0:T(8,128)}, f32[48,384]{1,0:T(8,128)}, f32[4,384]{1,0:T(4,128)}, /*index=...) custom-call(bf16[32,576,128]{2,1,0:T(8,128)(2,1)} %gather_steps.1.st, ...), custom_call_target="tpu_custom_call" | custom-call | tf_op jit(solution)/shard_map/turn_back/pallas_call | solution.py:902
Async XLA Ops:
  7.2 263.1 %all-gather.2.cloned.1.call-start = ((), (), s32[]{:S(2)}) async-start(), calls=%async_computation | async-start | bytes 6488064 | tf_op jit(solution)/shard_map/all_gather | solution.py:923
Sparse Core Ops, SparseCore 0:
  48.3 67.4 all-gather.1

commit v3 on v2

--- a/solution.py
+++ b/solution.py
@@ -86,8 +86,13 @@
     n2g_s,
     ff_s,
     qg_s,
+    wide_s,
+    ds_s,
+    dq_s,
+    ag_s,
     *,
     fc,
+    group,
 ):
     step = pl.program_id(0)
     last = pl.num_programs(0) - 1
@@ -97,7 +102,13 @@
         grad_ref[...] = jnp.zeros_like(grad_ref)
         sacc[...] = jnp.zeros_like(sacc)
 
-    length = len_ref[step]
+    rows = group * LMAX
+    lengths = [len_ref[step * group + i] for i in range(group)]
+
+    def live(width):
+        return jnp.concatenate(
+            [lax.broadcasted_iota(jnp.int32, (LMAX, width), 0) < length for length in lengths], axis=0
+        )
 
     def vec(at, blocks):
         return jnp.concatenate([small_ref[at + i : at + i + 1, :] for i in range(blocks)], axis=1)
@@ -135,36 +146,49 @@
     n1_s[...] = n1
     qkv_s[...] = nn(n1, wqkv_ref[...]).astype(BF)
 
-    key_live = lax.broadcasted_iota(jnp.int32, (LMAX, LMAX), 0) < length
     lane = lax.broadcasted_iota(jnp.int32, (1, LANES), 1)
     halves = [(lane < HEAD).astype(F32).astype(BF), (lane >= HEAD).astype(F32).astype(BF)]
     scale = HEAD ** (-0.5)
     scaled = [(h.astype(F32) * scale).astype(BF) for h in halves]
 
-    for pair in range(HEADS // 2):
-        cols = slice(pair * LANES, (pair + 1) * LANES)
-        q = qkv_s[:, cols]
-        k = qkv_s[:, D + pair * LANES : D + (pair + 1) * LANES]
-        v = qkv_s[:, 2 * D + pair * LANES : 2 * D + (pair + 1) * LANES]
-        v_t = v.T
-        for h in range(2):
-            s = nt(k, q * scaled[h])
-            s = jnp.where(key_live, s, NEG_FILL)
-            top = jnp.max(s, axis=0, keepdims=True)
-            e = jnp.exp(s - top)
-            total = jnp.sum(e, axis=0, keepdims=True)
-            p = (e * (1.0 / total)).astype(BF)
-            p_s[2 * pair + h] = p
-            o_t = nn(v_t[h * HEAD : (h + 1) * HEAD, :], p)
-            att_s[pair * LANES + h * HEAD : pair * LANES + (h + 1) * HEAD, :] = o_t.astype(BF)
+    key_live = [
+        lax.broadcasted_iota(jnp.int32, (LMAX, LMAX), 0) < length for length in lengths
+    ]
+    spans = [slice(i * LMAX, (i + 1) * LMAX) for i in range(group)]
+
+    heads = [(i, head) for head in range(HEADS) for i in range(group)]
+
+    def lanes_of(which, i, head):
+        at = which * D + head // 2 * LANES
+        return qkv_s[spans[i], at : at + LANES]
+
+    def staged(*stages):
+        for turn in range(len(heads) + len(stages) - 1):
+            for lag, stage in enumerate(stages):
+                if 0 <= turn - lag < len(heads):
+                    stage(turn - lag, *heads[turn - lag])
+
+    def scores(number, i, head):
+        wide_s[number % 3] = nt(lanes_of(1, i, head), lanes_of(0, i, head) * scaled[head % 2])
+
+    def soften(number, i, head):
+        s = jnp.where(key_live[i], wide_s[number % 3], NEG_FILL)
+        e = jnp.exp(s - jnp.max(s, axis=0, keepdims=True))
+        p_s[i * HEADS + head] = (e * (1.0 / jnp.sum(e, axis=0, keepdims=True))).astype(BF)
+
+    def attend(number, i, head):
+        at = head % 2 * HEAD
+        o_t = nn(lanes_of(2, i, head).T[at : at + HEAD, :], p_s[i * HEADS + head])
+        att_s[head * HEAD : (head + 1) * HEAD, spans[i]] = o_t.astype(BF)
+
+    staged(scores, soften, attend)
 
     branch_in = emb_s[...] + tn(att_s[...], wout_ref[...]) + attn_bias
     bin_s[...] = branch_in
     xhat_two, inv_two = norm_parts(branch_in)
     n2 = (xhat_two * gain_two + shift_two).astype(BF)
     n2_t = n2.T
-    row_live = lax.broadcasted_iota(jnp.int32, (LMAX, D), 0) < length
-    gy = jnp.where(row_live, cot_ref[...].astype(F32), 0.0)
+    gy = jnp.where(live(D), cot_ref[...].astype(F32), 0.0)
     gy_low = gy.astype(BF)
     gy_t = gy_low.T
     add_small(15, col8(gy))
@@ -206,31 +230,37 @@
     add_grad(OUT_AT, nn(att_s[...], bg_low))
     ag = nt(bg_low, wout_ref[...]).astype(BF)
 
-    for pair in range(HEADS // 2):
-        cols = slice(pair * LANES, (pair + 1) * LANES)
-        q = qkv_s[:, cols]
-        k = qkv_s[:, D + pair * LANES : D + (pair + 1) * LANES]
-        v = qkv_s[:, 2 * D + pair * LANES : 2 * D + (pair + 1) * LANES]
-        k_t = k.T
-        ago = ag[:, cols]
-        dq_t = []
-        dk = None
-        dv = None
-        for h in range(2):
-            p_low = p_s[2 * pair + h]
-            p = p_low.astype(F32)
-            ago_h = ago * halves[h]
-            dp = nt(v, ago_h)
-            rd = jnp.sum(p * dp, axis=0, keepdims=True)
-            ds = (p * (dp - rd)).astype(BF)
-            dv_h = nn(p_low, ago_h)
-            dk_h = nn(ds, q * scaled[h])
-            dv = dv_h if dv is None else dv + dv_h
-            dk = dk_h if dk is None else dk + dk_h
-            dq_t.append((nn(k_t[h * HEAD : (h + 1) * HEAD, :], ds) * scale).astype(BF))
-        qg_s[:, cols] = jnp.concatenate(dq_t, axis=0).T
-        qg_s[:, D + pair * LANES : D + (pair + 1) * LANES] = dk.astype(BF)
-        qg_s[:, 2 * D + pair * LANES : 2 * D + (pair + 1) * LANES] = dv.astype(BF)
+    ag_s[...] = ag
+    dk, dv = {}, {}
+
+    def ago_of(i, head):
+        at = head // 2 * LANES
+        return ag_s[spans[i], at : at + LANES] * halves[head % 2]
+
+    def probs_back(number, i, head):
+        wide_s[number % 3] = nt(lanes_of(2, i, head), ago_of(i, head))
+
+    def scores_back(number, i, head):
+        p = p_s[i * HEADS + head].astype(F32)
+        dp = wide_s[number % 3]
+        rd = jnp.sum(p * dp, axis=0, keepdims=True)
+        ds_s[number % 2] = (p * (dp - rd)).astype(BF)
+
+    def heads_back(number, i, head):
+        ds = ds_s[number % 2]
+        at = head % 2 * HEAD
+        dv[i, head] = nn(p_s[i * HEADS + head], ago_of(i, head))
+        dk[i, head] = nn(ds, lanes_of(0, i, head) * scaled[head % 2])
+        dq_t = nn(lanes_of(1, i, head).T[at : at + HEAD, :], ds) * scale
+        dq_s[head * HEAD : (head + 1) * HEAD, spans[i]] = dq_t.astype(BF)
+        if head % 2:
+            at = head // 2 * LANES
+            qg_s[spans[i], at : at + LANES] = dq_s[at : at + LANES, spans[i]].T
+            for which, terms in ((1, dk), (2, dv)):
+                total = terms.pop((i, head - 1)) + terms.pop((i, head))
+                qg_s[spans[i], which * D + at : which * D + at + LANES] = total.astype(BF)
+
+    staged(probs_back, scores_back, heads_back)
 
     qg = qg_s[...]
     add_grad(QKV_AT, nn(n1_s[...].T, qg))
@@ -262,13 +292,14 @@
             )
 
 
-def layer_pass(tokens, centres, lengths, cotangent, small_rows, wqkv, wout, wup, wdown, wpos, fc=512):
+def layer_pass(tokens, centres, lengths, cotangent, small_rows, wqkv, wout, wup, wdown, wpos, fc=768, group=2):
     clouds = lengths.shape[0]
     rows = clouds * LMAX
+    span = group * LMAX
     whole = lambda shape: pl.BlockSpec(shape, lambda i, *_: (0, 0), pipeline_mode=pl.Buffered(1))
-    tile = lambda: pl.BlockSpec((LMAX, D), lambda i, *_: (i, 0))
+    tile = lambda: pl.BlockSpec((span, D), lambda i, *_: (i, 0))
     return pl.pallas_call(
-        functools.partial(layer_kernel, fc=fc),
+        functools.partial(layer_kernel, fc=fc, group=group),
         out_shape=(
             jax.ShapeDtypeStruct((rows, D), BF),
             jax.ShapeDtypeStruct((rows, D), BF),
@@ -277,10 +308,10 @@
         ),
         grid_spec=pltpu.PrefetchScalarGridSpec(
             num_scalar_prefetch=1,
-            grid=(clouds,),
+            grid=(clouds // group,),
             in_specs=[
                 tile(),
-                pl.BlockSpec((3, LMAX), lambda i, *_: (0, i)),
+                pl.BlockSpec((3, span), lambda i, *_: (0, i)),
                 tile(),
                 whole((SMALL_ROWS, LANES)),
                 whole((D, 3 * D)),
@@ -297,17 +328,21 @@
             ],
             scratch_shapes=[
                 pltpu.VMEM((8, SMALL_ROWS * LANES), F32),
-                pltpu.VMEM((LMAX, PH), F32),
-                pltpu.VMEM((LMAX, D), F32),
-                pltpu.VMEM((LMAX, D), F32),
-                pltpu.VMEM((LMAX, D), BF),
-                pltpu.VMEM((LMAX, 3 * D), BF),
-                pltpu.VMEM((HEADS, LMAX, LMAX), BF),
-                pltpu.VMEM((D, LMAX), BF),
-                pltpu.VMEM((LMAX, D), F32),
-                pltpu.VMEM((LMAX, D), F32),
-                pltpu.VMEM((LMAX, D), F32),
-                pltpu.VMEM((LMAX, 3 * D), BF),
+                pltpu.VMEM((span, PH), F32),
+                pltpu.VMEM((span, D), F32),
+                pltpu.VMEM((span, D), F32),
+                pltpu.VMEM((span, D), BF),
+                pltpu.VMEM((span, 3 * D), BF),
+                pltpu.VMEM((group * HEADS, LMAX, LMAX), BF),
+                pltpu.VMEM((D, span), BF),
+                pltpu.VMEM((span, D), F32),
+                pltpu.VMEM((span, D), F32),
+                pltpu.VMEM((span, D), F32),
+                pltpu.VMEM((span, 3 * D), BF),
+                pltpu.VMEM((3, LMAX, LMAX), F32),
+                pltpu.VMEM((2, LMAX, LMAX), BF),
+                pltpu.VMEM((D, span), BF),
+                pltpu.VMEM((span, D), BF),
             ],
         ),
         compiler_params=pltpu.CompilerParams(vmem_limit_bytes=60 * 1024 * 1024),

time: 338 us -> 286 us (0.85)
  Pallas kernels: 321 us -> 269 us
    pallas_call x1, Pallas kernels: 168 us -> 115 us  [layer_pass(): pl.pallas_call(functools.partial(layer_kernel, fc=fc, group=group), out_s...]
  transfers between devices with their start and end apart: 1 -> 1, of which waited for: 0 -> 0; matrix products, arithmetic and copies ran while one was open for 0% -> 0% of each run, Pallas kernels for 65% -> 59%
where the time goes in v3:
time: 286 us
  Pallas kernels  269 us (94%)
  between operations  14.1 us (5%)
    pallas_call x1, Pallas kernels, layer_pass(): pl.pallas_call(functools.partial(layer_kernel, fc=fc, group=group), out_s...  115 us
    pallas_call x1, Pallas kernels, reduce_all(): pl.pallas_call(functools.partial(reduce_kernel, roles, sizes, extra), out...  54.5 us
    pallas_call x1, Pallas kernels, gather_weights(): pl.pallas_call(functools.partial(head_kernel, roles, sizes, lay), out_sha...  39.7 us
    pallas_call x1, Pallas kernels, gather_steps(): pl.pallas_call(functools.partial(steps_kernel, roles, sizes), out_shape=j...  33.4 us
    pallas_call x1, Pallas kernels, turn_in(): pl.pallas_call(functools.partial(turn_kernel, lay, D), out_shape=tuple(sh...  14.5 us
    pallas_call x1, Pallas kernels, turn_back(): pl.pallas_call(functools.partial(back_kernel, lay, D), out_shape=tuple((j...  11.9 us
  transfers between devices with their start and end apart: 1, of which 0 were waited for; matrix products, arithmetic and copies ran while one was open for 0% of the time, Pallas kernels for 59%

profile of v3, /device:TPU:1, one launch (start us, length us, event | category | flops | bytes accessed | tf_op | source)
XLA Modules:
  0.0 285.6 jit_solution(2181049424936175943)
XLA Ops:
  7.2 0.0 all-gather.2.cloned.1.call-start
  7.2 1.2 pad_bitcast_fusion.refs_5_
  8.5 39.7 %gather_weights.1 = (bf16[384,1152]{1,0:T(8,128)(2,1)}, bf16[384,384]{1,0:T(8,128)(2,1)}, bf16[384,1536]{1,0:T(8,128)(2,1)}, bf16[1536,384]{1,0:T(8,128)(2,1)}, ...) custom-call(f32[12,1152]{1,0:T(8,128)} %refs_10_.5, f32[12,384]{1,0:T(8,128)} %refs_11_.3, ...), custom_call_target="tpu_custom_call" | custom-call | tf_op jit(solution)/shard_map/gather_weights/pallas_call | solution.py:747
  48.2 0.0 all-gather.2.cloned.1.call-update
  48.2 114.8 %layer.1 = (bf16[4096,384]{1,0:T(8,128)(2,1)}, bf16[4096,384]{1,0:T(8,128)(2,1)}, f32[14336,128]{1,0:T(8,128)}, f32[37,128]{1,0:T(8,128)}) custom-call(s32[16]{0:T(128)} %len_ref.1, bf16[4096,384]{1,0:T(8,128)(2,1)} %tok_ref.1, f32[3,4096]{1,0:T(4,128)} %cen_ref.1, bf16[4096,384]{1,0:T(8,128)(2,1)} %cot_ref.1, f32[37,128]{1,0:T(8,128)} %get-tuple-element.67.small_ref, ...), custom_call_target="tpu_custom_call" | custom-call | tf_op jit(solution)/shard_map/layer/pallas_call | solution.py:301
  163.0 54.5 %reduce_all.1 = (bf16[32,448,128]{2,1,0:T(8,128)(2,1)}, f32[37,128]{1,0:T(8,128)}) custom-call(f32[32,448,128]{2,1,0:T(8,128)} %bitcast.7, f32[37,128]{1,0:T(8,128)} %get-tuple-element.76.small), custom_call_target="tpu_custom_call" | custom-call | tf_op jit(solution)/shard_map/reduce_all/pallas_call | solution.py:789
  217.4 1.3 dynamic_slice.3
  218.8 0.0 all-gather.2.cloned.1.call-done
  218.8 14.5 %turn_in.1 = (f32[12,1152]{1,0:T(8,128)}, f32[12,384]{1,0:T(8,128)}, f32[12,1536]{1,0:T(8,128)}, f32[48,384]{1,0:T(8,128)}, f32[4,384]{1,0:T(4,128)}, /*index=5*...) custom-call(s32[1]{0:T(128)} %bitcast.3.index_ref, ...), custom_call_target="tpu_custom_call" | custom-call | tf_op jit(solution)/shard_map/turn_in/pallas_call | solution.py:874
  233.3 33.4 %gather_steps.1.steps = bf16[32,576,128]{2,1,0:T(8,128)(2,1)} custom-call(bf16[576,128]{1,0:T(8,128)(2,1)} %get-tuple-element.95.slot), custom_call_target="tpu_custom_call" | custom-call | tf_op jit(solution)/shard_map/gather_steps/pallas_call | solution.py:895
  266.8 11.9 %turn_back.1 = (f32[12,1152]{1,0:T(8,128)}, f32[12,384]{1,0:T(8,128)}, f32[12,1536]{1,0:T(8,128)}, f32[48,384]{1,0:T(8,128)}, f32[4,384]{1,0:T(4,128)}, /*index=...) custom-call(bf16[32,576,128]{2,1,0:T(8,128)(2,1)} %gather_steps.1.st, ...), custom_call_target="tpu_custom_call" | custom-call | tf_op jit(solution)/shard_map/turn_back/pallas_call | solution.py:937
Async XLA Ops:
  7.2 211.6 %all-gather.2.cloned.1.call-start = ((), (), s32[]{:S(2)}) async-start(), calls=%async_computation | async-start | bytes 6488064 | tf_op jit(solution)/shard_map/all_gather | solution.py:958
Sparse Core Ops, SparseCore 0:
  48.3 67.5 all-gather.1

commit v4 on v3

--- a/solution.py
+++ b/solution.py
@@ -455,14 +455,18 @@
     return (nz - 1) + nz * (plane + core)
 
 
-def gather_all(grid, wire, buf, meanwhile=None):
+def nothing():
+    pass
+
+
+def gather_all(grid, wire, buf, tag, idle=nothing):
     rows = buf.shape[1]
     half = rows // 32 * 16
     parts = {"a": pl.ds(0, half), "b": pl.ds(half, rows - half)}
 
     def pass_on(key, slot, part, **offsets):
         ref = buf.at[slot] if part is None else buf.at[slot, parts[part]]
-        wire.send(("gather",) + key, ref, ref, **offsets)
+        wire.send((tag,) + key, ref, ref, **offsets)
 
     zs, ys, xs, cs = ([*grid.offsets(role)] for role in ("z", "y", "x", "c"))
 
@@ -480,12 +484,12 @@
 
     def relay(b):
         for y in ys:
-            wire.arrived(("gather", "y", b, y))
+            wire.arrived((tag, "y", b, y))
             for x in xs:
                 pass_on(("a", b, y, x), grid.slot(z=b, y=y), "a", x=x)
             to_core((b, y, 0, 0), grid.slot(z=b, y=y))
         for x in xs:
-            wire.arrived(("gather", "x", b, x))
+            wire.arrived((tag, "x", b, x))
             for y in ys:
                 pass_on(("b", b, y, x), grid.slot(z=b, x=x), "b", y=y)
             to_core((b, 0, x, 0), grid.slot(z=b, x=x))
@@ -493,21 +497,22 @@
     for z in zs:
         pass_on(("z", z), grid.slot(), None, z=z)
     have(0)
-    if meanwhile is not None:
-        meanwhile()
+    idle()
     for b in zs:
-        wire.arrived(("gather", "z", b))
+        wire.arrived((tag, "z", b))
         have(b)
+        idle()
         relay(b - 1)
+        idle()
     relay(len(zs))
     for b in [0] + zs:
         for y in ys:
             for x in xs:
                 for part in ("a", "b"):
-                    wire.arrived(("gather", part, b, y, x))
+                    wire.arrived((tag, part, b, y, x))
                     to_core((b, y, x, part), grid.slot(z=b, y=y, x=x), part)
     for key in list(wire.copies):
-        if key[:2] == ("gather", "c"):
+        if key[:2] == (tag, "c"):
             wire.arrived(key)
 
 
@@ -521,12 +526,12 @@
     return sum(roles[role][2] - 1 for role in ("z", "y", "x", "c"))
 
 
-def reduce_scatter(grid, wire, full, small, acc, out_c, in_c, out_p, in_p, out_z, in_z, s_out, s_in, extra):
+def reduce_scatter(grid, wire, full, small, acc, out_c, in_c, out_p, in_p, out_z, in_z, s_out, s_in, extra, ready=lambda b: None, idle=nothing):
     rows = full.shape[1]
     half = rows // 32 * 16
     first, second = pl.ds(0, half), pl.ds(half, rows - half)
     zs, ys, xs, cs = ([*grid.offsets(role)] for role in ("z", "y", "x", "c"))
-    order = zs + [0]
+    order = zs[::-1] + [0]
 
     small_order = ["c", "y", "x", "z"]
     small_state = {"value": small[...], "stage": 0}
@@ -551,6 +556,7 @@
 
     small_send()
     for b in order:
+        ready(b)
         for y in [0] + ys:
             for x in [0] + xs:
                 for c in cs:
@@ -601,6 +607,7 @@
 
     total = None
     for turn in range(len(order) + 2):
+        idle()
         if turn < len(order):
             diagonal(order[turn])
         if 1 <= turn <= len(order):
@@ -608,6 +615,7 @@
             if small_state["stage"] < 3:
                 small_take()
                 small_send()
+        idle()
         if turn >= 2:
             b = order[turn - 2]
             value = plane_sum(b)
@@ -684,6 +692,16 @@
     return jnp.concatenate([value, jnp.zeros((rows - have, value.shape[1]), value.dtype)], axis=0)
 
 
+def once(action):
+    pending = [action]
+
+    def run():
+        if pending:
+            pending.pop()()
+
+    return run
+
+
 def head_kernel(roles, sizes, lay, *refs):
     masters = dict(zip(NAMES, refs[:5]))
     small_ref = refs[5]
@@ -706,7 +724,7 @@
             bases[rows, cols] = pad_rows(lefts[name][...], rows.stop - rows.start).astype(BF)
 
     meet(grid)
-    gather_all(grid, wire, buf, pack_bases)
+    gather_all(grid, wire, buf, "w", once(pack_bases))
     for name in NAMES:
         spread = None if lay.rows[name] == lay.padded[name] else lay.spread(name)
         for block in range(WIDTH[name] // LANES):
@@ -765,36 +783,241 @@
     )(*masters, padded, *lefts)
 
 
-def reduce_kernel(roles, sizes, extra, full, small, out, small_out, acc, out_c, in_c, out_p, in_p, out_z, in_z, s_out, s_in, send_sems, recv_sems):
+def split(value):
+    high = value.astype(BF)
+    return jnp.concatenate([high, (value - high.astype(F32)).astype(BF)], axis=0)
+
+
+def joined(value):
+    half = value.shape[0] // 2
+    return value[:half] + value[half:]
+
+
+class Groups:
+    def __init__(self, lay):
+        self.lay = lay
+        wide = [(name, i) for name in ("qkv", "out", "up") for i in range(WIDTH[name] // LANES)]
+        self.members = [wide[i : i + 4] for i in range(0, len(wide), 4)]
+        self.members += [[("down", i)] for i in range(WIDTH["down"] // LANES)]
+        self.members += [[("pos", i) for i in range(WIDTH["pos"] // LANES)]]
+        self.rows = [pad16(sum(lay.rows[name] for name, _ in group)) for group in self.members]
+        self.starts = [sum(self.rows[:i]) for i in range(len(self.rows))]
+        self.total = sum(self.rows)
+        self.kinds = []
+        self.kind_of = []
+        for group, rows in zip(self.members, self.rows):
+            kind = (tuple(name for name, _ in group), rows)
+            if kind not in self.kinds:
+                self.kinds.append(kind)
+            self.kind_of.append(self.kinds.index(kind))
+
+    def span(self, number):
+        return slice(self.starts[number], self.starts[number] + self.rows[number])
+
+    def spread(self, name, rows, place):
+        own_rows = self.lay.rows[name]
+        shape = (HEIGHT[name], self.lay.count * rows)
+        row = lax.broadcasted_iota(jnp.int32, shape, 0)
+        col = lax.broadcasted_iota(jnp.int32, shape, 1)
+        owner = col // rows
+        own = col - owner * rows - place * own_rows
+        hit = (own >= 0) & (own < own_rows) & (owner * own_rows + own == row)
+        return hit.astype(F32).astype(BF)
+
+    def thin(self, number):
+        names, rows = self.kinds[number]
+        return sum(2 * self.lay.padded[name] for name in names), self.lay.count * rows
+
+
+RIGHT_CHUNK = 384
+STARTS = {"qkv": QKV_AT, "up": UP_AT, "out": OUT_AT, "down": DOWN_AT, "pos": POS_AT}
+
+
+def tail_kernel(roles, sizes, lay, groups, extra, full_hbm, small, bases_hbm, *refs):
+    rights_hbm, lefts, masters, firsts, seconds = (
+        dict(zip(NAMES, refs[5 * i : 5 * i + 5])) for i in range(5)
+    )
+    small_out = refs[25]
+    grads, firsts_next, seconds_next, nexts, lows = (
+        dict(zip(NAMES, refs[26 + 5 * i : 31 + 5 * i])) for i in range(5)
+    )
+    rest = refs[51:]
+    full, acc, out_c, in_c, out_p, in_p, out_z, in_z, s_out, s_in = rest[:10]
+    flat, steps, bases, coarse = rest[10:14]
+    rights = dict(zip(NAMES, rest[14:19]))
+    picks = dict(zip(NAMES, rest[19:24]))
+    thins = rest[24 : 24 + len(groups.kinds)]
+    send_sems, recv_sems, full_sems, base_sem, right_sems = rest[24 + len(groups.kinds) :]
     grid = Grid(roles, sizes)
     wire = Wire(grid, send_sems, recv_sems)
+    me = grid.slot()
+
+    plane = lay.count // grid.size("z")
+
+    def full_copy(b):
+        at = pl.multiple_of(flipped(grid.coord["z"], b, grid.size("z")) * plane, plane)
+        part = pl.ds(at, plane)
+        return pltpu.make_async_copy(full_hbm.at[part], full.at[part], full_sems.at[b])
+
+    for b in [*grid.offsets("z")][::-1] + [0]:
+        full_copy(b).start()
+    base_copy = pltpu.make_async_copy(bases_hbm, bases, base_sem)
+    base_copy.start()
+
+    chunks = [(name, at) for name in NAMES for at in range(0, WIDTH[name], RIGHT_CHUNK)]
+
+    def right_copy(number):
+        name, at = chunks[number]
+        return pltpu.make_async_copy(
+            rights_hbm[name].at[pl.ds(at, RIGHT_CHUNK), :],
+            coarse.at[number % 2, :, pl.ds(0, WIDTH[name])],
+            right_sems.at[number],
+        )
+
+    right_copy(0).start()
+    right_copy(1).start()
+
+    def round_right(number):
+        name, at = chunks[number]
+        right_copy(number).wait()
+        rights[name][at : at + RIGHT_CHUNK, :] = coarse[number % 2, :, : WIDTH[name]].astype(BF)
+        if number + 2 < len(chunks):
+            right_copy(number + 2).start()
+
+    def make_pick(name):
+        height, rows, padded = HEIGHT[name], lay.rows[name], lay.padded[name]
+        row = lax.broadcasted_iota(jnp.int32, (padded, height), 0)
+        col = lax.broadcasted_iota(jnp.int32, (padded, height), 1)
+        pick = ((row < rows) & (col == me * rows + row)).astype(F32).astype(BF)
+        base_rows, base_cols = lay.base_place(name)
+        base = bases[:, base_rows, base_cols]
+        left_rows = nt(pick, base.reshape(base.shape[0] * base.shape[1], height)).astype(BF)
+        if rows != padded:
+            left_rows = nt(left_rows, lay.spread(name)).astype(BF)
+        picks[name][:padded, :] = left_rows
+        picks[name][padded:, :] = pick
+
+    def make_thin(number):
+        names, rows = groups.kinds[number]
+        at = 0
+        for place, name in enumerate(names):
+            padded = lay.padded[name]
+            left = split(pad_rows(lefts[name][...], padded))
+            if len(names) > 1 or rows != lay.rows[name]:
+                left = nn(left, groups.spread(name, rows, place)).astype(BF)
+            thins[number][at : at + 2 * padded, :] = left
+            at += 2 * padded
+
+    duties = [functools.partial(round_right, i) for i in range(len(chunks))]
+    duties += [base_copy.wait]
+    duties += [functools.partial(make_pick, name) for name in NAMES]
+    duties += [functools.partial(make_thin, i) for i in range(len(groups.kinds))]
+
+    def idle():
+        if duties:
+            duties.pop(0)()
+
     meet(grid)
     total, smalls = reduce_scatter(
-        grid, wire, full, small, acc, out_c, in_c, out_p, in_p, out_z, in_z, s_out, s_in, extra
+        grid, wire, full, small, acc, out_c, in_c, out_p, in_p, out_z, in_z, s_out, s_in, extra,
+        lambda b: full_copy(b).wait(), idle,
     )
     small_out[...] = smalls
-    out[grid.slot()] = total.astype(BF)
-    gather_all(grid, wire, out)
+    flat[me] = total.astype(BF)
+    gather_all(grid, wire, flat, "flat", idle)
+    while duties:
+        idle()
+
+    def flat_block(block):
+        height = flat.shape[1]
+        pieces, at = [], block * D
+        while at < (block + 1) * D:
+            slot, row = at // height, at % height
+            take = min((block + 1) * D - at, height - row)
+            pieces.append(flat[slot, row : row + take, :])
+            at += take
+        return pieces[0] if len(pieces) == 1 else jnp.concatenate(pieces, axis=0)
+
+    directions = {}
+    for name in NAMES:
+        height, width = HEIGHT[name], WIDTH[name]
+        rows, padded = lay.rows[name], lay.padded[name]
+        lhs = picks[name][...]
+        if name in ("down", "pos"):
+            both = None
+            for block in range(height // LANES):
+                part = nt(
+                    lhs[:, block * LANES : (block + 1) * LANES], flat_block(STARTS[name] + block)
+                )
+                both = part if both is None else both + part
+        else:
+            both = jnp.concatenate(
+                [nn(lhs, flat_block(STARTS[name] + i)) for i in range(width // LANES)], axis=1
+            )
+        grads[name][...] = both[padded : padded + rows]
+        terms = split(both[:padded])
+        for at in range(0, width, D):
+            cols = slice(at, at + D)
+            rotated = joined(nn(terms, rights[name][:, cols]))[:rows]
+            first = DECAY * firsts[name][:, cols] + (1.0 - DECAY) * rotated
+            second = DECAY * seconds[name][:, cols] + (1.0 - DECAY) * rotated * rotated
+            firsts_next[name][:, cols] = first
+            seconds_next[name][:, cols] = second
+            direction = first / (jnp.sqrt(second) + ADAM_EPSILON)
+            for i in range(D // LANES):
+                directions[name, at // LANES + i] = direction[:, i * LANES : (i + 1) * LANES]
+    for number, group in enumerate(groups.members):
+        piece = jnp.concatenate([directions[member] for member in group], axis=0)
+        steps[me, groups.span(number), :] = pad_rows(piece, groups.rows[number]).astype(BF)
+
+    gather_all(grid, wire, steps, "steps")
+
+    partway = {}
+    for number, group in enumerate(groups.members):
+        rows = groups.rows[number]
+        piece = steps[:, groups.span(number), :].reshape(lay.count * rows, LANES)
+        whole = nn(thins[groups.kind_of[number]][...], piece)
+        at = 0
+        for name, block in group:
+            padded = lay.padded[name]
+            partway[name, block] = joined(whole[at : at + 2 * padded])
+            at += 2 * padded
+    for name in NAMES:
+        height, width = HEIGHT[name], WIDTH[name]
+        terms = split(
+            jnp.concatenate([partway[name, i] for i in range(width // LANES)], axis=1)
+        )
+        rate = height ** (-0.5)
+        for at in range(0, width, D):
+            cols = slice(at, at + D)
+            update = joined(nt(terms, rights[name][cols, :]))[: lay.rows[name]]
+            master = masters[name][:, cols] * (1.0 - rate * WEIGHT_DECAY) - rate * update
+            nexts[name][:, cols] = master
+            lows[name][:, cols] = master.astype(BF)
     wire.finish()
 
 
-def reduce_all(roles, sizes, full, small):
+def finish_step(roles, sizes, lay, full, small, bases, rights, lefts, masters, firsts, seconds):
     slots, rows, _ = full.shape
     nz, ny, nx, nc = (roles[role][2] for role in ("z", "y", "x", "c"))
-    count = reduce_copies(roles) + small_copies(roles) + gather_copies(roles)
+    count = reduce_copies(roles) + small_copies(roles) + 2 * gather_copies(roles)
     extra = {}
     for role in ("c", "y", "x", "z"):
         for offset in range(1, roles[role][2]):
             extra[(role, offset)] = len(extra)
+    groups = Groups(lay)
+    chunks = sum(WIDTH[name] // RIGHT_CHUNK for name in NAMES)
+    shapes = [(lay.rows[n], WIDTH[n]) for n in NAMES]
+    anywhere = pl.BlockSpec(memory_space=pl.ANY)
     return pl.pallas_call(
-        functools.partial(reduce_kernel, roles, sizes, extra),
-        out_shape=(
-            jax.ShapeDtypeStruct((slots, rows, LANES), BF),
-            jax.ShapeDtypeStruct((SMALL_ROWS, LANES), F32),
-        ),
-        in_specs=[vmem()] * 2,
-        out_specs=(vmem(), vmem()),
+        functools.partial(tail_kernel, roles, sizes, lay, groups, extra),
+        out_shape=(jax.ShapeDtypeStruct((SMALL_ROWS, LANES), F32),)
+        + tuple(jax.ShapeDtypeStruct(s, F32) for s in shapes * 4)
+        + tuple(jax.ShapeDtypeStruct(s, BF) for s in shapes),
+        in_specs=[anywhere, vmem(), anywhere] + [anywhere] * 5 + [vmem()] * 20,
+        out_specs=tuple([vmem()] * 26),
         scratch_shapes=[
+            pltpu.VMEM((slots, rows, LANES), F32),
             pltpu.VMEM((rows, LANES), F32),
             pltpu.VMEM((nc - 1, nz, ny, nx, rows, LANES), BF),
             pltpu.VMEM((nc - 1, nz, ny, nx, rows, LANES), BF),
@@ -804,145 +1027,26 @@
             pltpu.VMEM((nz - 1, rows, LANES), BF),
             pltpu.VMEM((4, SMALL_ROWS, LANES), F32),
             pltpu.VMEM((len(extra), SMALL_ROWS, LANES), F32),
+            pltpu.VMEM((slots, rows, LANES), BF),
+            pltpu.VMEM((slots, groups.total, LANES), BF),
+            pltpu.VMEM(bases.shape, BF),
+            pltpu.VMEM((2, RIGHT_CHUNK, FF), F32),
+        ]
+        + [pltpu.VMEM((WIDTH[name], WIDTH[name]), BF) for name in NAMES]
+        + [pltpu.VMEM((2 * lay.padded[name], HEIGHT[name]), BF) for name in NAMES]
+        + [pltpu.VMEM(groups.thin(i), BF) for i in range(len(groups.kinds))]
+        + [
             pltpu.SemaphoreType.DMA((count,)),
             pltpu.SemaphoreType.DMA((count,)),
+            pltpu.SemaphoreType.DMA((nz,)),
+            pltpu.SemaphoreType.DMA,
+            pltpu.SemaphoreType.DMA((chunks,)),
         ],
         compiler_params=pltpu.CompilerParams(
             collective_id=1, has_side_effects=True, vmem_limit_bytes=VMEM_LIMIT
         ),
-        name="reduce_all",
-    )(full, small)
-
-
-def split(value):
-    high = value.astype(BF)
-    return jnp.concatenate([high, (value - high.astype(F32)).astype(BF)], axis=0)
-
-
-def joined(value):
-    half = value.shape[0] // 2
-    return value[:half] + value[half:]
-
-
-def turn_kernel(lay, chunk, index_ref, flat, bases, *refs):
-    rights, firsts, seconds, grads, firsts_next, seconds_next = (
-        dict(zip(NAMES, refs[5 * i : 5 * i + 5])) for i in range(6)
-    )
-    slot = refs[30]
-    me = index_ref[0]
-    starts = {"qkv": QKV_AT, "up": UP_AT, "out": OUT_AT, "down": DOWN_AT, "pos": POS_AT}
-    for name in NAMES:
-        height, width = HEIGHT[name], WIDTH[name]
-        rows, padded = lay.rows[name], lay.padded[name]
-        row = lax.broadcasted_iota(jnp.int32, (padded, height), 0)
-        col = lax.broadcasted_iota(jnp.int32, (padded, height), 1)
-        pick = ((row < rows) & (col == me * rows + row)).astype(F32).astype(BF)
-        base_rows, base_cols = lay.base_place(name)
-        base = bases[:, base_rows, base_cols]
-        left_rows = nt(pick, base.reshape(base.shape[0] * base.shape[1], height)).astype(BF)
-        if rows != padded:
-            left_rows = nt(left_rows, lay.spread(name)).astype(BF)
-        lhs = jnp.concatenate([left_rows, pick], axis=0)
-        blocks = []
-        if name in ("down", "pos"):
-            both = None
-            for block in range(height // LANES):
-                at = (starts[name] + block) * D
-                part = nt(lhs[:, block * LANES : (block + 1) * LANES], flat[at : at + D, :])
-                both = part if both is None else both + part
-        else:
-            for block in range(width // LANES):
-                at = (starts[name] + block) * D
-                blocks.append(nn(lhs, flat[at : at + D, :]))
-            both = jnp.concatenate(blocks, axis=1)
-        grads[name][...] = both[padded : padded + rows]
-        terms = split(both[:padded])
-        for at in range(0, width, chunk):
-            cols = slice(at, at + chunk)
-            rotated = joined(nn(terms, rights[name][:, cols].astype(BF)))[:rows]
-            first = DECAY * firsts[name][:, cols] + (1.0 - DECAY) * rotated
-            second = DECAY * seconds[name][:, cols] + (1.0 - DECAY) * rotated * rotated
-            firsts_next[name][:, cols] = first
-            seconds_next[name][:, cols] = second
-            direction = pad_rows(first / (jnp.sqrt(second) + ADAM_EPSILON), padded).astype(BF)
-            for i in range(chunk // LANES):
-                slot[lay.span(name, at // LANES + i), :] = direction[:, i * LANES : (i + 1) * LANES]
-
-
-def turn_in(lay, index, flat, bases, rights, firsts, seconds):
-    shapes = [jax.ShapeDtypeStruct((lay.rows[n], WIDTH[n]), F32) for n in NAMES]
-    return pl.pallas_call(
-        functools.partial(turn_kernel, lay, D),
-        out_shape=tuple(shapes * 3) + (jax.ShapeDtypeStruct((lay.total, LANES), BF),),
-        in_specs=[pl.BlockSpec(memory_space=pltpu.SMEM)] + [vmem()] * 17,
-        out_specs=tuple([vmem()] * 16),
-        compiler_params=pltpu.CompilerParams(vmem_limit_bytes=VMEM_LIMIT),
-        name="turn_in",
-    )(index, flat, bases, *rights, *firsts, *seconds)
-
-
-def steps_kernel(roles, sizes, slot, buf, send_sems, recv_sems):
-    grid = Grid(roles, sizes)
-    wire = Wire(grid, send_sems, recv_sems)
-    buf[grid.slot()] = slot[...]
-    meet(grid)
-    gather_all(grid, wire, buf)
-    wire.finish()
-
-
-def gather_steps(roles, sizes, lay, slot):
-    count = gather_copies(roles)
-    return pl.pallas_call(
-        functools.partial(steps_kernel, roles, sizes),
-        out_shape=jax.ShapeDtypeStruct((lay.count, lay.total, LANES), BF),
-        in_specs=[vmem()],
-        out_specs=vmem(),
-        scratch_shapes=[
-            pltpu.SemaphoreType.DMA((count,)),
-            pltpu.SemaphoreType.DMA((count,)),
-        ],
-        compiler_params=pltpu.CompilerParams(
-            collective_id=2, has_side_effects=True, vmem_limit_bytes=VMEM_LIMIT
-        ),
-        name="gather_steps",
-    )(slot)
-
-
-def back_kernel(lay, chunk, steps, *refs):
-    lefts, rights, masters, nexts, lows = (
-        dict(zip(NAMES, refs[5 * i : 5 * i + 5])) for i in range(5)
-    )
-    for name in NAMES:
-        height, width = HEIGHT[name], WIDTH[name]
-        rows, padded = lay.rows[name], lay.padded[name]
-        left = split(pad_rows(lefts[name][...], padded))
-        if rows != padded:
-            left = nn(left, lay.spread(name)).astype(BF)
-        parts = []
-        for block in range(width // LANES):
-            piece = steps[:, lay.span(name, block), :].reshape(lay.count * padded, LANES)
-            parts.append(joined(nn(left, piece)))
-        partway = split(jnp.concatenate(parts, axis=1))
-        rate = height ** (-0.5)
-        for at in range(0, width, chunk):
-            cols = slice(at, at + chunk)
-            update = joined(nt(partway, rights[name][cols, :].astype(BF)))[:rows]
-            master = masters[name][:, cols] * (1.0 - rate * WEIGHT_DECAY) - rate * update
-            nexts[name][:, cols] = master
-            lows[name][:, cols] = master.astype(BF)
-
-
-def turn_back(lay, steps, lefts, rights, masters):
-    shapes = [(lay.rows[n], WIDTH[n]) for n in NAMES]
-    return pl.pallas_call(
-        functools.partial(back_kernel, lay, D),
-        out_shape=tuple(jax.ShapeDtypeStruct(s, F32) for s in shapes)
-        + tuple(jax.ShapeDtypeStruct(s, BF) for s in shapes),
-        in_specs=[vmem()] * 16,
-        out_specs=tuple([vmem()] * 10),
-        compiler_params=pltpu.CompilerParams(vmem_limit_bytes=VMEM_LIMIT),
-        name="turn_back",
-    )(steps, *lefts, *rights, *masters)
+        name="finish_step",
+    )(full, small, bases, *rights, *lefts, *masters, *firsts, *seconds)
 
 
 AXES = ("dp", "fsdp")
@@ -959,25 +1063,24 @@
     layer_out, grad_tokens, full, small_grads = layer_pass(
         tokens, centres, lengths, cotangent, small_rows, w_qkv, w_out, w_up, w_down, w_pos
     )
-    flat, small_total = reduce_all(
-        roles, sizes, full.reshape(count, FLAT_ROWS // count, LANES), small_grads
+    small_total, *finished = finish_step(
+        roles,
+        sizes,
+        lay,
+        full.reshape(count, FLAT_ROWS // count, LANES),
+        small_grads,
+        whole_bases.reshape(count, heads.base_rows, FF),
+        rights,
+        lefts,
+        masters,
+        firsts,
+        seconds,
     )
     me = lax.axis_index("dp") * sizes["fsdp"] + lax.axis_index("fsdp")
     grad_smalls = lax.dynamic_slice(
         small_total.reshape(SMALLS), (me * heads.small_len,), (heads.small_len,)
     )
-    *turned, slot = turn_in(
-        lay,
-        me.reshape(1),
-        flat.reshape(FLAT_ROWS, LANES),
-        whole_bases.reshape(count, heads.base_rows, FF),
-        rights,
-        firsts,
-        seconds,
-    )
-    steps = gather_steps(roles, sizes, lay, slot)
-    updated = turn_back(lay, steps, lefts, rights, masters)
-    return (layer_out, grad_tokens, grad_smalls, *turned, *updated)
+    return (layer_out, grad_tokens, grad_smalls, *finished)
 
 
 def solution(mesh):

time: 286 us -> 288 us (level)
  local copies, waits for them, and re-layouts: 2.59 us -> 38.2 us
  Pallas kernels: 269 us -> 234 us
    unnamed x0 -> x25, local copies, waits for them, and re-layouts: none -> 35.6 us
    pallas_call x4 -> x1, Pallas kernels: 114 us -> 79.7 us  [finish_step(): pl.pallas_call(functools.partial(tail_kernel, roles, sizes, lay, groups,...]
  transfers between devices with their start and end apart: 1 -> 1, of which waited for: 0 -> 0; matrix products, arithmetic and copies ran while one was open for 0% -> 0% of each run, Pallas kernels for 59% -> 40%
where the time goes in v4:
time: 288 us; the launch traced here: 287 us
  Pallas kernels  234 us (81%)
  local copies, waits for them, and re-layouts  38.2 us (13%)
  between operations  14.1 us (5%)
    pallas_call x1, Pallas kernels, layer_pass(): pl.pallas_call(functools.partial(layer_kernel, fc=fc, group=group), out_s...  115 us
    pallas_call x1, Pallas kernels, finish_step(): pl.pallas_call(functools.partial(tail_kernel, roles, sizes, lay, groups,...  79.7 us
    pallas_call x1, Pallas kernels, gather_weights(): pl.pallas_call(functools.partial(head_kernel, roles, sizes, lay), out_sha...  39.7 us
    unnamed x25, local copies, waits for them, and re-layouts  35.6 us
  transfers between devices with their start and end apart: 1, of which 0 were waited for; matrix products, arithmetic and copies ran while one was open for 0% of the time, Pallas kernels for 40%

profile of v4, /device:TPU:1, one launch (start us, length us, event | category | flops | bytes accessed | tf_op | source)
XLA Modules:
  0.0 286.5 jit_solution(5424743283722240733)
XLA Ops:
  7.2 0.0 all-gather.2.cloned.1.call-start
  7.2 1.2 pad_bitcast_fusion.refs_5_
  8.5 39.7 %gather_weights.1 = (bf16[384,1152]{1,0:T(8,128)(2,1)}, bf16[384,384]{1,0:T(8,128)(2,1)}, bf16[384,1536]{1,0:T(8,128)(2,1)}, bf16[1536,384]{1,0:T(8,128)(2,1)}, ...) custom-call(f32[12,1152]{1,0:T(8,128)} %refs_10_.3, f32[12,384]{1,0:T(8,128)} %refs_11_.1, ...), custom_call_target="tpu_custom_call" | custom-call | tf_op jit(solution)/shard_map/gather_weights/pallas_call | solution.py:765
  48.2 114.8 %layer.1 = (bf16[4096,384]{1,0:T(8,128)(2,1)}, bf16[4096,384]{1,0:T(8,128)(2,1)}, f32[14336,128]{1,0:T(8,128)}, f32[37,128]{1,0:T(8,128)}) custom-call(s32[16]{0:T(128)} %len_ref.1, bf16[4096,384]{1,0:T(8,128)(2,1)} %tok_ref.1, f32[3,4096]{1,0:T(4,128)} %cen_ref.1, bf16[4096,384]{1,0:T(8,128)(2,1)} %cot_ref.1, f32[37,128]{1,0:T(8,128)} %get-tuple-element.65.small_ref, ...), custom_call_target="tpu_custom_call" | custom-call | tf_op jit(solution)/shard_map/layer/pallas_call | solution.py:301
  163.0 0.0 all-gather.2.cloned.1.call-done
  163.0 79.7 %finish_step.1 = (f32[37,128]{1,0:T(8,128)}, f32[12,1152]{1,0:T(8,128)}, f32[12,384]{1,0:T(8,128)}, f32[12,1536]{1,0:T(8,128)}, f32[48,384]{1,0:T(8,128)}, /*ind...) custom-call(f32[32,448,128]{2,1,0:T(8,128)} %bitcast.5, ...), custom_call_target="tpu_custom_call" | custom-call | tf_op jit(solution)/shard_map/finish_step/pallas_call | solution.py:1012
  242.7 1.3 dynamic_slice.3
  244.1 1.5 copy.83
  245.6 1.3 copy.84
  246.9 1.5 copy.85
  248.5 1.5 copy.86
  250.0 1.3 copy.87
  251.3 1.5 copy.88
  252.8 1.3 copy.89
  254.1 1.5 copy.90
  255.7 1.5 copy.91
  257.2 1.3 copy.92
  258.5 1.5 copy.93
  260.0 1.3 copy.94
  261.4 1.5 copy.95
  262.9 1.5 copy.96
  264.4 1.3 copy.97
  265.7 1.5 copy.98
  267.2 1.3 copy.99
  268.6 1.5 copy.100
  270.1 1.5 copy.101
  271.6 1.3 copy.102
  272.9 1.4 copy.103
  274.3 1.3 copy.104
  275.6 1.4 copy.105
  277.0 1.4 copy.106
  278.4 1.3 copy.107
  (1 shorter events, 0.0 us)
Async XLA Ops:
  7.2 155.8 %all-gather.2.cloned.1.call-start = ((), (), s32[]{:S(2)}) async-start(), calls=%async_computation | async-start | bytes 6488064 | tf_op jit(solution)/shard_map/all_gather | solution.py:1062
Sparse Core Ops, SparseCore 0:
  48.3 67.5 all-gather.1

commit v5 on v4

--- a/solution.py
+++ b/solution.py
@@ -715,7 +715,14 @@
         for block in range(WIDTH[name] // LANES):
             piece = masters[name][:, block * LANES : (block + 1) * LANES]
             buf[own, lay.span(name, block), :] = pad_rows(piece, lay.padded[name]).astype(BF)
-    buf[own, lay.small_at : lay.small_at + 16, :] = pad_rows(small_ref[...], 16).astype(BF)
+    lines = []
+    for at in range(0, lay.small_len, LANES):
+        line = small_ref[:, at : min(at + LANES, lay.small_len)]
+        if line.shape[1] < LANES:
+            line = jnp.concatenate([line, jnp.zeros((1, LANES - line.shape[1]), F32)], axis=1)
+        lines.append(line)
+    lines = jnp.concatenate(lines, axis=0)
+    buf[own, lay.small_at : lay.small_at + 16, :] = pad_rows(lines, 16).astype(BF)
 
     def pack_bases():
         bases[lay.padded["down"] :, :] = jnp.zeros((16, FF), BF)
@@ -760,8 +767,6 @@
 
 def gather_weights(roles, sizes, lay, masters, smalls, lefts):
     count = gather_copies(roles)
-    lines = -(-lay.small_len // LANES)
-    padded = jnp.pad(smalls, (0, lines * LANES - lay.small_len)).reshape(lines, LANES)
     return pl.pallas_call(
         functools.partial(head_kernel, roles, sizes, lay),
         out_shape=tuple(jax.ShapeDtypeStruct((HEIGHT[n], WIDTH[n]), BF) for n in NAMES)
@@ -780,7 +785,7 @@
             collective_id=0, has_side_effects=True, vmem_limit_bytes=VMEM_LIMIT
         ),
         name="gather_weights",
-    )(*masters, padded, *lefts)
+    )(*masters, smalls.reshape(1, lay.small_len), *lefts)
 
 
 def split(value):
@@ -833,15 +838,63 @@
 STARTS = {"qkv": QKV_AT, "up": UP_AT, "out": OUT_AT, "down": DOWN_AT, "pos": POS_AT}
 
 
+WIDE_AT = {"qkv": 0, "out": 3 * D, "up": 4 * D}
+
+
+def packed_place(packed, name):
+    if name in WIDE_AT:
+        return packed[0], WIDE_AT[name]
+    return packed[1 if name == "down" else 2], 0
+
+
+def hand_out_kernel(lay, index_ref, small, *refs):
+    packed, small_out = refs[:3], refs[3]
+    outs = [dict(zip(NAMES, refs[4 + 5 * i : 9 + 5 * i])) for i in range(5)]
+    at = index_ref[0] * lay.small_len
+    row, shift = at // LANES, at % LANES
+    lane = lax.broadcasted_iota(jnp.int32, (1, LANES), 1)
+    for start in range(0, lay.small_len, LANES):
+        near, far = (
+            pltpu.roll(small[pl.ds(row + start // LANES + i, 1), :], LANES - shift, 1)
+            for i in range(2)
+        )
+        take = min(LANES, lay.small_len - start)
+        line = jnp.where(lane < LANES - shift, near, far)
+        small_out[:, start : start + take] = line[:, :take]
+    for name in NAMES:
+        source, at = packed_place(packed, name)
+        for kind in range(4):
+            value = source[kind, : lay.rows[name], at : at + WIDTH[name]]
+            outs[kind][name][...] = value
+            if kind == 3:
+                outs[4][name][...] = value.astype(BF)
+
+
+def hand_out(lay, index, small, packed):
+    shapes = [(lay.rows[n], WIDTH[n]) for n in NAMES]
+    return pl.pallas_call(
+        functools.partial(hand_out_kernel, lay),
+        out_shape=(jax.ShapeDtypeStruct((1, lay.small_len), F32),)
+        + tuple(jax.ShapeDtypeStruct(s, F32) for s in shapes * 4)
+        + tuple(jax.ShapeDtypeStruct(s, BF) for s in shapes),
+        in_specs=[pl.BlockSpec(memory_space=pltpu.SMEM)] + [vmem()] * 4,
+        out_specs=tuple([vmem()] * 26),
+        name="hand_out",
+    )(index, small, *packed)
+
+
 def tail_kernel(roles, sizes, lay, groups, extra, full_hbm, small, bases_hbm, *refs):
     rights_hbm, lefts, masters, firsts, seconds = (
         dict(zip(NAMES, refs[5 * i : 5 * i + 5])) for i in range(5)
     )
     small_out = refs[25]
-    grads, firsts_next, seconds_next, nexts, lows = (
-        dict(zip(NAMES, refs[26 + 5 * i : 31 + 5 * i])) for i in range(5)
-    )
-    rest = refs[51:]
+    packed = refs[26:29]
+    rest = refs[29:]
+
+    def keep(kind, name, cols, value):
+        target, at = packed_place(packed, name)
+        target[kind, : value.shape[0], at + cols.start : at + cols.stop] = value
+
     full, acc, out_c, in_c, out_p, in_p, out_z, in_z, s_out, s_in = rest[:10]
     flat, steps, bases, coarse = rest[10:14]
     rights = dict(zip(NAMES, rest[14:19]))
@@ -922,7 +975,8 @@
         grid, wire, full, small, acc, out_c, in_c, out_p, in_p, out_z, in_z, s_out, s_in, extra,
         lambda b: full_copy(b).wait(), idle,
     )
-    small_out[...] = smalls
+    small_out[:SMALL_ROWS, :] = smalls
+    small_out[SMALL_ROWS:, :] = jnp.zeros((40 - SMALL_ROWS, LANES), F32)
     flat[me] = total.astype(BF)
     gather_all(grid, wire, flat, "flat", idle)
     while duties:
@@ -954,15 +1008,15 @@
             both = jnp.concatenate(
                 [nn(lhs, flat_block(STARTS[name] + i)) for i in range(width // LANES)], axis=1
             )
-        grads[name][...] = both[padded : padded + rows]
+        keep(0, name, slice(0, width), both[padded : padded + rows])
         terms = split(both[:padded])
         for at in range(0, width, D):
             cols = slice(at, at + D)
             rotated = joined(nn(terms, rights[name][:, cols]))[:rows]
             first = DECAY * firsts[name][:, cols] + (1.0 - DECAY) * rotated
             second = DECAY * seconds[name][:, cols] + (1.0 - DECAY) * rotated * rotated
-            firsts_next[name][:, cols] = first
-            seconds_next[name][:, cols] = second
+            keep(1, name, cols, first)
+            keep(2, name, cols, second)
             direction = first / (jnp.sqrt(second) + ADAM_EPSILON)
             for i in range(D // LANES):
                 directions[name, at // LANES + i] = direction[:, i * LANES : (i + 1) * LANES]
@@ -992,8 +1046,7 @@
             cols = slice(at, at + D)
             update = joined(nt(terms, rights[name][cols, :]))[: lay.rows[name]]
             master = masters[name][:, cols] * (1.0 - rate * WEIGHT_DECAY) - rate * update
-            nexts[name][:, cols] = master
-            lows[name][:, cols] = master.astype(BF)
+            keep(3, name, cols, master)
     wire.finish()
 
 
@@ -1007,15 +1060,17 @@
             extra[(role, offset)] = len(extra)
     groups = Groups(lay)
     chunks = sum(WIDTH[name] // RIGHT_CHUNK for name in NAMES)
-    shapes = [(lay.rows[n], WIDTH[n]) for n in NAMES]
     anywhere = pl.BlockSpec(memory_space=pl.ANY)
     return pl.pallas_call(
         functools.partial(tail_kernel, roles, sizes, lay, groups, extra),
-        out_shape=(jax.ShapeDtypeStruct((SMALL_ROWS, LANES), F32),)
-        + tuple(jax.ShapeDtypeStruct(s, F32) for s in shapes * 4)
-        + tuple(jax.ShapeDtypeStruct(s, BF) for s in shapes),
+        out_shape=(
+            jax.ShapeDtypeStruct((40, LANES), F32),
+            jax.ShapeDtypeStruct((4, lay.padded["qkv"], 5 * D + 3 * D), F32),
+            jax.ShapeDtypeStruct((4, lay.padded["down"], D), F32),
+            jax.ShapeDtypeStruct((4, lay.padded["pos"], D), F32),
+        ),
         in_specs=[anywhere, vmem(), anywhere] + [anywhere] * 5 + [vmem()] * 20,
-        out_specs=tuple([vmem()] * 26),
+        out_specs=tuple([vmem()] * 4),
         scratch_shapes=[
             pltpu.VMEM((slots, rows, LANES), F32),
             pltpu.VMEM((rows, LANES), F32),
@@ -1063,7 +1118,7 @@
     layer_out, grad_tokens, full, small_grads = layer_pass(
         tokens, centres, lengths, cotangent, small_rows, w_qkv, w_out, w_up, w_down, w_pos
     )
-    small_total, *finished = finish_step(
+    small_total, *packed = finish_step(
         roles,
         sizes,
         lay,
@@ -1077,10 +1132,8 @@
         seconds,
     )
     me = lax.axis_index("dp") * sizes["fsdp"] + lax.axis_index("fsdp")
-    grad_smalls = lax.dynamic_slice(
-        small_total.reshape(SMALLS), (me * heads.small_len,), (heads.small_len,)
-    )
-    return (layer_out, grad_tokens, grad_smalls, *finished)
+    grad_smalls, *finished = hand_out(heads, me.reshape(1), small_total, packed)
+    return (layer_out, grad_tokens, grad_smalls.reshape(heads.small_len), *finished)
 
 
 def solution(mesh):

time: 288 us -> 251 us (0.87)
  local copies, waits for them, and re-layouts: 38.2 us -> 0 us
    unnamed x25 -> x0, local copies, waits for them, and re-layouts: 35.6 us -> none
  transfers between devices with their start and end apart: 1 -> 1, of which waited for: 0 -> 0; matrix products, arithmetic and copies ran while one was open for 0% -> 0% of each run, Pallas kernels for 40% -> 46%
where the time goes in v5:
time: 251 us
  Pallas kernels  236 us (94%)
  between operations  14.1 us (6%)
    pallas_call x1, Pallas kernels, layer_pass(): pl.pallas_call(functools.partial(layer_kernel, fc=fc, group=group), out_s...  115 us
    pallas_call x1, Pallas kernels, finish_step(): pl.pallas_call(functools.partial(tail_kernel, roles, sizes, lay, groups,...  79.6 us
    pallas_call x1, Pallas kernels, gather_weights(): pl.pallas_call(functools.partial(head_kernel, roles, sizes, lay), out_sha...  39.7 us
  transfers between devices with their start and end apart: 1, of which 0 were waited for; matrix products, arithmetic and copies ran while one was open for 0% of the time, Pallas kernels for 46%

profile of v5, /device:TPU:1, one launch (start us, length us, event | category | flops | bytes accessed | tf_op | source)
XLA Modules:
  0.0 250.6 jit_solution(16990631362791120303)
XLA Ops:
  7.2 0.0 all-gather.2.cloned.1.call-start
  7.2 39.7 %gather_weights.1 = (bf16[384,1152]{1,0:T(8,128)(2,1)}, bf16[384,384]{1,0:T(8,128)(2,1)}, bf16[384,1536]{1,0:T(8,128)(2,1)}, bf16[1536,384]{1,0:T(8,128)(2,1)}, ...) custom-call(f32[12,1152]{1,0:T(8,128)} %refs_10_.3, f32[12,384]{1,0:T(8,128)} %refs_11_.1, ...), custom_call_target="tpu_custom_call" | custom-call | tf_op jit(solution)/shard_map/gather_weights/pallas_call | solution.py:770
  46.9 0.0 all-gather.2.cloned.1.call-update
  47.0 114.8 %layer.1 = (bf16[4096,384]{1,0:T(8,128)(2,1)}, bf16[4096,384]{1,0:T(8,128)(2,1)}, f32[14336,128]{1,0:T(8,128)}, f32[37,128]{1,0:T(8,128)}) custom-call(s32[16]{0:T(128)} %len_ref.1, bf16[4096,384]{1,0:T(8,128)(2,1)} %tok_ref.1, f32[3,4096]{1,0:T(4,128)} %cen_ref.1, bf16[4096,384]{1,0:T(8,128)(2,1)} %cot_ref.1, f32[37,128]{1,0:T(8,128)} %get-tuple-element.69.small_ref, ...), custom_call_target="tpu_custom_call" | custom-call | tf_op jit(solution)/shard_map/layer/pallas_call | solution.py:301
  161.7 0.0 all-gather.2.cloned.1.call-done
  161.8 79.6 %finish_step.1 = (f32[40,128]{1,0:T(8,128)}, f32[4,16,3072]{2,1,0:T(8,128)}, f32[4,48,384]{2,1,0:T(8,128)}, f32[4,16,384]{2,1,0:T(8,128)}) custom-call(f32[32,448,128]{2,1,0:T(8,128)} %bitcast.5, f32[37,128]{1,0:T(8,128)} %get-tuple-element.78.small, bf16[32,64,1536]{2,1,0:T(8,128)(2,1)} %bitcast.6, f32[1152,1152]{1,0:T(8,128)} %refs_0_.3, ...), custom_call_target="tpu_custom_call" | custom-call | tf_op jit(solution)/shard_map/finish_step/pallas_call | solution.py:1064
  241.4 2.3 hand_out.1
Async XLA Ops:
  7.2 154.6 %all-gather.2.cloned.1.call-start = ((), (), s32[]{:S(2)}) async-start(), calls=%async_computation | async-start | bytes 6488064 | tf_op jit(solution)/shard_map/all_gather | solution.py:1117
Sparse Core Ops, SparseCore 0:
  47.1 67.5 all-gather.1

commit v6 on v5

--- a/solution.py
+++ b/solution.py
@@ -387,8 +387,24 @@
             for role, (axis, stride, size) in roles.items()
         }
 
-    def place(self, **offsets):
-        at = dict(self.index)
+        z = self.z = self.coord["z"]
+        self.line = [z] + [self.by_z(*row) for row in ((1, 0, 1, 2), (2, 2, 3, 1), (3, 3, 0, 0))]
+        self.came_by = [self.by_z(*row) for row in ((1, 0, 1, 2), (1, 2, 3, 2), (1, 2, 1, 2))]
+        self.inbox = [self.by_z(*row) for row in ((1, 0, 0, 0), (3, 1, 1, 2), (4, 3, 2, 4))]
+        self.inner = z // 2 + z % 2 == 1
+
+    def by_z(self, *values):
+        high, low = self.coord["z"] // 2, self.coord["z"] % 2
+        return (1 - high) * ((1 - low) * values[0] + low * values[1]) + high * (
+            (1 - low) * values[2] + low * values[3]
+        )
+
+    def at_z(self, coordinate):
+        axis, stride, _ = self.roles["z"]
+        return {**self.index, axis: self.index[axis] + (coordinate - self.z) * stride}
+
+    def place(self, line=0, **offsets):
+        at = self.at_z(self.line[line]) if line else dict(self.index)
         for role, offset in offsets.items():
             axis, stride, size = self.roles[role]
             other = flipped(self.coord[role], offset, size)
@@ -409,28 +425,48 @@
 class Wire:
     def __init__(self, grid, send_sems, recv_sems):
         self.grid, self.send_sems, self.recv_sems = grid, send_sems, recv_sems
+        self.count = 0
         self.copies = {}
 
-    def send(self, key, source, target, **offsets):
-        number = len(self.copies)
-        copy = pltpu.make_async_remote_copy(
+    def reserve(self, count):
+        self.count += count
+        return self.count - count
+
+    def make(self, number, into, source, target, place):
+        return pltpu.make_async_remote_copy(
             src_ref=source,
             dst_ref=target,
             send_sem=self.send_sems.at[number],
-            recv_sem=self.recv_sems.at[number],
-            device_id=self.grid.place(**offsets),
+            recv_sem=self.recv_sems.at[into],
+            device_id=place,
             device_id_type=MESH_ID,
         )
-        copy.start()
+
+    def send_to(self, key, number, into, source, target, place, when=None):
+        make = functools.partial(self.make, number, into, source, target, place)
+        if when is None:
+            make().start()
+        else:
+            pl.when(when)(lambda: make().start())
         assert key not in self.copies
-        self.copies[key] = copy
+        self.copies[key] = (make, when)
+
+    def send(self, key, source, target, **offsets):
+        number = self.reserve(1)
+        self.send_to(key, number, number, source, target, self.grid.place(**offsets))
 
     def arrived(self, key):
-        self.copies[key].wait_recv()
+        self.copies[key][0]().wait_recv()
+
+    def arrived_at(self, number, target):
+        self.make(number, number, target, target, self.grid.place(c=1)).wait_recv()
 
     def finish(self):
-        for copy in self.copies.values():
-            copy.wait_send()
+        for make, when in self.copies.values():
+            if when is None:
+                make().wait_send()
+            else:
+                pl.when(when)(lambda make=make: make().wait_send())
 
 
 def meet(grid):
@@ -452,30 +488,37 @@
     nz, ny, nx, nc = (roles[role][2] for role in ("z", "y", "x", "c"))
     plane = (ny - 1) + (nx - 1) + 2 * (ny - 1) * (nx - 1)
     core = (nc - 1) * (1 + plane)
-    return (nz - 1) + nz * (plane + core)
+    return 5 + nz * (plane + core)
 
 
 def nothing():
     pass
 
 
-def gather_all(grid, wire, buf, tag, idle=nothing):
-    rows = buf.shape[1]
+def gather_all(grid, wire, buf, tag, rows=None):
+    start, rows = (0, buf.shape[1]) if rows is None else rows
     half = rows // 32 * 16
-    parts = {"a": pl.ds(0, half), "b": pl.ds(half, rows - half)}
+    parts = {
+        None: pl.ds(start, rows),
+        "a": pl.ds(start, half),
+        "b": pl.ds(start + half, rows - half),
+    }
 
     def pass_on(key, slot, part, **offsets):
-        ref = buf.at[slot] if part is None else buf.at[slot, parts[part]]
+        ref = buf.at[slot, parts[part]]
         wire.send((tag,) + key, ref, ref, **offsets)
 
-    zs, ys, xs, cs = ([*grid.offsets(role)] for role in ("z", "y", "x", "c"))
+    def arrived(*key):
+        wire.arrived((tag,) + key)
+
+    ys, xs, cs = ([*grid.offsets(role)] for role in ("y", "x", "c"))
 
     def to_core(key, slot, part=None):
         for c in cs:
             pass_on(("c", c) + key, slot, part, c=c)
 
     def have(b):
-        slot = grid.slot(z=b)
+        slot = grid.slot(line=b)
         for y in ys:
             pass_on(("y", b, y), slot, None, y=y)
         for x in xs:
@@ -484,151 +527,178 @@
 
     def relay(b):
         for y in ys:
-            wire.arrived((tag, "y", b, y))
+            yield
+            arrived("y", b, y)
             for x in xs:
-                pass_on(("a", b, y, x), grid.slot(z=b, y=y), "a", x=x)
-            to_core((b, y, 0, 0), grid.slot(z=b, y=y))
+                pass_on(("a", b, y, x), grid.slot(line=b, y=y), "a", x=x)
+            to_core((b, y, 0, 0), grid.slot(line=b, y=y))
         for x in xs:
-            wire.arrived((tag, "x", b, x))
+            yield
+            arrived("x", b, x)
             for y in ys:
-                pass_on(("b", b, y, x), grid.slot(z=b, x=x), "b", y=y)
-            to_core((b, 0, x, 0), grid.slot(z=b, x=x))
-
-    for z in zs:
-        pass_on(("z", z), grid.slot(), None, z=z)
+                pass_on(("b", b, y, x), grid.slot(line=b, x=x), "b", y=y)
+            to_core((b, 0, x, 0), grid.slot(line=b, x=x))
+
+    base = wire.reserve(5)
+    z = grid.z
+
+    def along(site, line, target, into, when):
+        ref = buf.at[grid.slot(line=line), parts[None]]
+        place = grid.at_z(target)
+        wire.send_to((tag, "z", site), base + site, base + into, ref, ref, place, when)
+
+    along(0, 0, z + 1, 0, z < 3)
+    along(1, 0, z - 1, z // 2, z > 0)
     have(0)
-    idle()
-    for b in zs:
-        wire.arrived((tag, "z", b))
+    onward = ((z + 1, 3 - z), (z - 1, z), (3 * (z - 1), 2))
+    for b in (1, 2, 3):
+        yield
+        wire.arrived_at(base + b - 1, buf.at[grid.slot(line=b), parts[None]])
+        along(1 + b, b, *onward[b - 1], grid.inner)
         have(b)
-        idle()
-        relay(b - 1)
-        idle()
-    relay(len(zs))
-    for b in [0] + zs:
+        yield from relay(b - 1)
+    yield from relay(3)
+    for b in range(4):
         for y in ys:
             for x in xs:
                 for part in ("a", "b"):
-                    wire.arrived((tag, part, b, y, x))
-                    to_core((b, y, x, part), grid.slot(z=b, y=y, x=x), part)
+                    yield
+                    arrived(part, b, y, x)
+                    to_core((b, y, x, part), grid.slot(line=b, y=y, x=x), part)
+    yield
     for key in list(wire.copies):
         if key[:2] == (tag, "c"):
             wire.arrived(key)
 
 
+def together(*chains, idle=nothing):
+    chains = list(chains)
+    while chains:
+        for chain in list(chains):
+            try:
+                next(chain)
+            except StopIteration:
+                chains.remove(chain)
+        idle()
+
+
 def reduce_copies(roles):
     nz, ny, nx, nc = (roles[role][2] for role in ("z", "y", "x", "c"))
     plane = (ny - 1) + (nx - 1) + 2 * (ny - 1) * (nx - 1)
-    return (nc - 1) * nz * ny * nx + nz * plane + (nz - 1)
+    return (nc - 1) * nz * ny * nx + nz * plane + 5
 
 
 def small_copies(roles):
     return sum(roles[role][2] - 1 for role in ("z", "y", "x", "c"))
 
 
-def reduce_scatter(grid, wire, full, small, acc, out_c, in_c, out_p, in_p, out_z, in_z, s_out, s_in, extra, ready=lambda b: None, idle=nothing):
-    rows = full.shape[1]
+def reduce_small(grid, wire, small, s_out, s_in, numbers, result):
+    value = small[...]
+    for stage, role in enumerate(("c", "y", "x", "z")):
+        s_out[stage] = value
+        for offset in grid.offsets(role):
+            number = numbers[role, offset]
+            wire.send(("s", role, offset), s_out.at[stage], s_in.at[number], **{role: offset})
+        yield
+        for offset in grid.offsets(role):
+            wire.arrived(("s", role, offset))
+            value = value + s_in[numbers[role, offset]]
+    result[: value.shape[0], :] = value
+
+
+def reduce_scatter(grid, wire, tag, take, out_c, in_c, out_p, in_p, out_z, in_z, acc, ready, done):
+    rows = acc.shape[0]
     half = rows // 32 * 16
     first, second = pl.ds(0, half), pl.ds(half, rows - half)
-    zs, ys, xs, cs = ([*grid.offsets(role)] for role in ("z", "y", "x", "c"))
-    order = zs[::-1] + [0]
-
-    small_order = ["c", "y", "x", "z"]
-    small_state = {"value": small[...], "stage": 0}
-
-    def small_send():
-        stage = small_state["stage"]
-        role = small_order[stage]
-        s_out[stage] = small_state["value"]
-        for offset in grid.offsets(role):
-            number = extra[(role, offset)]
-            wire.send(("s", role, offset), s_out.at[stage], s_in.at[number], **{role: offset})
-
-    def small_take():
-        stage = small_state["stage"]
-        role = small_order[stage]
-        value = small_state["value"]
-        for offset in grid.offsets(role):
-            wire.arrived(("s", role, offset))
-            value = value + s_in[extra[(role, offset)]]
-        small_state["value"] = value
-        small_state["stage"] = stage + 1
-
-    small_send()
-    for b in order:
-        ready(b)
-        for y in [0] + ys:
-            for x in [0] + xs:
-                for c in cs:
-                    out_c[c - 1, b, y, x] = full[grid.slot(z=b, y=y, x=x, c=c)].astype(BF)
-                    wire.send(
-                        ("c", c, b, y, x), out_c.at[c - 1, b, y, x], in_c.at[c - 1, b, y, x], c=c
-                    )
+    ys, xs, cs = ([*grid.offsets(role)] for role in ("y", "x", "c"))
+    order = [3, 2, 1, 0]
+    base = wire.reserve(5)
+
+    def send(key, source, target, **offsets):
+        wire.send((tag,) + key, source, target, **offsets)
+
+    def arrived(*key):
+        wire.arrived((tag,) + key)
 
     def core_sum(b, y, x):
-        value = full[grid.slot(z=b, y=y, x=x)]
+        value = take(grid.slot(line=b, y=y, x=x))
         for c in cs:
-            wire.arrived(("c", c, b, y, x))
+            arrived("c", c, b, y, x)
             value = value + in_c[c - 1, b, y, x].astype(F32)
         return value
+
+    def to_core(b):
+        ready(b)
+        for y in [*ys, 0]:
+            for x in [*xs, 0]:
+                for c in cs:
+                    out_c[c - 1, b, y, x] = take(grid.slot(line=b, y=y, x=x, c=c)).astype(BF)
+                    send(("c", c, b, y, x), out_c.at[c - 1, b, y, x], in_c.at[c - 1, b, y, x], c=c)
 
     def diagonal(b):
         for y in ys:
             for x in xs:
                 out_p[b, y, x] = core_sum(b, y, x).astype(BF)
-                wire.send(("a", b, y, x), out_p.at[b, y, x, first], in_p.at[b, y, x, first], x=x)
-                wire.send(("b", b, y, x), out_p.at[b, y, x, second], in_p.at[b, y, x, second], y=y)
+                send(("a", b, y, x), out_p.at[b, y, x, first], in_p.at[b, y, x, first], x=x)
+                send(("b", b, y, x), out_p.at[b, y, x, second], in_p.at[b, y, x, second], y=y)
 
     def neighbour(b):
         for y in ys:
             acc[...] = core_sum(b, y, 0)
             for x in xs:
-                wire.arrived(("a", b, y, x))
+                arrived("a", b, y, x)
                 acc[first, :] += in_p[b, y, x, first].astype(F32)
             out_p[b, y, 0] = acc[...].astype(BF)
-            wire.send(("y", b, y), out_p.at[b, y, 0], in_p.at[b, y, 0], y=y)
+            send(("y", b, y), out_p.at[b, y, 0], in_p.at[b, y, 0], y=y)
         for x in xs:
             acc[...] = core_sum(b, 0, x)
             for y in ys:
-                wire.arrived(("b", b, y, x))
+                arrived("b", b, y, x)
                 acc[second, :] += in_p[b, y, x, second].astype(F32)
             out_p[b, 0, x] = acc[...].astype(BF)
-            wire.send(("x", b, x), out_p.at[b, 0, x], in_p.at[b, 0, x], x=x)
+            send(("x", b, x), out_p.at[b, 0, x], in_p.at[b, 0, x], x=x)
 
     def plane_sum(b):
         value = core_sum(b, 0, 0)
         for y in ys:
-            wire.arrived(("y", b, y))
+            arrived("y", b, y)
             value = value + in_p[b, y, 0].astype(F32)
         for x in xs:
-            wire.arrived(("x", b, x))
+            arrived("x", b, x)
             value = value + in_p[b, 0, x].astype(F32)
         return value
 
-    total = None
+    def add_from(inbox):
+        wire.arrived_at(base + inbox, in_z.at[inbox])
+        acc[...] += in_z[inbox].astype(F32)
+
+    for b in order:
+        to_core(b)
+        yield
     for turn in range(len(order) + 2):
-        idle()
         if turn < len(order):
+            yield
             diagonal(order[turn])
         if 1 <= turn <= len(order):
+            yield
             neighbour(order[turn - 1])
-            if small_state["stage"] < 3:
-                small_take()
-                small_send()
-        idle()
         if turn >= 2:
+            yield
             b = order[turn - 2]
-            value = plane_sum(b)
+            acc[...] = plane_sum(b)
             if b:
-                out_z[b - 1] = value.astype(BF)
-                wire.send(("z", b), out_z.at[b - 1], in_z.at[b - 1], z=b)
-            else:
-                total = value
-    small_take()
-    for b in zs:
-        wire.arrived(("z", b))
-        total = total + in_z[b - 1].astype(F32)
-    return total, small_state["value"]
+                yield
+                pl.when(grid.inner)(functools.partial(add_from, 1 + b))
+                out_z[b - 1] = acc[...].astype(BF)
+                inbox = grid.inbox[b - 1]
+                wire.send_to(
+                    (tag, "z", b), base + b - 1, base + inbox, out_z.at[b - 1], in_z.at[inbox],
+                    grid.at_z(grid.came_by[b - 1]),
+                )
+    yield
+    pl.when(grid.z < 3)(functools.partial(add_from, 0))
+    pl.when(grid.z > 0)(functools.partial(add_from, 1))
+    done(acc[...])
 
 
 DECAY = 0.5
@@ -731,7 +801,7 @@
             bases[rows, cols] = pad_rows(lefts[name][...], rows.stop - rows.start).astype(BF)
 
     meet(grid)
-    gather_all(grid, wire, buf, "w", once(pack_bases))
+    together(gather_all(grid, wire, buf, "w"), idle=once(pack_bases))
     for name in NAMES:
         spread = None if lay.rows[name] == lay.padded[name] else lay.spread(name)
         for block in range(WIDTH[name] // LANES):
@@ -908,11 +978,11 @@
     plane = lay.count // grid.size("z")
 
     def full_copy(b):
-        at = pl.multiple_of(flipped(grid.coord["z"], b, grid.size("z")) * plane, plane)
+        at = pl.multiple_of(grid.line[b] * plane, plane)
         part = pl.ds(at, plane)
         return pltpu.make_async_copy(full_hbm.at[part], full.at[part], full_sems.at[b])
 
-    for b in [*grid.offsets("z")][::-1] + [0]:
+    for b in (3, 2, 1, 0):
         full_copy(b).start()
     base_copy = pltpu.make_async_copy(bases_hbm, bases, base_sem)
     base_copy.start()
@@ -971,14 +1041,21 @@
             duties.pop(0)()
 
     meet(grid)
-    total, smalls = reduce_scatter(
-        grid, wire, full, small, acc, out_c, in_c, out_p, in_p, out_z, in_z, s_out, s_in, extra,
-        lambda b: full_copy(b).wait(), idle,
+    small_out[...] = jnp.zeros_like(small_out)
+
+    def share():
+        def done(total):
+            flat[me] = total.astype(BF)
+
+        yield from reduce_scatter(
+            grid, wire, "sum", lambda slot: full[slot], out_c, in_c, out_p, in_p, out_z, in_z, acc,
+            lambda b: full_copy(b).wait(), done,
+        )
+        yield from gather_all(grid, wire, flat, "flat")
+
+    together(
+        share(), reduce_small(grid, wire, small, s_out, s_in, extra, small_out), idle=idle
     )
-    small_out[:SMALL_ROWS, :] = smalls
-    small_out[SMALL_ROWS:, :] = jnp.zeros((40 - SMALL_ROWS, LANES), F32)
-    flat[me] = total.astype(BF)
-    gather_all(grid, wire, flat, "flat", idle)
     while duties:
         idle()
 
@@ -1024,7 +1101,7 @@
         piece = jnp.concatenate([directions[member] for member in group], axis=0)
         steps[me, groups.span(number), :] = pad_rows(piece, groups.rows[number]).astype(BF)
 
-    gather_all(grid, wire, steps, "steps")
+    together(gather_all(grid, wire, steps, "steps"))
 
     partway = {}
     for number, group in enumerate(groups.members):
@@ -1079,7 +1156,7 @@
             pltpu.VMEM((nz, ny, nx, rows, LANES), BF),
             pltpu.VMEM((nz, ny, nx, rows, LANES), BF),
             pltpu.VMEM((nz - 1, rows, LANES), BF),
-            pltpu.VMEM((nz - 1, rows, LANES), BF),
+            pltpu.VMEM((5, rows, LANES), BF),
             pltpu.VMEM((4, SMALL_ROWS, LANES), F32),
             pltpu.VMEM((len(extra), SMALL_ROWS, LANES), F32),
             pltpu.VMEM((slots, rows, LANES), BF),

time: 251 us -> 260 us (1.036)
  Pallas kernels: 236 us -> 245 us
    pallas_call x1, Pallas kernels: 79.6 us -> 91.5 us  [finish_step(): pl.pallas_call(functools.partial(tail_kernel, roles, sizes, lay, groups,...]
    pallas_call x1, Pallas kernels: 39.7 us -> 36.8 us  [gather_weights(): pl.pallas_call(functools.partial(head_kernel, roles, sizes, lay), out_sha...]
  transfers between devices with their start and end apart: 1 -> 1, of which waited for: 0 -> 0; matrix products, arithmetic and copies ran while one was open for 0% -> 0% of each run, Pallas kernels for 46% -> 44%
where the time goes in v6:
time: 260 us
  Pallas kernels  245 us (94%)
  between operations  14.1 us (5%)
    pallas_call x1, Pallas kernels, layer_pass(): pl.pallas_call(functools.partial(layer_kernel, fc=fc, group=group), out_s...  115 us
    pallas_call x1, Pallas kernels, finish_step(): pl.pallas_call(functools.partial(tail_kernel, roles, sizes, lay, groups,...  91.5 us
    pallas_call x1, Pallas kernels, gather_weights(): pl.pallas_call(functools.partial(head_kernel, roles, sizes, lay), out_sha...  36.8 us
  transfers between devices with their start and end apart: 1, of which 0 were waited for; matrix products, arithmetic and copies ran while one was open for 0% of the time, Pallas kernels for 44%

profile of v6, /device:TPU:1, one launch (start us, length us, event | category | flops | bytes accessed | tf_op | source)
XLA Modules:
  0.0 259.6 jit_solution(7919675199017890984)
XLA Ops:
  7.2 0.0 all-gather.2.cloned.1.call-start
  7.2 36.8 %gather_weights.1 = (bf16[384,1152]{1,0:T(8,128)(2,1)}, bf16[384,384]{1,0:T(8,128)(2,1)}, bf16[384,1536]{1,0:T(8,128)(2,1)}, bf16[1536,384]{1,0:T(8,128)(2,1)}, ...) custom-call(f32[12,1152]{1,0:T(8,128)} %refs_10_.3, f32[12,384]{1,0:T(8,128)} %refs_11_.1, ...), custom_call_target="tpu_custom_call" | custom-call | tf_op jit(solution)/shard_map/gather_weights/pallas_call | solution.py:840
  44.1 0.0 all-gather.2.cloned.1.call-update
  44.1 114.8 %layer.1 = (bf16[4096,384]{1,0:T(8,128)(2,1)}, bf16[4096,384]{1,0:T(8,128)(2,1)}, f32[14336,128]{1,0:T(8,128)}, f32[37,128]{1,0:T(8,128)}) custom-call(s32[16]{0:T(128)} %len_ref.1, bf16[4096,384]{1,0:T(8,128)(2,1)} %tok_ref.1, f32[3,4096]{1,0:T(4,128)} %cen_ref.1, bf16[4096,384]{1,0:T(8,128)(2,1)} %cot_ref.1, f32[37,128]{1,0:T(8,128)} %get-tuple-element.69.small_ref, ...), custom_call_target="tpu_custom_call" | custom-call | tf_op jit(solution)/shard_map/layer/pallas_call | solution.py:301
  158.9 0.0 all-gather.2.cloned.1.call-done
  158.9 91.5 %finish_step.1 = (f32[40,128]{1,0:T(8,128)}, f32[4,16,3072]{2,1,0:T(8,128)}, f32[4,48,384]{2,1,0:T(8,128)}, f32[4,16,384]{2,1,0:T(8,128)}) custom-call(f32[32,448,128]{2,1,0:T(8,128)} %bitcast.5, f32[37,128]{1,0:T(8,128)} %get-tuple-element.78.small, bf16[32,64,1536]{2,1,0:T(8,128)(2,1)} %bitcast.6, f32[1152,1152]{1,0:T(8,128)} %refs_0_.3, ...), custom_call_target="tpu_custom_call" | custom-call | tf_op jit(solution)/shard_map/finish_step/pallas_call | solution.py:1141
  250.4 2.3 hand_out.1
Async XLA Ops:
  7.2 151.7 %all-gather.2.cloned.1.call-start = ((), (), s32[]{:S(2)}) async-start(), calls=%async_computation | async-start | bytes 6488064 | tf_op jit(solution)/shard_map/all_gather | solution.py:1194
Sparse Core Ops, SparseCore 0:
  44.2 67.4 all-gather.1

commit v7 on v6

--- a/solution.py
+++ b/solution.py
@@ -52,6 +52,15 @@
     spread = jnp.mean(centred * centred, axis=-1, keepdims=True)
     inv = lax.rsqrt(spread + EPSILON)
     return centred * inv, inv
+
+
+def thirds(value):
+    terms = []
+    for _ in range(3):
+        term = value.astype(BF)
+        terms.append(term)
+        value = value - term.astype(F32)
+    return terms
 
 
 def col8(x):
@@ -90,6 +99,14 @@
     ds_s,
     dq_s,
     ag_s,
+    hid_s,
+    act_s,
+    low_s,
+    hg_s,
+    inv_s,
+    xh2_s,
+    gy_s,
+    bgl_s,
     *,
     fc,
     group,
@@ -129,12 +146,11 @@
     pos_first = small_ref[34:37, :]
     cen = cen_ref[...]
 
-    pos_hidden = (
-        lax.dot_general(
-            cen, pos_first, (((0,), (0,)), ((), ())), precision=HIGHEST, preferred_element_type=F32
-        )
-        + hidden_bias
+    cen_terms = jnp.concatenate(thirds(cen) + [jnp.zeros((7, rows), BF)], axis=0)
+    first_terms = jnp.concatenate(
+        [pos_first.astype(BF)] * 3 + [jnp.zeros((7, PH), BF)], axis=0
     )
+    pos_hidden = tn(cen_terms, first_terms) + hidden_bias
     pos_act, pos_slope = gelu_pair(pos_hidden)
     pos_low = pos_act.astype(BF)
     posh_s[...] = pos_slope
@@ -186,47 +202,67 @@
     branch_in = emb_s[...] + tn(att_s[...], wout_ref[...]) + attn_bias
     bin_s[...] = branch_in
     xhat_two, inv_two = norm_parts(branch_in)
+    xh2_s[...] = xhat_two
     n2 = (xhat_two * gain_two + shift_two).astype(BF)
     n2_t = n2.T
     gy = jnp.where(live(D), cot_ref[...].astype(F32), 0.0)
+    gy_s[...] = gy
     gy_low = gy.astype(BF)
     gy_t = gy_low.T
     add_small(15, col8(gy))
 
-    for c in range(FF // fc):
+    blocks = fc // LANES
+
+    def widen(c):
         cols = slice(c * fc, (c + 1) * fc)
-        up_bias = vec(21 + c * (fc // LANES), fc // LANES)
-        hidden = nn(n2, wup_ref[:, cols]) + up_bias
-        act, slope = gelu_pair(hidden)
-        act_low = act.astype(BF)
-        part = nn(act_low, wdown_ref[cols, :])
-        act_grad = nt(gy_low, wdown_ref[cols, :])
-        hg = (act_grad * slope).astype(BF)
-        add_small(21 + c * (fc // LANES), col8(hg.astype(F32)))
-        back = nt(hg, wup_ref[:, cols])
-        if c == 0:
-            ff_s[...] = part
-            n2g_s[...] = back
-        else:
-            ff_s[...] += part
-            n2g_s[...] += back
-        add_grad(UP_AT + c * (fc // LANES), nn(n2_t, hg))
-        add_grad(DOWN_AT + c * (fc // LANES), nn(gy_t, act_low))
+        hid_s[c % 2] = nn(n2, wup_ref[:, cols])
+        act_s[c % 2] = nt(gy_low, wdown_ref[cols, :])
+
+    def bend(c):
+        cols = slice(c * fc, (c + 1) * fc)
+        act, slope = gelu_pair(hid_s[c % 2] + vec(21 + c * blocks, blocks))
+        low_s[:, cols] = act.astype(BF)
+        hg = (act_s[c % 2] * slope).astype(BF)
+        hg_s[:, cols] = hg
+        add_small(21 + c * blocks, col8(hg.astype(F32)))
+
+    def narrow(c):
+        cols = slice(c * fc, (c + 1) * fc)
+        add_grad(UP_AT + c * blocks, nn(n2_t, hg_s[:, cols]))
+        add_grad(DOWN_AT + c * blocks, nn(gy_t, low_s[:, cols]))
+
+    count = FF // fc
+    for turn in range(count + 1):
+        for lag, stage in enumerate((widen, bend)):
+            if 0 <= turn - lag < count:
+                stage(turn - lag)
+    n2g_s[...] = nt(hg_s[...], wup_ref[...])
+    ff_s[...] = nn(low_s[...], wdown_ref[...])
 
     out_ref[...] = (bin_s[...] + ff_s[...] + down_bias).astype(BF)
 
-    n2g = n2g_s[...]
-    add_small(6, col8(n2g * xhat_two))
-    add_small(9, col8(n2g))
-    u = n2g * gain_two
-    bg = gy + inv_two * (
-        u
-        - jnp.mean(u, axis=-1, keepdims=True)
-        - xhat_two * jnp.mean(u * xhat_two, axis=-1, keepdims=True)
-    )
-    bin_s[...] = bg
-    add_small(12, col8(bg))
-    bg_low = bg.astype(BF)
+    inv_s[...] = inv_two
+    parts = count
+    height = rows // parts if rows % (16 * parts) == 0 else rows // 4
+    for turn in range(max(count, rows // height)):
+        if turn < rows // height:
+            at = slice(turn * height, (turn + 1) * height)
+            n2g = n2g_s[at, :]
+            xhat_two = xh2_s[at, :]
+            add_small(6, col8(n2g * xhat_two))
+            add_small(9, col8(n2g))
+            u = n2g * gain_two
+            bg = gy_s[at, :] + inv_s[at, :] * (
+                u
+                - jnp.mean(u, axis=-1, keepdims=True)
+                - xhat_two * jnp.mean(u * xhat_two, axis=-1, keepdims=True)
+            )
+            bin_s[at, :] = bg
+            add_small(12, col8(bg))
+            bgl_s[at, :] = bg.astype(BF)
+        if turn < count:
+            narrow(turn)
+    bg_low = bgl_s[...]
     add_grad(OUT_AT, nn(att_s[...], bg_low))
     ag = nt(bg_low, wout_ref[...]).astype(BF)
 
@@ -263,26 +299,36 @@
     staged(probs_back, scores_back, heads_back)
 
     qg = qg_s[...]
-    add_grad(QKV_AT, nn(n1_s[...].T, qg))
-    n1g = nt(qg, wqkv_ref[...])
-    xhat = xh1_s[...]
-    add_small(0, col8(n1g * xhat))
-    add_small(3, col8(n1g))
-    u = n1g * gain_one
-    eg = bin_s[...] + inv_one * (
-        u
-        - jnp.mean(u, axis=-1, keepdims=True)
-        - xhat * jnp.mean(u * xhat, axis=-1, keepdims=True)
-    )
-    add_small(18, col8(eg))
-    eg_low = eg.astype(BF)
-    gtok_ref[...] = eg_low
+    n2g_s[...] = nt(qg, wqkv_ref[...])
+    inv_s[...] = inv_one
+    n1_t = n1_s[...].T
+    height = rows // 4
+    for turn in range(4):
+        at = slice(turn * height, (turn + 1) * height)
+        n1g = n2g_s[at, :]
+        xhat = xh1_s[at, :]
+        add_small(0, col8(n1g * xhat))
+        add_small(3, col8(n1g))
+        u = n1g * gain_one
+        eg = bin_s[at, :] + inv_s[at, :] * (
+            u
+            - jnp.mean(u, axis=-1, keepdims=True)
+            - xhat * jnp.mean(u * xhat, axis=-1, keepdims=True)
+        )
+        add_small(18, col8(eg))
+        gtok_ref[at, :] = eg.astype(BF)
+        if turn < 3:
+            add_grad(QKV_AT + 3 * turn, nn(n1_t, qg_s[:, turn * D : (turn + 1) * D]))
+    eg_low = gtok_ref[...]
     add_grad(POS_AT, tn(eg_low, pos_low))
     phg = nt(eg_low, wpos_ref[...]) * posh_s[...]
     add_small(33, col8(phg))
-    pf_grad = jnp.dot(cen, phg, precision=HIGHEST, preferred_element_type=F32)
+    products = nn(cen_terms, jnp.concatenate(thirds(phg), axis=1))
+    pf_grad = products[:, :PH] + products[:, PH : 2 * PH] + products[:, 2 * PH :]
     for i in range(3):
-        sacc[0:1, (34 + i) * LANES : (35 + i) * LANES] += pf_grad[i : i + 1, :]
+        sacc[0:1, (34 + i) * LANES : (35 + i) * LANES] += (
+            pf_grad[i : i + 1, :] + pf_grad[i + 3 : i + 4, :] + pf_grad[i + 6 : i + 7, :]
+        )
 
     @pl.when(step == last)
     def _():
@@ -292,7 +338,7 @@
             )
 
 
-def layer_pass(tokens, centres, lengths, cotangent, small_rows, wqkv, wout, wup, wdown, wpos, fc=768, group=2):
+def layer_pass(tokens, centres, lengths, cotangent, small_rows, wqkv, wout, wup, wdown, wpos, fc=256, group=2):
     clouds = lengths.shape[0]
     rows = clouds * LMAX
     span = group * LMAX
@@ -343,6 +389,14 @@
                 pltpu.VMEM((2, LMAX, LMAX), BF),
                 pltpu.VMEM((D, span), BF),
                 pltpu.VMEM((span, D), BF),
+                pltpu.VMEM((2, span, fc), F32),
+                pltpu.VMEM((2, span, fc), F32),
+                pltpu.VMEM((span, FF), BF),
+                pltpu.VMEM((span, FF), BF),
+                pltpu.VMEM((span, 1), F32),
+                pltpu.VMEM((span, D), F32),
+                pltpu.VMEM((span, D), F32),
+                pltpu.VMEM((span, D), BF),
             ],
         ),
         compiler_params=pltpu.CompilerParams(vmem_limit_bytes=60 * 1024 * 1024),
@@ -571,15 +625,37 @@
             wire.arrived(key)
 
 
-def together(*chains, idle=nothing):
-    chains = list(chains)
+def together(*chains, idle=nothing, quiet=0):
+    chains = [chain if isinstance(chain, tuple) else (chain, 1) for chain in chains]
+    turn = 0
     while chains:
         for chain in list(chains):
-            try:
-                next(chain)
-            except StopIteration:
-                chains.remove(chain)
-        idle()
+            if turn % chain[1] == 0 or len(chains) == 1:
+                try:
+                    next(chain[0])
+                except StopIteration:
+                    chains.remove(chain)
+        if turn >= quiet:
+            idle()
+        turn += 1
+
+
+def exchange_copies(roles):
+    return sum(roles[role][2] - 1 for role in ("c", "x", "y", "z"))
+
+
+def exchange_all(grid, wire, tag, blocks, pack):
+    pack()
+    for stage, role in enumerate(("c", "x", "y", "z")):
+        source, target = blocks[stage], blocks[stage + 1]
+        coord, size = grid.coord[role], grid.size(role)
+        for offset in grid.offsets(role):
+            part = source.at[:, :, :, flipped(coord, offset, size)]
+            wire.send((tag, role, offset), part, target.at[offset], **{role: offset})
+        target[0] = source[:, :, :, coord]
+        yield
+        for offset in grid.offsets(role):
+            wire.arrived((tag, role, offset))
 
 
 def reduce_copies(roles):
@@ -610,9 +686,8 @@
     rows = acc.shape[0]
     half = rows // 32 * 16
     first, second = pl.ds(0, half), pl.ds(half, rows - half)
-    ys, xs, cs = ([*grid.offsets(role)] for role in ("y", "x", "c"))
-    order = [3, 2, 1, 0]
-    base = wire.reserve(5)
+    zs, ys, xs, cs = ([*grid.offsets(role)] for role in ("z", "y", "x", "c"))
+    order = zs + [0]
 
     def send(key, source, target, **offsets):
         wire.send((tag,) + key, source, target, **offsets)
@@ -621,7 +696,7 @@
         wire.arrived((tag,) + key)
 
     def core_sum(b, y, x):
-        value = take(grid.slot(line=b, y=y, x=x))
+        value = take(grid.slot(z=b, y=y, x=x))
         for c in cs:
             arrived("c", c, b, y, x)
             value = value + in_c[c - 1, b, y, x].astype(F32)
@@ -632,7 +707,7 @@
         for y in [*ys, 0]:
             for x in [*xs, 0]:
                 for c in cs:
-                    out_c[c - 1, b, y, x] = take(grid.slot(line=b, y=y, x=x, c=c)).astype(BF)
+                    out_c[c - 1, b, y, x] = take(grid.slot(z=b, y=y, x=x, c=c)).astype(BF)
                     send(("c", c, b, y, x), out_c.at[c - 1, b, y, x], in_c.at[c - 1, b, y, x], c=c)
 
     def diagonal(b):
@@ -668,10 +743,6 @@
             value = value + in_p[b, 0, x].astype(F32)
         return value
 
-    def add_from(inbox):
-        wire.arrived_at(base + inbox, in_z.at[inbox])
-        acc[...] += in_z[inbox].astype(F32)
-
     for b in order:
         to_core(b)
         yield
@@ -685,19 +756,16 @@
         if turn >= 2:
             yield
             b = order[turn - 2]
-            acc[...] = plane_sum(b)
+            value = plane_sum(b)
             if b:
-                yield
-                pl.when(grid.inner)(functools.partial(add_from, 1 + b))
-                out_z[b - 1] = acc[...].astype(BF)
-                inbox = grid.inbox[b - 1]
-                wire.send_to(
-                    (tag, "z", b), base + b - 1, base + inbox, out_z.at[b - 1], in_z.at[inbox],
-                    grid.at_z(grid.came_by[b - 1]),
-                )
+                out_z[b - 1] = value.astype(BF)
+                send(("z", b), out_z.at[b - 1], in_z.at[b - 1], z=b)
+            else:
+                acc[...] = value
     yield
-    pl.when(grid.z < 3)(functools.partial(add_from, 0))
-    pl.when(grid.z > 0)(functools.partial(add_from, 1))
+    for b in zs:
+        arrived("z", b)
+        acc[...] += in_z[b - 1].astype(F32)
     done(acc[...])
 
 
@@ -706,6 +774,7 @@
 WEIGHT_DECAY = 0.05
 VMEM_LIMIT = 60 * 1024 * 1024
 NAMES = ("qkv", "out", "up", "down", "pos")
+BASE_LANES = {"qkv": 64, "out": 80, "up": 96, "pos": 112}
 HEIGHT = {"qkv": D, "out": D, "up": D, "down": FF, "pos": PH}
 WIDTH = {"qkv": 3 * D, "out": D, "up": FF, "down": D, "pos": D}
 SMALLS = SMALL_ROWS * LANES
@@ -731,16 +800,6 @@
             at += 16
         self.total = at
 
-    @property
-    def base_rows(self):
-        return self.padded["down"] + 16
-
-    def base_place(self, name):
-        if name == "down":
-            return slice(0, self.padded["down"]), slice(0, FF)
-        at = {"qkv": 0, "out": D, "up": 2 * D, "pos": 3 * D}[name]
-        return slice(self.padded["down"], self.base_rows), slice(at, at + HEIGHT[name])
-
     def span(self, name, block):
         at = self.start[name] + block * self.padded[name]
         return slice(at, at + self.padded[name])
@@ -777,7 +836,8 @@
     small_ref = refs[5]
     lefts = dict(zip(NAMES, refs[6:11]))
     outs = dict(zip(NAMES, refs[11:16]))
-    flat_ref, bases, buf, send_sems, recv_sems = refs[16:]
+    flat_ref, bases, buf = refs[16:19]
+    blocks, (send_sems, recv_sems) = refs[19:24], refs[24:]
     grid = Grid(roles, sizes)
     wire = Wire(grid, send_sems, recv_sems)
     own = grid.slot()
@@ -795,13 +855,44 @@
     buf[own, lay.small_at : lay.small_at + 16, :] = pad_rows(lines, 16).astype(BF)
 
     def pack_bases():
-        bases[lay.padded["down"] :, :] = jnp.zeros((16, FF), BF)
-        for name in NAMES:
-            rows, cols = lay.base_place(name)
-            bases[rows, cols] = pad_rows(lefts[name][...], rows.stop - rows.start).astype(BF)
+        lane = lax.broadcasted_iota(jnp.int32, (1, LANES), 1)
+
+        def piece(name, owner, target):
+            width = lay.rows[name]
+            at = owner * width
+            tile, place = at // LANES * LANES, at % LANES
+            value = lefts[name][:, tile : tile + LANES]
+            shift = (target - place) % LANES
+            value = pltpu.roll(value, shift, 1) if shift else value
+            if place + width > LANES:
+                after = lefts[name][:, tile + LANES : tile + 2 * LANES]
+                after = pltpu.roll(after, shift, 1) if shift else after
+                value = jnp.where(lane < target + LANES - place, value, after)
+            value = jnp.where((lane >= target) & (lane < target + width), value, 0.0)
+            return pad_rows(value, lay.padded["down"])
+
+        for owner in range(lay.count):
+            index = {"dp": owner // sizes["fsdp"], "fsdp": owner % sizes["fsdp"]}
+            z, y, x, core = (
+                index[axis] // stride % size
+                for axis, stride, size in (roles[role] for role in ("z", "y", "x", "c"))
+            )
+            value = piece("down", owner, 0)
+            for name, target in BASE_LANES.items():
+                value = value + piece(name, owner, target)
+            blocks[0][z, y, x, core] = value.astype(BF)
 
     meet(grid)
-    together(gather_all(grid, wire, buf, "w"), idle=once(pack_bases))
+    together(
+        gather_all(grid, wire, buf, "w"),
+        (exchange_all(grid, wire, "e", blocks, pack_bases), 4),
+    )
+    nz, ny, nx, nc = (grid.size(role) for role in ("z", "y", "x", "c"))
+    for z in range(nz):
+        for y in range(ny):
+            for x in range(nx):
+                for core in range(nc):
+                    bases[grid.slot(z=z, y=y, x=x, c=core)] = blocks[4][z, y, x, core]
     for name in NAMES:
         spread = None if lay.rows[name] == lay.padded[name] else lay.spread(name)
         for block in range(WIDTH[name] // LANES):
@@ -836,18 +927,25 @@
 
 
 def gather_weights(roles, sizes, lay, masters, smalls, lefts):
-    count = gather_copies(roles)
+    count = gather_copies(roles) + exchange_copies(roles)
+    nz, ny, nx, nc = (roles[role][2] for role in ("z", "y", "x", "c"))
+    block = (lay.padded["down"], LANES)
     return pl.pallas_call(
         functools.partial(head_kernel, roles, sizes, lay),
         out_shape=tuple(jax.ShapeDtypeStruct((HEIGHT[n], WIDTH[n]), BF) for n in NAMES)
         + (
             jax.ShapeDtypeStruct((SMALL_ROWS, LANES), F32),
-            jax.ShapeDtypeStruct((lay.base_rows, FF), BF),
+            jax.ShapeDtypeStruct((lay.count,) + block, BF),
         ),
         in_specs=[vmem()] * 11,
         out_specs=tuple([vmem()] * 7),
         scratch_shapes=[
             pltpu.VMEM((lay.count, lay.total, LANES), BF),
+            pltpu.VMEM((nz, ny, nx, nc) + block, BF),
+            pltpu.VMEM((nc, nz, ny, nx) + block, BF),
+            pltpu.VMEM((nx, nc, nz, ny) + block, BF),
+            pltpu.VMEM((ny, nx, nc, nz) + block, BF),
+            pltpu.VMEM((nz, ny, nx, nc) + block, BF),
             pltpu.SemaphoreType.DMA((count,)),
             pltpu.SemaphoreType.DMA((count,)),
         ],
@@ -953,7 +1051,7 @@
     )(index, small, *packed)
 
 
-def tail_kernel(roles, sizes, lay, groups, extra, full_hbm, small, bases_hbm, *refs):
+def tail_kernel(roles, sizes, lay, groups, extra, full_hbm, small, bases, *refs):
     rights_hbm, lefts, masters, firsts, seconds = (
         dict(zip(NAMES, refs[5 * i : 5 * i + 5])) for i in range(5)
     )
@@ -966,11 +1064,11 @@
         target[kind, : value.shape[0], at + cols.start : at + cols.stop] = value
 
     full, acc, out_c, in_c, out_p, in_p, out_z, in_z, s_out, s_in = rest[:10]
-    flat, steps, bases, coarse = rest[10:14]
-    rights = dict(zip(NAMES, rest[14:19]))
-    picks = dict(zip(NAMES, rest[19:24]))
-    thins = rest[24 : 24 + len(groups.kinds)]
-    send_sems, recv_sems, full_sems, base_sem, right_sems = rest[24 + len(groups.kinds) :]
+    flat, steps, coarse = rest[10:13]
+    rights = dict(zip(NAMES, rest[13:18]))
+    picks = dict(zip(NAMES, rest[18:23]))
+    thins = rest[23 : 23 + len(groups.kinds)]
+    send_sems, recv_sems, full_sems, right_sems = rest[23 + len(groups.kinds) :]
     grid = Grid(roles, sizes)
     wire = Wire(grid, send_sems, recv_sems)
     me = grid.slot()
@@ -978,14 +1076,12 @@
     plane = lay.count // grid.size("z")
 
     def full_copy(b):
-        at = pl.multiple_of(grid.line[b] * plane, plane)
+        at = pl.multiple_of(flipped(grid.coord["z"], b, grid.size("z")) * plane, plane)
         part = pl.ds(at, plane)
         return pltpu.make_async_copy(full_hbm.at[part], full.at[part], full_sems.at[b])
 
-    for b in (3, 2, 1, 0):
+    for b in (1, 2, 3, 0):
         full_copy(b).start()
-    base_copy = pltpu.make_async_copy(bases_hbm, bases, base_sem)
-    base_copy.start()
 
     chunks = [(name, at) for name in NAMES for at in range(0, WIDTH[name], RIGHT_CHUNK)]
 
@@ -997,8 +1093,9 @@
             right_sems.at[number],
         )
 
-    right_copy(0).start()
-    right_copy(1).start()
+    def begin():
+        right_copy(0).start()
+        right_copy(1).start()
 
     def round_right(number):
         name, at = chunks[number]
@@ -1012,9 +1109,9 @@
         row = lax.broadcasted_iota(jnp.int32, (padded, height), 0)
         col = lax.broadcasted_iota(jnp.int32, (padded, height), 1)
         pick = ((row < rows) & (col == me * rows + row)).astype(F32).astype(BF)
-        base_rows, base_cols = lay.base_place(name)
-        base = bases[:, base_rows, base_cols]
-        left_rows = nt(pick, base.reshape(base.shape[0] * base.shape[1], height)).astype(BF)
+        at = BASE_LANES.get(name, 0)
+        base = bases[:, :padded, :].reshape(lay.count * padded, LANES).T
+        left_rows = base[at : at + padded, :]
         if rows != padded:
             left_rows = nt(left_rows, lay.spread(name)).astype(BF)
         picks[name][:padded, :] = left_rows
@@ -1031,8 +1128,7 @@
             thins[number][at : at + 2 * padded, :] = left
             at += 2 * padded
 
-    duties = [functools.partial(round_right, i) for i in range(len(chunks))]
-    duties += [base_copy.wait]
+    duties = [begin] + [functools.partial(round_right, i) for i in range(len(chunks))]
     duties += [functools.partial(make_pick, name) for name in NAMES]
     duties += [functools.partial(make_thin, i) for i in range(len(groups.kinds))]
 
@@ -1053,9 +1149,8 @@
         )
         yield from gather_all(grid, wire, flat, "flat")
 
-    together(
-        share(), reduce_small(grid, wire, small, s_out, s_in, extra, small_out), idle=idle
-    )
+    smalls = reduce_small(grid, wire, small, s_out, s_in, extra, small_out)
+    together(share(), (smalls, 6), idle=idle, quiet=5)
     while duties:
         idle()
 
@@ -1146,7 +1241,7 @@
             jax.ShapeDtypeStruct((4, lay.padded["down"], D), F32),
             jax.ShapeDtypeStruct((4, lay.padded["pos"], D), F32),
         ),
-        in_specs=[anywhere, vmem(), anywhere] + [anywhere] * 5 + [vmem()] * 20,
+        in_specs=[anywhere, vmem(), vmem()] + [anywhere] * 5 + [vmem()] * 20,
         out_specs=tuple([vmem()] * 4),
         scratch_shapes=[
             pltpu.VMEM((slots, rows, LANES), F32),
@@ -1156,12 +1251,11 @@
             pltpu.VMEM((nz, ny, nx, rows, LANES), BF),
             pltpu.VMEM((nz, ny, nx, rows, LANES), BF),
             pltpu.VMEM((nz - 1, rows, LANES), BF),
-            pltpu.VMEM((5, rows, LANES), BF),
+            pltpu.VMEM((nz - 1, rows, LANES), BF),
             pltpu.VMEM((4, SMALL_ROWS, LANES), F32),
             pltpu.VMEM((len(extra), SMALL_ROWS, LANES), F32),
             pltpu.VMEM((slots, rows, LANES), BF),
             pltpu.VMEM((slots, groups.total, LANES), BF),
-            pltpu.VMEM(bases.shape, BF),
             pltpu.VMEM((2, RIGHT_CHUNK, FF), F32),
         ]
         + [pltpu.VMEM((WIDTH[name], WIDTH[name]), BF) for name in NAMES]
@@ -1171,7 +1265,6 @@
             pltpu.SemaphoreType.DMA((count,)),
             pltpu.SemaphoreType.DMA((count,)),
             pltpu.SemaphoreType.DMA((nz,)),
-            pltpu.SemaphoreType.DMA,
             pltpu.SemaphoreType.DMA((chunks,)),
         ],
         compiler_params=pltpu.CompilerParams(
@@ -1191,7 +1284,6 @@
     lay = Layout(count, False)
     *weights, small_rows, bases = gather_weights(roles, sizes, heads, masters, smalls, lefts)
     w_qkv, w_out, w_up, w_down, w_pos = weights
-    whole_bases = lax.all_gather(bases, AXES, axis=0, tiled=True)
     layer_out, grad_tokens, full, small_grads = layer_pass(
         tokens, centres, lengths, cotangent, small_rows, w_qkv, w_out, w_up, w_down, w_pos
     )
@@ -1201,7 +1293,7 @@
         lay,
         full.reshape(count, FLAT_ROWS // count, LANES),
         small_grads,
-        whole_bases.reshape(count, heads.base_rows, FF),
+        bases,
         rights,
         lefts,
         masters,

time: 260 us -> 243 us (0.935)
  between operations: 14.1 us -> 0.87 us
  Pallas kernels: 245 us -> 242 us
    pallas_call x1, Pallas kernels: 91.5 us -> 82.9 us  [finish_step(): pl.pallas_call(functools.partial(tail_kernel, roles, sizes, lay, groups,...]
    pallas_call x1, Pallas kernels: 36.8 us -> 45.1 us  [gather_weights(): pl.pallas_call(functools.partial(head_kernel, roles, sizes, lay), out_sha...]
    pallas_call x1, Pallas kernels: 115 us -> 111 us  [layer_pass(): pl.pallas_call(functools.partial(layer_kernel, fc=fc, group=group), out_s...]
  transfers between devices with their start and end apart: 1 -> 0, of which waited for: 0 -> 0; matrix products, arithmetic and copies ran while one was open for 0% -> 0% of each run, Pallas kernels for 44% -> 0%
where the time goes in v7:
time: 243 us
  Pallas kernels  242 us (100%)
    pallas_call x1, Pallas kernels, layer_pass(): pl.pallas_call(functools.partial(layer_kernel, fc=fc, group=group), out_s...  111 us
    pallas_call x1, Pallas kernels, finish_step(): pl.pallas_call(functools.partial(tail_kernel, roles, sizes, lay, groups,...  82.9 us
    pallas_call x1, Pallas kernels, gather_weights(): pl.pallas_call(functools.partial(head_kernel, roles, sizes, lay), out_sha...  45.1 us

profile of v7, /device:TPU:1, one launch (start us, length us, event | category | flops | bytes accessed | tf_op | source)
XLA Modules:
  0.0 242.6 jit_solution(15870772964103950669)
XLA Ops:
  0.7 45.1 %gather_weights.1 = (bf16[384,1152]{1,0:T(8,128)(2,1)}, bf16[384,384]{1,0:T(8,128)(2,1)}, bf16[384,1536]{1,0:T(8,128)(2,1)}, bf16[1536,384]{1,0:T(8,128)(2,1)}, ...) custom-call(f32[12,1152]{1,0:T(8,128)} %refs_10_.3, f32[12,384]{1,0:T(8,128)} %refs_11_.1, ...), custom_call_target="tpu_custom_call" | custom-call | tf_op jit(solution)/shard_map/gather_weights/pallas_call | solution.py:933
  45.8 111.4 %layer.1 = (bf16[4096,384]{1,0:T(8,128)(2,1)}, bf16[4096,384]{1,0:T(8,128)(2,1)}, f32[14336,128]{1,0:T(8,128)}, f32[37,128]{1,0:T(8,128)}) custom-call(s32[16]{0:T(128)} %len_ref.1, bf16[4096,384]{1,0:T(8,128)(2,1)} %tok_ref.1, f32[3,4096]{1,0:T(4,128)} %cen_ref.1, bf16[4096,384]{1,0:T(8,128)(2,1)} %cot_ref.1, f32[37,128]{1,0:T(8,128)} %get-tuple-element.69.small_ref, ...), custom_call_target="tpu_custom_call" | custom-call | tf_op jit(solution)/shard_map/layer/pallas_call | solution.py:347
  157.2 82.9 %finish_step.1 = (f32[40,128]{1,0:T(8,128)}, f32[4,16,3072]{2,1,0:T(8,128)}, f32[4,48,384]{2,1,0:T(8,128)}, f32[4,16,384]{2,1,0:T(8,128)}) custom-call(f32[32,448,128]{2,1,0:T(8,128)} %bitcast.4, f32[37,128]{1,0:T(8,128)} %get-tuple-element.78.small, bf16[32,48,128]{2,1,0:T(8,128)(2,1)} %get-tuple-element.79.bases, f32[1152,1152]{1,0:T(8,128)} %refs_0_.3, ...), custom_call_target="tpu_custom_call" | custom-call | tf_op jit(solution)/shard_map/finish_step/pallas_call | solution.py:1236
  240.1 2.3 hand_out.1

commit v8 on v7

--- a/solution.py
+++ b/solution.py
@@ -774,7 +774,8 @@
 WEIGHT_DECAY = 0.05
 VMEM_LIMIT = 60 * 1024 * 1024
 NAMES = ("qkv", "out", "up", "down", "pos")
-BASE_LANES = {"qkv": 64, "out": 80, "up": 96, "pos": 112}
+BASE_PLACE = {"qkv": (0, 96), "out": (0, 112), "up": (16, 96), "pos": (16, 112)}
+BASE_ROWS = 32
 HEIGHT = {"qkv": D, "out": D, "up": D, "down": FF, "pos": PH}
 WIDTH = {"qkv": 3 * D, "out": D, "up": FF, "down": D, "pos": D}
 SMALLS = SMALL_ROWS * LANES
@@ -869,7 +870,7 @@
                 after = pltpu.roll(after, shift, 1) if shift else after
                 value = jnp.where(lane < target + LANES - place, value, after)
             value = jnp.where((lane >= target) & (lane < target + width), value, 0.0)
-            return pad_rows(value, lay.padded["down"])
+            return value
 
         for owner in range(lay.count):
             index = {"dp": owner // sizes["fsdp"], "fsdp": owner % sizes["fsdp"]}
@@ -877,9 +878,15 @@
                 index[axis] // stride % size
                 for axis, stride, size in (roles[role] for role in ("z", "y", "x", "c"))
             )
-            value = piece("down", owner, 0)
-            for name, target in BASE_LANES.items():
-                value = value + piece(name, owner, target)
+            half = lay.rows["down"] // 2
+            value = pad_rows(
+                piece("down", owner, 0)[:half] + piece("down", owner, 48)[half:], BASE_ROWS
+            )
+            for name, (top, target) in BASE_PLACE.items():
+                below = piece(name, owner, target)
+                if top:
+                    below = jnp.concatenate([jnp.zeros((top, LANES), F32), below], axis=0)
+                value = value + pad_rows(below, BASE_ROWS)
             blocks[0][z, y, x, core] = value.astype(BF)
 
     meet(grid)
@@ -929,7 +936,7 @@
 def gather_weights(roles, sizes, lay, masters, smalls, lefts):
     count = gather_copies(roles) + exchange_copies(roles)
     nz, ny, nx, nc = (roles[role][2] for role in ("z", "y", "x", "c"))
-    block = (lay.padded["down"], LANES)
+    block = (BASE_ROWS, LANES)
     return pl.pallas_call(
         functools.partial(head_kernel, roles, sizes, lay),
         out_shape=tuple(jax.ShapeDtypeStruct((HEIGHT[n], WIDTH[n]), BF) for n in NAMES)
@@ -1109,11 +1116,21 @@
         row = lax.broadcasted_iota(jnp.int32, (padded, height), 0)
         col = lax.broadcasted_iota(jnp.int32, (padded, height), 1)
         pick = ((row < rows) & (col == me * rows + row)).astype(F32).astype(BF)
-        at = BASE_LANES.get(name, 0)
-        base = bases[:, :padded, :].reshape(lay.count * padded, LANES).T
-        left_rows = base[at : at + padded, :]
-        if rows != padded:
-            left_rows = nt(left_rows, lay.spread(name)).astype(BF)
+        base = bases[...].reshape(lay.count * BASE_ROWS, LANES).T
+        places = [(*BASE_PLACE[name], rows, 0)] if name in BASE_PLACE else [
+            (0, half * 48, rows // 2, half * (rows // 2)) for half in range(2)
+        ]
+        left_rows = None
+        for top, at, height_part, first_row in places:
+            shape = (height, lay.count * BASE_ROWS)
+            to = lax.broadcasted_iota(jnp.int32, shape, 0)
+            col = lax.broadcasted_iota(jnp.int32, shape, 1)
+            owner = col // BASE_ROWS
+            own = col - owner * BASE_ROWS - top
+            hit = (own >= 0) & (own < height_part) & (owner * rows + first_row + own == to)
+            term = nt(base[at : at + padded, :], hit.astype(F32).astype(BF))
+            left_rows = term if left_rows is None else left_rows + term
+        left_rows = left_rows.astype(BF)
         picks[name][:padded, :] = left_rows
         picks[name][padded:, :] = pick
 
@@ -1164,68 +1181,75 @@
             at += take
         return pieces[0] if len(pieces) == 1 else jnp.concatenate(pieces, axis=0)
 
-    directions = {}
-    for name in NAMES:
-        height, width = HEIGHT[name], WIDTH[name]
-        rows, padded = lay.rows[name], lay.padded[name]
-        lhs = picks[name][...]
-        if name in ("down", "pos"):
-            both = None
-            for block in range(height // LANES):
-                part = nt(
-                    lhs[:, block * LANES : (block + 1) * LANES], flat_block(STARTS[name] + block)
+    def step(tag, names):
+        numbers = [
+            (number, group)
+            for number, group in enumerate(groups.members)
+            if group[0][0] in names
+        ]
+        start = groups.starts[numbers[0][0]]
+        end = groups.starts[numbers[-1][0]] + groups.rows[numbers[-1][0]]
+        directions, partway = {}, {}
+        for name in names:
+            height, width = HEIGHT[name], WIDTH[name]
+            rows, padded = lay.rows[name], lay.padded[name]
+            lhs = picks[name][...]
+            if name in ("down", "pos"):
+                both = None
+                for block in range(height // LANES):
+                    part = nt(
+                        lhs[:, block * LANES : (block + 1) * LANES], flat_block(STARTS[name] + block)
+                    )
+                    both = part if both is None else both + part
+            else:
+                both = jnp.concatenate(
+                    [nn(lhs, flat_block(STARTS[name] + i)) for i in range(width // LANES)], axis=1
                 )
-                both = part if both is None else both + part
-        else:
-            both = jnp.concatenate(
-                [nn(lhs, flat_block(STARTS[name] + i)) for i in range(width // LANES)], axis=1
+            keep(0, name, slice(0, width), both[padded : padded + rows])
+            terms = split(both[:padded])
+            for at in range(0, width, D):
+                cols = slice(at, at + D)
+                rotated = joined(nn(terms, rights[name][:, cols]))[:rows]
+                first = DECAY * firsts[name][:, cols] + (1.0 - DECAY) * rotated
+                second = DECAY * seconds[name][:, cols] + (1.0 - DECAY) * rotated * rotated
+                keep(1, name, cols, first)
+                keep(2, name, cols, second)
+                direction = first / (jnp.sqrt(second) + ADAM_EPSILON)
+                for i in range(D // LANES):
+                    directions[name, at // LANES + i] = direction[:, i * LANES : (i + 1) * LANES]
+        for number, group in numbers:
+            piece = jnp.concatenate([directions[member] for member in group], axis=0)
+            steps[me, groups.span(number), :] = pad_rows(piece, groups.rows[number]).astype(BF)
+        yield from gather_all(grid, wire, steps, tag, (start, end - start))
+        for number, group in numbers:
+            rows = groups.rows[number]
+            piece = steps[:, groups.span(number), :].reshape(lay.count * rows, LANES)
+            whole = nn(thins[groups.kind_of[number]][...], piece)
+            at = 0
+            for name, block in group:
+                padded = lay.padded[name]
+                partway[name, block] = joined(whole[at : at + 2 * padded])
+                at += 2 * padded
+        for name in names:
+            height, width = HEIGHT[name], WIDTH[name]
+            terms = split(
+                jnp.concatenate([partway[name, i] for i in range(width // LANES)], axis=1)
             )
-        keep(0, name, slice(0, width), both[padded : padded + rows])
-        terms = split(both[:padded])
-        for at in range(0, width, D):
-            cols = slice(at, at + D)
-            rotated = joined(nn(terms, rights[name][:, cols]))[:rows]
-            first = DECAY * firsts[name][:, cols] + (1.0 - DECAY) * rotated
-            second = DECAY * seconds[name][:, cols] + (1.0 - DECAY) * rotated * rotated
-            keep(1, name, cols, first)
-            keep(2, name, cols, second)
-            direction = first / (jnp.sqrt(second) + ADAM_EPSILON)
-            for i in range(D // LANES):
-                directions[name, at // LANES + i] = direction[:, i * LANES : (i + 1) * LANES]
-    for number, group in enumerate(groups.members):
-        piece = jnp.concatenate([directions[member] for member in group], axis=0)
-        steps[me, groups.span(number), :] = pad_rows(piece, groups.rows[number]).astype(BF)
-
-    together(gather_all(grid, wire, steps, "steps"))
-
-    partway = {}
-    for number, group in enumerate(groups.members):
-        rows = groups.rows[number]
-        piece = steps[:, groups.span(number), :].reshape(lay.count * rows, LANES)
-        whole = nn(thins[groups.kind_of[number]][...], piece)
-        at = 0
-        for name, block in group:
-            padded = lay.padded[name]
-            partway[name, block] = joined(whole[at : at + 2 * padded])
-            at += 2 * padded
-    for name in NAMES:
-        height, width = HEIGHT[name], WIDTH[name]
-        terms = split(
-            jnp.concatenate([partway[name, i] for i in range(width // LANES)], axis=1)
-        )
-        rate = height ** (-0.5)
-        for at in range(0, width, D):
-            cols = slice(at, at + D)
-            update = joined(nt(terms, rights[name][cols, :]))[: lay.rows[name]]
-            master = masters[name][:, cols] * (1.0 - rate * WEIGHT_DECAY) - rate * update
-            keep(3, name, cols, master)
+            rate = height ** (-0.5)
+            for at in range(0, width, D):
+                cols = slice(at, at + D)
+                update = joined(nt(terms, rights[name][cols, :]))[: lay.rows[name]]
+                master = masters[name][:, cols] * (1.0 - rate * WEIGHT_DECAY) - rate * update
+                keep(3, name, cols, master)
+
+    together(step("down steps", ("down", "pos")), step("wide steps", ("qkv", "out", "up")))
     wire.finish()
 
 
 def finish_step(roles, sizes, lay, full, small, bases, rights, lefts, masters, firsts, seconds):
     slots, rows, _ = full.shape
     nz, ny, nx, nc = (roles[role][2] for role in ("z", "y", "x", "c"))
-    count = reduce_copies(roles) + small_copies(roles) + 2 * gather_copies(roles)
+    count = reduce_copies(roles) + small_copies(roles) + 3 * gather_copies(roles)
     extra = {}
     for role in ("c", "y", "x", "z"):
         for offset in range(1, roles[role][2]):

time: 243 us -> 239 us (0.984)
  Pallas kernels: 242 us -> 238 us
    pallas_call x1, Pallas kernels: 45.1 us -> 41.6 us  [gather_weights(): pl.pallas_call(functools.partial(head_kernel, roles, sizes, lay), out_sha...]
where the time goes in v8:
time: 239 us
  Pallas kernels  238 us (100%)
    pallas_call x1, Pallas kernels, layer_pass(): pl.pallas_call(functools.partial(layer_kernel, fc=fc, group=group), out_s...  111 us
    pallas_call x1, Pallas kernels, finish_step(): pl.pallas_call(functools.partial(tail_kernel, roles, sizes, lay, groups,...  82.6 us
    pallas_call x1, Pallas kernels, gather_weights(): pl.pallas_call(functools.partial(head_kernel, roles, sizes, lay), out_sha...  41.6 us

profile of v8, /device:TPU:1, one launch (start us, length us, event | category | flops | bytes accessed | tf_op | source)
XLA Modules:
  0.0 238.8 jit_solution(217571191613189049)
XLA Ops:
  0.7 41.6 %gather_weights.1 = (bf16[384,1152]{1,0:T(8,128)(2,1)}, bf16[384,384]{1,0:T(8,128)(2,1)}, bf16[384,1536]{1,0:T(8,128)(2,1)}, bf16[1536,384]{1,0:T(8,128)(2,1)}, ...) custom-call(f32[12,1152]{1,0:T(8,128)} %refs_10_.3, f32[12,384]{1,0:T(8,128)} %refs_11_.1, ...), custom_call_target="tpu_custom_call" | custom-call | tf_op jit(solution)/shard_map/gather_weights/pallas_call | solution.py:940
  42.3 111.4 %layer.1 = (bf16[4096,384]{1,0:T(8,128)(2,1)}, bf16[4096,384]{1,0:T(8,128)(2,1)}, f32[14336,128]{1,0:T(8,128)}, f32[37,128]{1,0:T(8,128)}) custom-call(s32[16]{0:T(128)} %len_ref.1, bf16[4096,384]{1,0:T(8,128)(2,1)} %tok_ref.1, f32[3,4096]{1,0:T(4,128)} %cen_ref.1, bf16[4096,384]{1,0:T(8,128)(2,1)} %cot_ref.1, f32[37,128]{1,0:T(8,128)} %get-tuple-element.69.small_ref, ...), custom_call_target="tpu_custom_call" | custom-call | tf_op jit(solution)/shard_map/layer/pallas_call | solution.py:347
  153.6 82.6 %finish_step.1 = (f32[40,128]{1,0:T(8,128)}, f32[4,16,3072]{2,1,0:T(8,128)}, f32[4,48,384]{2,1,0:T(8,128)}, f32[4,16,384]{2,1,0:T(8,128)}) custom-call(f32[32,448,128]{2,1,0:T(8,128)} %bitcast.4, f32[37,128]{1,0:T(8,128)} %get-tuple-element.78.small, bf16[32,32,128]{2,1,0:T(8,128)(2,1)} %get-tuple-element.79.bases, f32[1152,1152]{1,0:T(8,128)} %refs_0_.3, ...), custom_call_target="tpu_custom_call" | custom-call | tf_op jit(solution)/shard_map/finish_step/pallas_call | solution.py:1260
  236.3 2.3 hand_out.1

commit v9 on v8

--- a/solution.py
+++ b/solution.py
@@ -892,7 +892,7 @@
     meet(grid)
     together(
         gather_all(grid, wire, buf, "w"),
-        (exchange_all(grid, wire, "e", blocks, pack_bases), 4),
+        (exchange_all(grid, wire, "e", blocks, pack_bases), 3),
     )
     nz, ny, nx, nc = (grid.size(role) for role in ("z", "y", "x", "c"))
     for z in range(nz):

time: 239 us -> 238 us (level)
  no operation moved by 1% of the time
where the time goes in v9:
time: 238 us
  Pallas kernels  237 us (100%)
    pallas_call x1, Pallas kernels, layer_pass(): pl.pallas_call(functools.partial(layer_kernel, fc=fc, group=group), out_s...  111 us
    pallas_call x1, Pallas kernels, finish_step(): pl.pallas_call(functools.partial(tail_kernel, roles, sizes, lay, groups,...  80.8 us
    pallas_call x1, Pallas kernels, gather_weights(): pl.pallas_call(functools.partial(head_kernel, roles, sizes, lay), out_sha...  42.2 us

profile of v9, /device:TPU:1, one launch (start us, length us, event | category | flops | bytes accessed | tf_op | source)
XLA Modules:
  0.0 237.5 jit_solution(11429951466944825159)
XLA Ops:
  0.7 42.2 %gather_weights.1 = (bf16[384,1152]{1,0:T(8,128)(2,1)}, bf16[384,384]{1,0:T(8,128)(2,1)}, bf16[384,1536]{1,0:T(8,128)(2,1)}, bf16[1536,384]{1,0:T(8,128)(2,1)}, ...) custom-call(f32[12,1152]{1,0:T(8,128)} %refs_10_.3, f32[12,384]{1,0:T(8,128)} %refs_11_.1, ...), custom_call_target="tpu_custom_call" | custom-call | tf_op jit(solution)/shard_map/gather_weights/pallas_call | solution.py:940
  42.8 111.4 %layer.1 = (bf16[4096,384]{1,0:T(8,128)(2,1)}, bf16[4096,384]{1,0:T(8,128)(2,1)}, f32[14336,128]{1,0:T(8,128)}, f32[37,128]{1,0:T(8,128)}) custom-call(s32[16]{0:T(128)} %len_ref.1, bf16[4096,384]{1,0:T(8,128)(2,1)} %tok_ref.1, f32[3,4096]{1,0:T(4,128)} %cen_ref.1, bf16[4096,384]{1,0:T(8,128)(2,1)} %cot_ref.1, f32[37,128]{1,0:T(8,128)} %get-tuple-element.69.small_ref, ...), custom_call_target="tpu_custom_call" | custom-call | tf_op jit(solution)/shard_map/layer/pallas_call | solution.py:347
  154.2 80.8 %finish_step.1 = (f32[40,128]{1,0:T(8,128)}, f32[4,16,3072]{2,1,0:T(8,128)}, f32[4,48,384]{2,1,0:T(8,128)}, f32[4,16,384]{2,1,0:T(8,128)}) custom-call(f32[32,448,128]{2,1,0:T(8,128)} %bitcast.4, f32[37,128]{1,0:T(8,128)} %get-tuple-element.78.small, bf16[32,32,128]{2,1,0:T(8,128)(2,1)} %get-tuple-element.79.bases, f32[1152,1152]{1,0:T(8,128)} %refs_0_.3, ...), custom_call_target="tpu_custom_call" | custom-call | tf_op jit(solution)/shard_map/finish_step/pallas_call | solution.py:1260
  235.0 2.3 hand_out.1
